TPU v7x, 512 devices: a whole 4x8x8 slice. The times are simulated.
512 devices in a mesh: dp: 8 (over x, z_hi), seq: 64 (over y, z_lo, core).
Axes of the slice: x: 4, y: 8, z: 8 (z_hi: 2, z_lo: 4; z = z_hi * 4 + z_lo), core: 2. Of those that a mesh axis runs over, the one named last changes fastest.
Arguments:
- clean: bfloat16 [8, 16384, 768], P('dp', 'seq'), may hold values from -12 to 12
- out_cot: bfloat16 [8, 16384, 768], P('dp', 'seq'), may hold values from -6 to 6
- mask_bits: int32 [8, 1024], P('dp', 'seq'), may hold values from 0 to 65535
- levels: int32 [8, 1024], P('dp', 'seq'), may hold values from 1 to 16
- importance: int32 [8, 1024, 2], P('dp', 'seq'), may hold values from 1 to 8
- w_query: bfloat16 [768, 768], replicated, may hold values from -0.21875 to 0.21875
- w_key: bfloat16 [768, 768], replicated, may hold values from -0.21875 to 0.21875
- w_value: bfloat16 [768, 768], replicated, may hold values from -0.21875 to 0.21875
- mask_embed: bfloat16 [768], replicated, may hold values from -6 to 6
Outputs:
- attn_out: bfloat16 [8, 16384, 768], P('dp', 'seq')
- clean_grad: float32 [8, 16384, 768], P('dp', 'seq')
All inputs are finite; a program needn't handle non-finite values.
Results may differ from a plain program's by a relative error of at most 0.025.
Values may be sent and summed in bfloat16 or wider, within the bound.
A program may use at most 64 MiB of HBM per device.

v0:
```python
import math

import jax
import jax.numpy as jnp
from jax import lax
from jax.sharding import PartitionSpec as P

HEADS = 12
HEAD_DIM = 64
BLOCK = 16
WINDOW = 1024
LEVELS = 16


EPS = 1e-06
CLIP = 0.25


def from_behind(block, axis, distance):
    devices = range(lax.axis_size(axis))
    route = [(i - distance, i) for i in devices if i - distance in devices]
    return lax.ppermute(block, axis, route)


def to_heads(rows):
    return rows.reshape(rows.shape[0], HEADS, HEAD_DIM).transpose(1, 0, 2)


def from_heads(stacked):
    return stacked.transpose(1, 0, 2).reshape(stacked.shape[1], HEADS * HEAD_DIM)


def forward_head(
    query_h, key_h, value_h, nkey_h, nvalue_h, grad_h, allow_clean, allow_noisy, scale
):
    score_clean = (
        jnp.einsum("qe,ke->qk", query_h, key_h, preferred_element_type=jnp.float32) * scale
    )
    score_noisy = (
        jnp.einsum("qe,ke->qk", query_h, nkey_h, preferred_element_type=jnp.float32) * scale
    )
    score_clean = jnp.where(allow_clean, score_clean, -jnp.inf)
    score_noisy = jnp.where(allow_noisy, score_noisy, -jnp.inf)
    peak = jnp.maximum(jnp.max(score_clean, axis=-1), jnp.max(score_noisy, axis=-1))
    exp_clean = jnp.where(allow_clean, jnp.exp(score_clean - peak[:, None]), 0.0)
    exp_noisy = jnp.where(allow_noisy, jnp.exp(score_noisy - peak[:, None]), 0.0)
    denom = jnp.sum(exp_clean, axis=-1) + jnp.sum(exp_noisy, axis=-1)
    prob_clean = exp_clean / denom[:, None]
    prob_noisy = exp_noisy / denom[:, None]
    weight_clean = prob_clean.astype(jnp.bfloat16)
    weight_noisy = prob_noisy.astype(jnp.bfloat16)
    mixed = jnp.einsum("qk,ke->qe", weight_clean, value_h, preferred_element_type=jnp.float32)
    mixed = mixed + jnp.einsum(
        "qk,ke->qe", weight_noisy, nvalue_h, preferred_element_type=jnp.float32
    )
    out_h = mixed.astype(jnp.bfloat16)
    delta = jnp.sum(grad_h.astype(jnp.float32) * out_h.astype(jnp.float32), axis=-1)
    return (out_h, prob_clean, weight_clean, peak, denom, delta)


def on_device(clean, out_cot, mask_bits, levels, importance, w_query, w_key, w_value, mask_embed):
    clean_rows = clean[0]
    cotangent = out_cot[0]
    tok_count = clean_rows.shape[0]
    width = clean_rows.shape[1]
    span = WINDOW // tok_count
    scale = 1.0 / math.sqrt(HEAD_DIM)
    position = lax.axis_index("seq") * tok_count
    local = jnp.arange(tok_count, dtype=jnp.int32)
    local_block = local // BLOCK
    within = local % BLOCK
    bits = jnp.right_shift(mask_bits[0][local_block], within) & 1
    masked = bits == 1
    noisy = jnp.where(masked[:, None], mask_embed[None, :], clean_rows)
    query = jnp.dot(noisy, w_query, preferred_element_type=jnp.float32).astype(jnp.bfloat16)
    key_noisy = jnp.dot(noisy, w_key, preferred_element_type=jnp.float32).astype(jnp.bfloat16)
    value_noisy = jnp.dot(noisy, w_value, preferred_element_type=jnp.float32).astype(jnp.bfloat16)
    key_wide = w_key.astype(jnp.float32).T
    value_wide = w_value.astype(jnp.float32).T
    key_mine = jnp.dot(clean_rows, w_key, preferred_element_type=jnp.float32).astype(jnp.bfloat16)
    value_mine = jnp.dot(clean_rows, w_value, preferred_element_type=jnp.float32).astype(
        jnp.bfloat16
    )
    carried = jnp.stack([key_mine, value_mine])
    collected = [carried]
    for step in range(span):
        carried = from_behind(carried, "seq", 1)
        collected.insert(0, carried)
    window_kv = jnp.concatenate(collected, axis=1)
    key_clean = window_kv[0]
    value_clean = window_kv[1]
    context = key_clean.shape[0]
    ctx_pos = position - span * tok_count + jnp.arange(context, dtype=jnp.int32)
    q_start = (position + local) // BLOCK * BLOCK
    allow_clean = (
        (ctx_pos[None, :] < q_start[:, None])
        & (ctx_pos[None, :] >= q_start[:, None] - WINDOW)
        & (ctx_pos[None, :] >= 0)
    )
    allow_noisy = local_block[None, :] == local_block[:, None]
    level_f = levels[0].astype(jnp.float32)
    ratio_f = importance[0].astype(jnp.float32)
    block_weight = LEVELS / level_f * (ratio_f[:, 0] / ratio_f[:, 1])
    token_weight = block_weight[local_block] * bits.astype(jnp.float32)
    grad_out = (cotangent.astype(jnp.float32) * token_weight[:, None]).astype(jnp.bfloat16)
    head_inputs = (
        to_heads(query),
        to_heads(key_clean),
        to_heads(value_clean),
        to_heads(key_noisy),
        to_heads(value_noisy),
        to_heads(grad_out),
    )

    def full_pass(items):
        query_h, key_h, value_h, nkey_h, nvalue_h, grad_h = items
        out_h, prob_clean, weight_clean, peak, denom, delta = forward_head(
            query_h, key_h, value_h, nkey_h, nvalue_h, grad_h, allow_clean, allow_noisy, scale
        )
        dprob = jnp.einsum("qe,ke->qk", grad_h, value_h, preferred_element_type=jnp.float32)
        dscore = (prob_clean * (dprob - delta[:, None]) * scale).astype(jnp.bfloat16)
        dkey_h = jnp.einsum("qk,qe->ke", dscore, query_h, preferred_element_type=jnp.float32)
        dvalue_h = jnp.einsum("qk,qe->ke", weight_clean, grad_h, preferred_element_type=jnp.float32)
        return (out_h, dkey_h, dvalue_h)

    out_heads, dkey_heads, dvalue_heads = lax.map(full_pass, head_inputs)
    terms = jnp.stack([from_heads(dkey_heads), from_heads(dvalue_heads)])
    running = terms[:, :tok_count]
    for step in range(span):
        running = from_behind(running, "seq", -1)
        running = running + terms[:, (step + 1) * tok_count : (step + 2) * tok_count]
    raw = jnp.dot(running[0], key_wide, precision=lax.Precision.HIGHEST)
    raw = raw + jnp.dot(running[1], value_wide, precision=lax.Precision.HIGHEST)
    attn_rows = from_heads(out_heads)
    squares = jnp.sum(raw * raw)
    total_squares = lax.psum(squares, ("dp", "seq"))
    entries = float(tok_count * width * lax.axis_size("dp") * lax.axis_size("seq"))
    rms = jnp.sqrt(total_squares / entries + EPS)
    factor = jnp.minimum(1.0, CLIP / rms)
    return (attn_rows[None], (raw * factor)[None])


def solution(mesh):
    in_specs = (
        P("dp", "seq", None),
        P("dp", "seq", None),
        P("dp", "seq"),
        P("dp", "seq"),
        P("dp", "seq", None),
        P(),
        P(),
        P(),
        P(),
    )
    out_specs = (P("dp", "seq", None), P("dp", "seq", None))
    return jax.shard_map(
        on_device, mesh=mesh, in_specs=in_specs, out_specs=out_specs, check_vma=False
    )
```

profile of v0, /device:TPU:1, one launch (start us, length us, event | category | flops | bytes accessed | tf_op | source)
XLA Modules:
  0.0 428.4 jit_solution(6213927635284822919)
XLA Ops:
  4.0 5.4 %collective-permute-start = (bf16[2,256,768]{2,1,0:T(8,128)(2,1)S(1)}, bf16[2,256,768]{2,1,0:T(8,128)(2,1)S(1)}, u32[]{:S(2)}, u32[]{:S(2)}) collective-permute-start(bf16[2,256,768]{2,1,0:T(8,128)(2,1)S(1)} %pad_maximum_fusion.1), channel_id=1, source_target_pairs={{0,1},{1,2},{2,3},{3,4},{4,5},{5,6},{6,7},{7,8},{8,9},{9,10},{10,1... | collective-permute-start | bytes 2359304 | tf_op jit(solution)/shard_map/ppermute | solution.py:22
  9.4 8.9 %collective-permute-done = bf16[2,256,768]{2,1,0:T(8,128)(2,1)S(1)} collective-permute-done((bf16[2,256,768]{2,1,0:T(8,128)(2,1)S(1)}, bf16[2,256,768]{2,1,0:T(8,128)(2,1)S(1)}, u32[]{:S(2)}, u32[]{:S(2)}) %collective-permute-start) | collective-permute-done | bytes 786464 | tf_op jit(solution)/shard_map/ppermute | solution.py:22
  19.3 4.4 %collective-permute-start.1 = (bf16[2,256,768]{2,1,0:T(8,128)(2,1)S(1)}, bf16[2,256,768]{2,1,0:T(8,128)(2,1)S(1)}, u32[]{:S(2)}, u32[]{:S(2)}) collective-permute-start(bf16[2,256,768]{2,1,0:T(8,128)(2,1)S(1)} %collective-permute-done), channel_id=1, source_target_pairs={{0,1},{1,2},{2,3},{3,4},{4,5},{5,6},{6,7},{7,8},{8,9},{9,10},{10,1... | collective-permute-start | bytes 2359304 | tf_op jit(solution)/shard_map/ppermute | solution.py:22
  24.7 4.3 compare_select_fusion.3
  29.7 4.3 compare_select_fusion.2
  34.0 2.9 collective-permute-start.2
  37.0 12.1 %select_multiply_fusion = (f32[256]{0:T(256)}, s32[256]{0:T(256)S(1)}) fusion(pred[256]{0:T(512)(128)(4,1)S(1)} %compare_reduce_fusion, pred[256]{0:T(512)(128)(4,1)S(1)} %compare_reduce_fusion.1, pred[256]{0:T(512)(128)(4,1)S(1)} %compare_reduce_fusion.2, pred[256]{0:T(512)(128)(4,1)S(1)} %compare_reduce_fusion.3, ...), kind=kLoop, calls=%fused_computation.136 | loop fusion | flops 7168 | bytes 6472 | tf_op jit(solution)/shard_map/mul | solution.py:104
  50.1 3.4 collective-permute-start.3
  58.5 4.3 %collective-permute-done.3 = bf16[2,256,768]{2,1,0:T(8,128)(2,1)} collective-permute-done((bf16[2,256,768]{2,1,0:T(8,128)(2,1)}, bf16[2,256,768]{2,1,0:T(8,128)(2,1)}, u32[]{:S(2)}, u32[]{:S(2)}) %collective-permute-start.3) | collective-permute-done | bytes 786464 | tf_op jit(solution)/shard_map/ppermute | solution.py:22
  67.0 4.0 copy.21
  70.9 2.3 copy.19
  73.2 127.1 %while.16 = (s32[]{:T(128)}, bf16[12,256,64]{1,2,0:T(8,128)(2,1)}, f32[12,1280,64]{1,2,0:T(8,128)}, f32[12,1280,64]{1,2,0:T(8,128)}, bf16[12,256,64]{1,2,0:T(8,1...) while((s32[]{:T(128)}, bf16[12,256,64]{1,2,0:T(8,128)(2,1)}, ...), condition=%wide.region_6.7_spmd.clone.clone, body=%wide.region_0.6_spmd.clone.clone.sunk | while | flops 240876800 | bytes 9070557 | solution.py:126
  79.8 2.5 fusion.113
  90.4 2.6 fusion.113
  101.0 2.6 fusion.113
  111.6 2.6 fusion.113
  122.2 2.6 fusion.113
  132.8 2.5 fusion.113
  143.4 2.6 fusion.113
  154.0 2.6 fusion.113
  164.5 2.6 fusion.113
  175.1 2.6 fusion.113
  185.7 2.6 fusion.113
  196.3 2.6 fusion.113
  201.9 2.2 collective-permute-start.4
  204.1 20.6 %collective-permute-done.4 = f32[2,256,768]{1,2,0:T(8,128)S(1)} collective-permute-done((f32[2,256,768]{1,2,0:T(8,128)S(1)}, f32[2,256,768]{1,2,0:T(8,128)S(1)}, u32[]{:S(2)}, u32[]{:S(2)}) %collective-permute-start.4) | collective-permute-done | bytes 1572896 | tf_op jit(solution)/shard_map/ppermute | solution.py:22
  226.8 19.8 %collective-permute-done.5 = f32[2,256,768]{1,2,0:T(8,128)S(1)} collective-permute-done((f32[2,256,768]{1,2,0:T(8,128)S(1)}, f32[2,256,768]{1,2,0:T(8,128)S(1)}, u32[]{:S(2)}, u32[]{:S(2)}) %collective-permute-start.5) | collective-permute-done | bytes 1572896 | tf_op jit(solution)/shard_map/ppermute | solution.py:22
  248.9 19.8 %collective-permute-done.6 = f32[2,256,768]{1,2,0:T(8,128)S(1)} collective-permute-done((f32[2,256,768]{1,2,0:T(8,128)S(1)}, f32[2,256,768]{1,2,0:T(8,128)S(1)}, u32[]{:S(2)}, u32[]{:S(2)}) %collective-permute-start.6) | collective-permute-done | bytes 1572896 | tf_op jit(solution)/shard_map/ppermute | solution.py:22
  270.1 2.1 collective-permute-start.7
  273.2 18.9 %collective-permute-done.7 = f32[2,256,768]{1,2,0:T(8,128)S(1)} collective-permute-done((f32[2,256,768]{1,2,0:T(8,128)}, f32[2,256,768]{1,2,0:T(8,128)S(1)}, u32[]{:S(2)}, u32[]{:S(2)}) %collective-permute-start.7) | collective-permute-done | bytes 1572896 | tf_op jit(solution)/shard_map/ppermute | solution.py:22
  295.7 2.8 multiply_reduce_fusion.1
  298.5 128.3 %psum.7 = f32[]{:T(128)} all-reduce(f32[]{:T(128)} %get-tuple-element.227), channel_id=1, replica_groups=mesh['dp'=8,'seq'=64] {'dp','seq'}, use_global_device_ids=true, to_apply=%region_8.9 | all-reduce | flops 1 | bytes 8 | tf_op jit(solution)/shard_map/psum | solution.py:136
  (252 shorter events, 125.1 us)
Async XLA Ops:
  0.6 2.7 copy-start.5
  0.7 2.7 copy-start.3
  3.4 20.3 %copy-start.15 = (s32[1,16,2]{1,2,0:T(2,128)S(1)}, s32[1,16,2]{1,2,0:T(2,128)}, u32[]{:S(2)}) copy-start(s32[1,16,2]{1,2,0:T(2,128)} %param.15) | copy-start | bytes 388
  3.4 20.6 %copy-start.16 = (s32[1,16]{1,0:T(1,128)S(1)}, s32[1,16]{1,0:T(1,128)}, u32[]{:S(2)}) copy-start(s32[1,16]{1,0:T(1,128)} %param.14) | copy-start | bytes 196
  3.4 25.6 %copy-start.12 = (s32[1,16]{1,0:T(1,128)S(1)}, s32[1,16]{1,0:T(1,128)}, u32[]{:S(2)}) copy-start(s32[1,16]{1,0:T(1,128)} %param.13) | copy-start | bytes 196
  3.4 45.6 %copy-start.18 = (bf16[768]{0:T(1024)(128)(2,1)S(1)}, bf16[768]{0:T(1024)(128)(2,1)}, u32[]{:S(2)}) copy-start(bf16[768]{0:T(1024)(128)(2,1)} %param.19) | copy-start | bytes 4612
  4.0 14.3 %collective-permute-start = (bf16[2,256,768]{2,1,0:T(8,128)(2,1)S(1)}, bf16[2,256,768]{2,1,0:T(8,128)(2,1)S(1)}, u32[]{:S(2)}, u32[]{:S(2)}) collective-permute-start(bf16[2,256,768]{2,1,0:T(8,128)(2,1)S(1)} %pad_maximum_fusion.1), channel_id=1, source_target_pairs={{0,1},{1,2},{2,3},{3,4},{4,5},{5,6},{6,7},{7,8},{8,9},{9,10},{10,1... | collective-permute-start | bytes 2359304 | tf_op jit(solution)/shard_map/ppermute | solution.py:22
  19.3 14.7 %collective-permute-start.1 = (bf16[2,256,768]{2,1,0:T(8,128)(2,1)S(1)}, bf16[2,256,768]{2,1,0:T(8,128)(2,1)S(1)}, u32[]{:S(2)}, u32[]{:S(2)}) collective-permute-start(bf16[2,256,768]{2,1,0:T(8,128)(2,1)S(1)} %collective-permute-done), channel_id=1, source_target_pairs={{0,1},{1,2},{2,3},{3,4},{4,5},{5,6},{6,7},{7,8},{8,9},{9,10},{10,1... | collective-permute-start | bytes 2359304 | tf_op jit(solution)/shard_map/ppermute | solution.py:22
  34.0 16.1 %copy-start.8 = (bf16[2,256,768]{2,1,0:T(8,128)(2,1)}, bf16[2,256,768]{2,1,0:T(8,128)(2,1)S(1)}, u32[]{:S(2)}) copy-start(bf16[2,256,768]{2,1,0:T(8,128)(2,1)S(1)} %collective-permute-done.1) | copy-start | bytes 2359300
  34.0 16.1 %collective-permute-start.2 = (bf16[2,256,768]{2,1,0:T(8,128)(2,1)S(1)}, bf16[2,256,768]{2,1,0:T(8,128)(2,1)}, u32[]{:S(2)}, u32[]{:S(2)}) collective-permute-start(bf16[2,256,768]{2,1,0:T(8,128)(2,1)S(1)} %collective-permute-done.1), channel_id=1, source_target_pairs={{0,1},{1,2},{2,3},{3,4},{4,5},{5,6},{6,7},{7,8},{8,9},{9,10},{10,1... | collective-permute-start | bytes 2359304 | tf_op jit(solution)/shard_map/ppermute | solution.py:22
  49.6 3.9 copy-start.17
  50.1 12.6 %collective-permute-start.3 = (bf16[2,256,768]{2,1,0:T(8,128)(2,1)}, bf16[2,256,768]{2,1,0:T(8,128)(2,1)}, u32[]{:S(2)}, u32[]{:S(2)}) collective-permute-start(bf16[2,256,768]{2,1,0:T(8,128)(2,1)} %collective-permute-done.2), channel_id=1, source_target_pairs={{0,1},{1,2},{2,3},{3,4},{4,5},{5,6},{6,7},{7,8},{8,9},{9,10},{10,1... | collective-permute-start | bytes 2359304 | tf_op jit(solution)/shard_map/ppermute | solution.py:22
  54.1 2.8 copy-start.11
  58.4 6.8 %copy-start.9 = (bf16[2,256,768]{2,1,0:T(8,128)(2,1)S(1)}, bf16[2,256,768]{2,1,0:T(8,128)(2,1)}, u32[]{:S(2)}) copy-start(bf16[2,256,768]{2,1,0:T(8,128)(2,1)} %copy-done.8) | copy-start | bytes 2359300
  73.2 2.7 copy-start.14
  83.8 2.7 copy-start.14
  94.4 2.7 copy-start.14
  115.6 2.7 copy-start.14
  126.2 2.7 copy-start.14
  147.4 2.7 copy-start.14
  157.9 2.7 copy-start.14
  168.5 2.7 copy-start.14
  179.1 2.7 copy-start.14
  189.7 2.7 copy-start.14
  200.3 24.4 %copy-start.1 = (f32[12,1280,64]{1,2,0:T(8,128)S(1)}, f32[12,1280,64]{1,2,0:T(8,128)}, u32[]{:S(2)}) copy-start(f32[12,1280,64]{1,2,0:T(8,128)} %get-tuple-element.71) | copy-start | bytes 11796484
  200.3 24.4 %copy-start.2 = (f32[12,1280,64]{1,2,0:T(8,128)S(1)}, f32[12,1280,64]{1,2,0:T(8,128)}, u32[]{:S(2)}) copy-start(f32[12,1280,64]{1,2,0:T(8,128)} %get-tuple-element.70) | copy-start | bytes 11796484
  201.9 22.7 %collective-permute-start.4 = (f32[2,256,768]{1,2,0:T(8,128)S(1)}, f32[2,256,768]{1,2,0:T(8,128)S(1)}, u32[]{:S(2)}, u32[]{:S(2)}) collective-permute-start(f32[2,256,768]{1,2,0:T(8,128)S(1)} %fusion.58), channel_id=1, source_target_pairs={{1,0},{2,1},{3,2},{4,3},{5,4},{6,5},{7,6},{8,7},{9,8},{10,9},{11,1... | collective-permute-start | bytes 4718600 | tf_op jit(solution)/shard_map/ppermute | solution.py:22
  224.9 21.7 %collective-permute-start.5 = (f32[2,256,768]{1,2,0:T(8,128)S(1)}, f32[2,256,768]{1,2,0:T(8,128)S(1)}, u32[]{:S(2)}, u32[]{:S(2)}) collective-permute-start(f32[2,256,768]{1,2,0:T(8,128)S(1)} %fusion.60), channel_id=1, source_target_pairs={{1,0},{2,1},{3,2},{4,3},{5,4},{6,5},{7,6},{8,7},{9,8},{10,9},{11,1... | collective-permute-start | bytes 4718600 | tf_op jit(solution)/shard_map/ppermute | solution.py:22
  246.8 25.4 %copy-start.10 = (bf16[12,256,64]{1,2,0:T(8,128)(2,1)S(1)}, bf16[12,256,64]{1,2,0:T(8,128)(2,1)}, u32[]{:S(2)}) copy-start(bf16[12,256,64]{1,2,0:T(8,128)(2,1)} %get-tuple-element.69) | copy-start | bytes 1179652
  246.8 21.9 %collective-permute-start.6 = (f32[2,256,768]{1,2,0:T(8,128)S(1)}, f32[2,256,768]{1,2,0:T(8,128)S(1)}, u32[]{:S(2)}, u32[]{:S(2)}) collective-permute-start(f32[2,256,768]{1,2,0:T(8,128)S(1)} %fusion.62), channel_id=1, source_target_pairs={{1,0},{2,1},{3,2},{4,3},{5,4},{6,5},{7,6},{8,7},{9,8},{10,9},{11,1... | collective-permute-start | bytes 4718600 | tf_op jit(solution)/shard_map/ppermute | solution.py:22
  270.1 21.9 %collective-permute-start.7 = (f32[2,256,768]{1,2,0:T(8,128)}, f32[2,256,768]{1,2,0:T(8,128)S(1)}, u32[]{:S(2)}, u32[]{:S(2)}) collective-permute-start(f32[2,256,768]{1,2,0:T(8,128)} %fusion.57), channel_id=1, source_target_pairs={{1,0},{2,1},{3,2},{4,3},{5,4},{6,5},{7,6},{8,7},{9,8},{10,9},{11,1... | collective-permute-start | bytes 4718600 | tf_op jit(solution)/shard_map/ppermute | solution.py:22
  273.2 20.5 %copy-start.4 = (bf16[768,768]{1,0:T(8,128)(2,1)S(1)}, bf16[768,768]{1,0:T(8,128)(2,1)}, u32[]{:S(2)}) copy-start(bf16[768,768]{1,0:T(8,128)(2,1)} %param.18) | copy-start | bytes 3538948
  (17 other events, 41.5 us)
where the time goes:
time: 432 us; the launch traced here: 428 us
  blocking collectives  128 us (30%)
  matrix products  126 us (29%)
  waiting for transfers between devices  92.3 us (21%)
  other arithmetic  37.7 us (9%)
  starting transfers between devices  24.3 us (6%)
  local copies, waits for them, and re-layouts  18 us (4%)
    psum x1, blocking collectives, on_device(): total_squares = lax.psum(squares, ('dp', 'seq'))  128 us
    ppermute x8, waiting for transfers between devices, from_behind(): return lax.ppermute(block, axis, route)  92.3 us
    dot_general x12, matrix products, full_pass(): jnp.einsum('qk,qe->ke', dscore, query_h, preferred_element_type=jnp.float32)  30.7 us
    ppermute x8, starting transfers between devices, from_behind(): return lax.ppermute(block, axis, route)  24.3 us
    dot_general x12, matrix products, forward_head(): jnp.einsum('qk,ke->qe', weight_noisy, nvalue_h, preferred_element_type=jn...  19.4 us
    dot_general x12, matrix products, forward_head(): jnp.einsum('qk,ke->qe', weight_clean, value_h, preferred_element_type=jnp...  19.4 us
    dot_general x12, matrix products, forward_head(): jnp.einsum('qe,ke->qk', query_h, key_h, preferred_element_type=jnp.float32)  18.4 us
    dot_general x12, matrix products, full_pass(): jnp.einsum('qk,qe->ke', weight_clean, grad_h, preferred_element_type=jnp....  17.1 us
  transfers between devices with their start and end apart: 8, of which 6 were waited for; matrix products, arithmetic and copies ran while one was open for 7% of the time, Pallas kernels for 0%

commit v1 on v0

--- a/solution.py
+++ b/solution.py
@@ -1,9 +1,12 @@
+import functools
 import math
 
 import jax
 import jax.numpy as jnp
 from jax import lax
 from jax.sharding import PartitionSpec as P
+from jax.experimental import pallas as pl
+from jax.experimental.pallas import tpu as pltpu
 
 HEADS = 12
 HEAD_DIM = 64
@@ -20,6 +23,83 @@
     devices = range(lax.axis_size(axis))
     route = [(i - distance, i) for i in devices if i - distance in devices]
     return lax.ppermute(block, axis, route)
+
+
+def group_stages(axes):
+    stages = []
+    for axis in axes:
+        rest, stride = lax.axis_size(axis), 1
+        while rest > 1:
+            size = max(g for g in range(1, 9) if rest % g == 0)
+            stages.append((axis, stride, size))
+            stride, rest = stride * size, rest // size
+    return stages
+
+
+def stage_peer(axis, stride, size, offset):
+    index = lax.axis_index(axis)
+    digit = (index // stride) % size
+    return index + ((digit + offset) % size - digit) * stride
+
+
+def device_of(axes, axis, peer):
+    return tuple(peer if name == axis else lax.axis_index(name) for name in axes)
+
+
+def total_kernel(axes, stages, part_ref, out_ref, slots, send_sems, recv_sems):
+    barrier = pltpu.get_barrier_semaphore()
+    greeted = 0
+    for axis, stride, size in stages:
+        for offset in range(1, size):
+            peer = stage_peer(axis, stride, size, offset)
+            pl.semaphore_signal(
+                barrier, 1, device_id=device_of(axes, axis, peer),
+                device_id_type=pl.DeviceIdType.MESH,
+            )
+            greeted += 1
+    pl.semaphore_wait(barrier, greeted)
+    current = part_ref[...]
+    for number, (axis, stride, size) in enumerate(stages):
+        digit = (lax.axis_index(axis) // stride) % size
+        slots[number, digit] = current
+        copies = []
+        for offset in range(1, size):
+            peer = stage_peer(axis, stride, size, offset)
+            copy = pltpu.make_async_remote_copy(
+                src_ref=slots.at[number, digit],
+                dst_ref=slots.at[number, digit],
+                send_sem=send_sems.at[number, offset],
+                recv_sem=recv_sems.at[number, offset],
+                device_id=device_of(axes, axis, peer),
+                device_id_type=pl.DeviceIdType.MESH,
+            )
+            copy.start()
+            copies.append(copy)
+        for copy in copies:
+            copy.wait()
+        current = slots[number, 0]
+        for member in range(1, size):
+            current = current + slots[number, member]
+    out_ref[...] = current
+
+
+def global_total(value, axes):
+    stages = group_stages(axes)
+    widest = max(size for _, _, size in stages)
+    part = jnp.broadcast_to(value.astype(jnp.float32), (8, 128))
+    summed = pl.pallas_call(
+        functools.partial(total_kernel, axes, stages),
+        out_shape=jax.ShapeDtypeStruct((8, 128), jnp.float32),
+        in_specs=[pl.BlockSpec(memory_space=pltpu.VMEM)],
+        out_specs=pl.BlockSpec(memory_space=pltpu.VMEM),
+        scratch_shapes=[
+            pltpu.VMEM((len(stages), widest, 8, 128), jnp.float32),
+            pltpu.SemaphoreType.DMA((len(stages), widest)),
+            pltpu.SemaphoreType.DMA((len(stages), widest)),
+        ],
+        compiler_params=pltpu.CompilerParams(collective_id=0, has_side_effects=True),
+    )(part)
+    return summed[0, 0]
 
 
 def to_heads(rows):
@@ -133,7 +213,7 @@
     raw = raw + jnp.dot(running[1], value_wide, precision=lax.Precision.HIGHEST)
     attn_rows = from_heads(out_heads)
     squares = jnp.sum(raw * raw)
-    total_squares = lax.psum(squares, ("dp", "seq"))
+    total_squares = global_total(squares, ("dp", "seq"))
     entries = float(tok_count * width * lax.axis_size("dp") * lax.axis_size("seq"))
     rms = jnp.sqrt(total_squares / entries + EPS)
     factor = jnp.minimum(1.0, CLIP / rms)

time: 432 us -> 357 us (0.83)
  blocking collectives: 128 us -> 0 us
  Pallas kernels: 0 us -> 50.6 us
    psum x1 -> x0, blocking collectives: 128 us -> none  [on_device(): total_squares = lax.psum(squares, ('dp', 'seq'))]
    pallas_call x0 -> x1, Pallas kernels: none -> 50.6 us  [global_total(): pl.pallas_call(functools.partial(total_kernel, axes, stages), out_shape=j...]
  transfers between devices with their start and end apart: 8 -> 8, of which waited for: 6 -> 6; matrix products, arithmetic and copies ran while one was open for 7% -> 8% of each run, Pallas kernels for 0% -> 0%
where the time goes in v1:
time: 357 us; the launch traced here: 353 us
  matrix products  126 us (35%)
  waiting for transfers between devices  92.3 us (26%)
  Pallas kernels  50.6 us (14%)
  other arithmetic  37.7 us (11%)
  starting transfers between devices  24.3 us (7%)
  local copies, waits for them, and re-layouts  20.5 us (6%)
    ppermute x8, waiting for transfers between devices, from_behind(): return lax.ppermute(block, axis, route)  92.3 us
    pallas_call x1, Pallas kernels, global_total(): pl.pallas_call(functools.partial(total_kernel, axes, stages), out_shape=j...  50.6 us
    dot_general x12, matrix products, full_pass(): jnp.einsum('qk,qe->ke', dscore, query_h, preferred_element_type=jnp.float32)  30.7 us
    ppermute x8, starting transfers between devices, from_behind(): return lax.ppermute(block, axis, route)  24.3 us
    dot_general x12, matrix products, forward_head(): jnp.einsum('qk,ke->qe', weight_noisy, nvalue_h, preferred_element_type=jn...  19.4 us
    dot_general x12, matrix products, forward_head(): jnp.einsum('qk,ke->qe', weight_clean, value_h, preferred_element_type=jnp...  19.4 us
    dot_general x12, matrix products, forward_head(): jnp.einsum('qe,ke->qk', query_h, key_h, preferred_element_type=jnp.float32)  18.4 us
    dot_general x12, matrix products, full_pass(): jnp.einsum('qk,qe->ke', weight_clean, grad_h, preferred_element_type=jnp....  17.1 us
  transfers between devices with their start and end apart: 8, of which 6 were waited for; matrix products, arithmetic and copies ran while one was open for 8% of the time, Pallas kernels for 0%

profile of v1, /device:TPU:1, one launch (start us, length us, event | category | flops | bytes accessed | tf_op | source)
XLA Modules:
  0.0 353.3 jit_solution(6682246345125134866)
XLA Ops:
  4.0 5.4 %collective-permute-start = (bf16[2,256,768]{2,1,0:T(8,128)(2,1)S(1)}, bf16[2,256,768]{2,1,0:T(8,128)(2,1)S(1)}, u32[]{:S(2)}, u32[]{:S(2)}) collective-permute-start(bf16[2,256,768]{2,1,0:T(8,128)(2,1)S(1)} %pad_maximum_fusion.1), channel_id=1, source_target_pairs={{0,1},{1,2},{2,3},{3,4},{4,5},{5,6},{6,7},{7,8},{8,9},{9,10},{10,1... | collective-permute-start | bytes 2359304 | tf_op jit(solution)/shard_map/ppermute | solution.py:25
  9.4 8.9 %collective-permute-done = bf16[2,256,768]{2,1,0:T(8,128)(2,1)S(1)} collective-permute-done((bf16[2,256,768]{2,1,0:T(8,128)(2,1)S(1)}, bf16[2,256,768]{2,1,0:T(8,128)(2,1)S(1)}, u32[]{:S(2)}, u32[]{:S(2)}) %collective-permute-start) | collective-permute-done | bytes 786464 | tf_op jit(solution)/shard_map/ppermute | solution.py:25
  19.3 4.4 %collective-permute-start.1 = (bf16[2,256,768]{2,1,0:T(8,128)(2,1)S(1)}, bf16[2,256,768]{2,1,0:T(8,128)(2,1)S(1)}, u32[]{:S(2)}, u32[]{:S(2)}) collective-permute-start(bf16[2,256,768]{2,1,0:T(8,128)(2,1)S(1)} %collective-permute-done), channel_id=1, source_target_pairs={{0,1},{1,2},{2,3},{3,4},{4,5},{5,6},{6,7},{7,8},{8,9},{9,10},{10,1... | collective-permute-start | bytes 2359304 | tf_op jit(solution)/shard_map/ppermute | solution.py:25
  24.7 4.3 %compare_select_fusion.3 = f32[256,1]{0,1:T(1,128)S(1)} fusion(f32[]{:T(128)} %bitcast.43, f32[]{:T(128)} %bitcast.44, f32[]{:T(128)} %bitcast.45, f32[]{:T(128)} %bitcast.46, f32[]{:T(128)} %bitcast.47, f32[]{:T(128)} %bitcast.49, f32[]{:T(128)} %bitcast.48), kind=kLoop, calls=%fused_computation.113 | loop fusion | flops 5888 | bytes 1052 | tf_op jit(solution)/shard_map/gather | solution.py:184
  29.7 4.3 %compare_select_fusion.2 = s32[256,1]{0,1:T(1,128)S(1)} fusion(s32[]{:T(128)} %bitcast.9, s32[]{:T(128)} %bitcast.10, s32[]{:T(128)} %bitcast.11, s32[]{:T(128)} %bitcast.12, s32[]{:T(128)} %bitcast.13, s32[]{:T(128)} %bitcast.15, s32[]{:T(128)} %bitcast.14), kind=kLoop, calls=%fused_computation.112 | loop fusion | flops 5888 | bytes 1052 | tf_op jit(solution)/shard_map/gather | solution.py:152
  34.0 2.9 collective-permute-start.2
  37.0 12.1 %select_multiply_fusion = (f32[256]{0:T(256)}, s32[256]{0:T(256)S(1)}) fusion(pred[256]{0:T(512)(128)(4,1)S(1)} %compare_reduce_fusion, pred[256]{0:T(512)(128)(4,1)S(1)} %compare_reduce_fusion.1, pred[256]{0:T(512)(128)(4,1)S(1)} %compare_reduce_fusion.2, pred[256]{0:T(512)(128)(4,1)S(1)} %compare_reduce_fusion.3, ...), kind=kLoop, calls=%fused_computation.136 | loop fusion | flops 7168 | bytes 6472 | tf_op jit(solution)/shard_map/mul | solution.py:184
  50.1 3.4 collective-permute-start.3
  58.5 4.3 %collective-permute-done.3 = bf16[2,256,768]{2,1,0:T(8,128)(2,1)} collective-permute-done((bf16[2,256,768]{2,1,0:T(8,128)(2,1)}, bf16[2,256,768]{2,1,0:T(8,128)(2,1)}, u32[]{:S(2)}, u32[]{:S(2)}) %collective-permute-start.3) | collective-permute-done | bytes 786464 | tf_op jit(solution)/shard_map/ppermute | solution.py:25
  67.0 4.0 %copy.21 = bf16[1,1280,768]{1,2,0:T(8,128)(2,1)} copy(bf16[1,1280,768]{2,1,0:T(8,128)(2,1)} %get-tuple-element.193) | data formatting | bytes 3932160 | tf_op jit(solution)/shard_map/slice | solution.py:171
  70.9 2.3 copy.19
  73.2 127.1 %while.16 = (s32[]{:T(128)}, bf16[12,256,64]{1,2,0:T(8,128)(2,1)}, f32[12,1280,64]{1,2,0:T(8,128)}, f32[12,1280,64]{1,2,0:T(8,128)}, bf16[12,256,64]{1,2,0:T(8,1...) while((s32[]{:T(128)}, bf16[12,256,64]{1,2,0:T(8,128)(2,1)}, ...), condition=%wide.region_6.7_spmd.clone.clone, body=%wide.region_0.6_spmd.clone.clone.sunk | while | flops 240876800 | bytes 9070557 | solution.py:206
  79.8 2.5 fusion.113
  90.4 2.6 fusion.113
  101.0 2.6 fusion.113
  111.6 2.6 fusion.113
  122.2 2.6 fusion.113
  132.8 2.5 fusion.113
  143.4 2.6 fusion.113
  154.0 2.6 fusion.113
  164.5 2.6 fusion.113
  175.1 2.6 fusion.113
  185.7 2.6 fusion.113
  196.3 2.6 fusion.113
  201.9 2.2 collective-permute-start.4
  204.1 20.6 %collective-permute-done.4 = f32[2,256,768]{1,2,0:T(8,128)S(1)} collective-permute-done((f32[2,256,768]{1,2,0:T(8,128)S(1)}, f32[2,256,768]{1,2,0:T(8,128)S(1)}, u32[]{:S(2)}, u32[]{:S(2)}) %collective-permute-start.4) | collective-permute-done | bytes 1572896 | tf_op jit(solution)/shard_map/ppermute | solution.py:25
  226.8 19.8 %collective-permute-done.5 = f32[2,256,768]{1,2,0:T(8,128)S(1)} collective-permute-done((f32[2,256,768]{1,2,0:T(8,128)S(1)}, f32[2,256,768]{1,2,0:T(8,128)S(1)}, u32[]{:S(2)}, u32[]{:S(2)}) %collective-permute-start.5) | collective-permute-done | bytes 1572896 | tf_op jit(solution)/shard_map/ppermute | solution.py:25
  248.9 19.8 %collective-permute-done.6 = f32[2,256,768]{1,2,0:T(8,128)S(1)} collective-permute-done((f32[2,256,768]{1,2,0:T(8,128)S(1)}, f32[2,256,768]{1,2,0:T(8,128)S(1)}, u32[]{:S(2)}, u32[]{:S(2)}) %collective-permute-start.6) | collective-permute-done | bytes 1572896 | tf_op jit(solution)/shard_map/ppermute | solution.py:25
  270.1 2.1 collective-permute-start.7
  273.2 18.9 %collective-permute-done.7 = f32[2,256,768]{1,2,0:T(8,128)S(1)} collective-permute-done((f32[2,256,768]{1,2,0:T(8,128)}, f32[2,256,768]{1,2,0:T(8,128)S(1)}, u32[]{:S(2)}, u32[]{:S(2)}) %collective-permute-start.7) | collective-permute-done | bytes 1572896 | tf_op jit(solution)/shard_map/ppermute | solution.py:25
  295.7 2.8 multiply_reduce_fusion.1
  299.8 50.6 %shard_map.104 = f32[8,128]{1,0:T(8,128)} custom-call(f32[8,128]{1,0:T(8,128)} %broadcast_in_dim.70.part_ref), custom_call_target="tpu_custom_call" | custom-call | tf_op jit(solution)/shard_map/pallas_call | solution.py:90
  (254 shorter events, 127.5 us)
Async XLA Ops:
  0.6 2.7 copy-start.5
  0.7 2.7 copy-start.3
  3.4 20.3 %copy-start.15 = (s32[1,16,2]{1,2,0:T(2,128)S(1)}, s32[1,16,2]{1,2,0:T(2,128)}, u32[]{:S(2)}) copy-start(s32[1,16,2]{1,2,0:T(2,128)} %param.15) | copy-start | bytes 388
  3.4 20.6 %copy-start.16 = (s32[1,16]{1,0:T(1,128)S(1)}, s32[1,16]{1,0:T(1,128)}, u32[]{:S(2)}) copy-start(s32[1,16]{1,0:T(1,128)} %param.14) | copy-start | bytes 196
  3.4 25.6 %copy-start.12 = (s32[1,16]{1,0:T(1,128)S(1)}, s32[1,16]{1,0:T(1,128)}, u32[]{:S(2)}) copy-start(s32[1,16]{1,0:T(1,128)} %param.13) | copy-start | bytes 196
  3.4 45.6 %copy-start.18 = (bf16[768]{0:T(1024)(128)(2,1)S(1)}, bf16[768]{0:T(1024)(128)(2,1)}, u32[]{:S(2)}) copy-start(bf16[768]{0:T(1024)(128)(2,1)} %param.19) | copy-start | bytes 4612
  4.0 14.3 %collective-permute-start = (bf16[2,256,768]{2,1,0:T(8,128)(2,1)S(1)}, bf16[2,256,768]{2,1,0:T(8,128)(2,1)S(1)}, u32[]{:S(2)}, u32[]{:S(2)}) collective-permute-start(bf16[2,256,768]{2,1,0:T(8,128)(2,1)S(1)} %pad_maximum_fusion.1), channel_id=1, source_target_pairs={{0,1},{1,2},{2,3},{3,4},{4,5},{5,6},{6,7},{7,8},{8,9},{9,10},{10,1... | collective-permute-start | bytes 2359304 | tf_op jit(solution)/shard_map/ppermute | solution.py:25
  19.3 14.7 %collective-permute-start.1 = (bf16[2,256,768]{2,1,0:T(8,128)(2,1)S(1)}, bf16[2,256,768]{2,1,0:T(8,128)(2,1)S(1)}, u32[]{:S(2)}, u32[]{:S(2)}) collective-permute-start(bf16[2,256,768]{2,1,0:T(8,128)(2,1)S(1)} %collective-permute-done), channel_id=1, source_target_pairs={{0,1},{1,2},{2,3},{3,4},{4,5},{5,6},{6,7},{7,8},{8,9},{9,10},{10,1... | collective-permute-start | bytes 2359304 | tf_op jit(solution)/shard_map/ppermute | solution.py:25
  34.0 16.1 %copy-start.8 = (bf16[2,256,768]{2,1,0:T(8,128)(2,1)}, bf16[2,256,768]{2,1,0:T(8,128)(2,1)S(1)}, u32[]{:S(2)}) copy-start(bf16[2,256,768]{2,1,0:T(8,128)(2,1)S(1)} %collective-permute-done.1) | copy-start | bytes 2359300
  34.0 16.1 %collective-permute-start.2 = (bf16[2,256,768]{2,1,0:T(8,128)(2,1)S(1)}, bf16[2,256,768]{2,1,0:T(8,128)(2,1)}, u32[]{:S(2)}, u32[]{:S(2)}) collective-permute-start(bf16[2,256,768]{2,1,0:T(8,128)(2,1)S(1)} %collective-permute-done.1), channel_id=1, source_target_pairs={{0,1},{1,2},{2,3},{3,4},{4,5},{5,6},{6,7},{7,8},{8,9},{9,10},{10,1... | collective-permute-start | bytes 2359304 | tf_op jit(solution)/shard_map/ppermute | solution.py:25
  49.6 3.9 %copy-start.17 = (bf16[768,768]{1,0:T(8,128)(2,1)S(1)}, bf16[768,768]{1,0:T(8,128)(2,1)}, u32[]{:S(2)}) copy-start(bf16[768,768]{1,0:T(8,128)(2,1)} %param.16) | copy-start | bytes 3538948
  50.1 12.6 %collective-permute-start.3 = (bf16[2,256,768]{2,1,0:T(8,128)(2,1)}, bf16[2,256,768]{2,1,0:T(8,128)(2,1)}, u32[]{:S(2)}, u32[]{:S(2)}) collective-permute-start(bf16[2,256,768]{2,1,0:T(8,128)(2,1)} %collective-permute-done.2), channel_id=1, source_target_pairs={{0,1},{1,2},{2,3},{3,4},{4,5},{5,6},{6,7},{7,8},{8,9},{9,10},{10,1... | collective-permute-start | bytes 2359304 | tf_op jit(solution)/shard_map/ppermute | solution.py:25
  54.1 2.8 copy-start.11
  58.4 6.8 %copy-start.9 = (bf16[2,256,768]{2,1,0:T(8,128)(2,1)S(1)}, bf16[2,256,768]{2,1,0:T(8,128)(2,1)}, u32[]{:S(2)}) copy-start(bf16[2,256,768]{2,1,0:T(8,128)(2,1)} %copy-done.8) | copy-start | bytes 2359300
  73.2 2.7 copy-start.14
  83.8 2.7 copy-start.14
  94.4 2.7 copy-start.14
  115.6 2.7 copy-start.14
  126.2 2.7 copy-start.14
  147.4 2.7 copy-start.14
  157.9 2.7 copy-start.14
  168.5 2.7 copy-start.14
  179.1 2.7 copy-start.14
  189.7 2.7 copy-start.14
  200.3 24.4 %copy-start.1 = (f32[12,1280,64]{1,2,0:T(8,128)S(1)}, f32[12,1280,64]{1,2,0:T(8,128)}, u32[]{:S(2)}) copy-start(f32[12,1280,64]{1,2,0:T(8,128)} %get-tuple-element.71) | copy-start | bytes 11796484
  200.3 24.4 %copy-start.2 = (f32[12,1280,64]{1,2,0:T(8,128)S(1)}, f32[12,1280,64]{1,2,0:T(8,128)}, u32[]{:S(2)}) copy-start(f32[12,1280,64]{1,2,0:T(8,128)} %get-tuple-element.70) | copy-start | bytes 11796484
  201.9 22.7 %collective-permute-start.4 = (f32[2,256,768]{1,2,0:T(8,128)S(1)}, f32[2,256,768]{1,2,0:T(8,128)S(1)}, u32[]{:S(2)}, u32[]{:S(2)}) collective-permute-start(f32[2,256,768]{1,2,0:T(8,128)S(1)} %fusion.58), channel_id=1, source_target_pairs={{1,0},{2,1},{3,2},{4,3},{5,4},{6,5},{7,6},{8,7},{9,8},{10,9},{11,1... | collective-permute-start | bytes 4718600 | tf_op jit(solution)/shard_map/ppermute | solution.py:25
  224.9 21.7 %collective-permute-start.5 = (f32[2,256,768]{1,2,0:T(8,128)S(1)}, f32[2,256,768]{1,2,0:T(8,128)S(1)}, u32[]{:S(2)}, u32[]{:S(2)}) collective-permute-start(f32[2,256,768]{1,2,0:T(8,128)S(1)} %fusion.60), channel_id=1, source_target_pairs={{1,0},{2,1},{3,2},{4,3},{5,4},{6,5},{7,6},{8,7},{9,8},{10,9},{11,1... | collective-permute-start | bytes 4718600 | tf_op jit(solution)/shard_map/ppermute | solution.py:25
  246.8 25.4 %copy-start.10 = (bf16[12,256,64]{1,2,0:T(8,128)(2,1)S(1)}, bf16[12,256,64]{1,2,0:T(8,128)(2,1)}, u32[]{:S(2)}) copy-start(bf16[12,256,64]{1,2,0:T(8,128)(2,1)} %get-tuple-element.69) | copy-start | bytes 1179652
  246.8 21.9 %collective-permute-start.6 = (f32[2,256,768]{1,2,0:T(8,128)S(1)}, f32[2,256,768]{1,2,0:T(8,128)S(1)}, u32[]{:S(2)}, u32[]{:S(2)}) collective-permute-start(f32[2,256,768]{1,2,0:T(8,128)S(1)} %fusion.62), channel_id=1, source_target_pairs={{1,0},{2,1},{3,2},{4,3},{5,4},{6,5},{7,6},{8,7},{9,8},{10,9},{11,1... | collective-permute-start | bytes 4718600 | tf_op jit(solution)/shard_map/ppermute | solution.py:25
  270.1 21.9 %collective-permute-start.7 = (f32[2,256,768]{1,2,0:T(8,128)}, f32[2,256,768]{1,2,0:T(8,128)S(1)}, u32[]{:S(2)}, u32[]{:S(2)}) collective-permute-start(f32[2,256,768]{1,2,0:T(8,128)} %fusion.57), channel_id=1, source_target_pairs={{1,0},{2,1},{3,2},{4,3},{5,4},{6,5},{7,6},{8,7},{9,8},{10,9},{11,1... | collective-permute-start | bytes 4718600 | tf_op jit(solution)/shard_map/ppermute | solution.py:25
  273.2 20.5 %copy-start.4 = (bf16[768,768]{1,0:T(8,128)(2,1)S(1)}, bf16[768,768]{1,0:T(8,128)(2,1)}, u32[]{:S(2)}) copy-start(bf16[768,768]{1,0:T(8,128)(2,1)} %param.18) | copy-start | bytes 3538948
  (17 other events, 41.5 us)

commit v2 on v1

--- a/solution.py
+++ b/solution.py
@@ -138,6 +138,74 @@
     return (out_h, prob_clean, weight_clean, peak, denom, delta)
 
 
+def attention_kernel(place_ref, q_ref, kc_ref, vc_ref, kn_ref, vn_ref, g_ref,
+                     out_ref, dk_ref, dv_ref):
+    scale = 1.0 / math.sqrt(HEAD_DIM)
+    query = q_ref[0]
+    key_clean = kc_ref[0]
+    value_clean = vc_ref[0]
+    grad = g_ref[0]
+    rows, context = query.shape[0], key_clean.shape[0]
+    row_block = lax.broadcasted_iota(jnp.int32, (rows, context), 0) // BLOCK * BLOCK
+    col = lax.broadcasted_iota(jnp.int32, (rows, context), 1)
+    allow_clean = (col >= row_block) & (col < row_block + WINDOW) & (col >= place_ref[0])
+    own_row = lax.broadcasted_iota(jnp.int32, (rows, rows), 0) // BLOCK
+    own_col = lax.broadcasted_iota(jnp.int32, (rows, rows), 1) // BLOCK
+    allow_noisy = own_row == own_col
+    contract = (((1,), (1,)), ((), ()))
+    score_clean = lax.dot_general(query, key_clean, contract, preferred_element_type=jnp.float32) * scale
+    score_noisy = lax.dot_general(query, kn_ref[0], contract, preferred_element_type=jnp.float32) * scale
+    score_clean = jnp.where(allow_clean, score_clean, -jnp.inf)
+    score_noisy = jnp.where(allow_noisy, score_noisy, -jnp.inf)
+    peak = jnp.maximum(
+        jnp.max(score_clean, axis=-1, keepdims=True), jnp.max(score_noisy, axis=-1, keepdims=True)
+    )
+    exp_clean = jnp.where(allow_clean, jnp.exp(score_clean - peak), 0.0)
+    exp_noisy = jnp.where(allow_noisy, jnp.exp(score_noisy - peak), 0.0)
+    denom = jnp.sum(exp_clean, axis=-1, keepdims=True) + jnp.sum(exp_noisy, axis=-1, keepdims=True)
+    inverse = 1.0 / denom
+    prob_clean = exp_clean * inverse
+    weight_clean = prob_clean.astype(jnp.bfloat16)
+    weight_noisy = (exp_noisy * inverse).astype(jnp.bfloat16)
+    mixed = jnp.dot(weight_clean, value_clean, preferred_element_type=jnp.float32)
+    mixed = mixed + jnp.dot(weight_noisy, vn_ref[0], preferred_element_type=jnp.float32)
+    out_h = mixed.astype(jnp.bfloat16)
+    out_ref[0] = out_h
+    delta = jnp.sum(grad.astype(jnp.float32) * out_h.astype(jnp.float32), axis=-1, keepdims=True)
+    dprob = lax.dot_general(grad, value_clean, contract, preferred_element_type=jnp.float32)
+    dscore = (prob_clean * (dprob - delta) * scale).astype(jnp.bfloat16)
+    lead = (((0,), (0,)), ((), ()))
+    dk_ref[0] = lax.dot_general(dscore, query, lead, preferred_element_type=jnp.float32)
+    dv_ref[0] = lax.dot_general(weight_clean, grad, lead, preferred_element_type=jnp.float32)
+
+
+def attention_heads(place, query_h, key_h, value_h, nkey_h, nvalue_h, grad_h):
+    heads, rows, dim = query_h.shape
+    context = key_h.shape[1]
+    row_spec = pl.BlockSpec((1, rows, dim), lambda h, place: (h, 0, 0))
+    ctx_spec = pl.BlockSpec((1, context, dim), lambda h, place: (h, 0, 0))
+    flops = heads * 2 * dim * (5 * rows * context + 3 * rows * rows)
+    return pl.pallas_call(
+        attention_kernel,
+        out_shape=(
+            jax.ShapeDtypeStruct((heads, rows, dim), jnp.bfloat16),
+            jax.ShapeDtypeStruct((heads, context, dim), jnp.float32),
+            jax.ShapeDtypeStruct((heads, context, dim), jnp.float32),
+        ),
+        grid_spec=pltpu.PrefetchScalarGridSpec(
+            num_scalar_prefetch=1,
+            grid=(heads,),
+            in_specs=[row_spec, ctx_spec, ctx_spec, row_spec, row_spec, row_spec],
+            out_specs=[row_spec, ctx_spec, ctx_spec],
+        ),
+        cost_estimate=pl.CostEstimate(
+            flops=flops,
+            transcendentals=heads * rows * (context + rows),
+            bytes_accessed=heads * dim * (8 * rows + 4 * context + 8 * context),
+        ),
+    )(place, query_h, key_h, value_h, nkey_h, nvalue_h, grad_h)
+
+
 def on_device(clean, out_cot, mask_bits, levels, importance, w_query, w_key, w_value, mask_embed):
     clean_rows = clean[0]
     cotangent = out_cot[0]
@@ -192,18 +260,8 @@
         to_heads(grad_out),
     )
 
-    def full_pass(items):
-        query_h, key_h, value_h, nkey_h, nvalue_h, grad_h = items
-        out_h, prob_clean, weight_clean, peak, denom, delta = forward_head(
-            query_h, key_h, value_h, nkey_h, nvalue_h, grad_h, allow_clean, allow_noisy, scale
-        )
-        dprob = jnp.einsum("qe,ke->qk", grad_h, value_h, preferred_element_type=jnp.float32)
-        dscore = (prob_clean * (dprob - delta[:, None]) * scale).astype(jnp.bfloat16)
-        dkey_h = jnp.einsum("qk,qe->ke", dscore, query_h, preferred_element_type=jnp.float32)
-        dvalue_h = jnp.einsum("qk,qe->ke", weight_clean, grad_h, preferred_element_type=jnp.float32)
-        return (out_h, dkey_h, dvalue_h)
-
-    out_heads, dkey_heads, dvalue_heads = lax.map(full_pass, head_inputs)
+    place = jnp.reshape(span * tok_count - position, (1,)).astype(jnp.int32)
+    out_heads, dkey_heads, dvalue_heads = attention_heads(place, *head_inputs)
     terms = jnp.stack([from_heads(dkey_heads), from_heads(dvalue_heads)])
     running = terms[:, :tok_count]
     for step in range(span):

time: 357 us -> 285 us (0.80)
  matrix products: 126 us -> 12.9 us
  local copies, waits for them, and re-layouts: 20.5 us -> 48.3 us
  Pallas kernels: 50.6 us -> 78.1 us
  other arithmetic: 37.7 us -> 28.6 us
  waiting for transfers between devices: 92.3 us -> 88.6 us
    dot_general x72 -> x0, matrix products: 117 us -> none  [the longest x12 30.7 us: full_pass(): jnp.einsum('qk,qe->ke', dscore, query_h, preferred_element_type=jnp.float32)]
    pallas_call x0 -> x1, Pallas kernels: none -> 29 us  [attention_heads(): pl.pallas_call(attention_kernel, out_shape=(jax.ShapeDtypeStruct((heads,...]
    transpose x0 -> x3, local copies, waits for them, and re-layouts: none -> 14.5 us  [from_heads(): stacked.transpose(1, 0, 2).reshape(stacked.shape[1], HEADS * HEAD_DIM)]
    reduce_sum x36 -> x0, other arithmetic: 9.13 us -> none  [the longest x24 8.77 us: forward_head(): denom = jnp.sum(exp_clean, axis=-1) + jnp.sum(exp_noisy, axis=-1)]
    another operation x0 -> x2, local copies, waits for them, and re-layouts: none -> 6.22 us  [to_heads(): return rows.reshape(rows.shape[0], HEADS, HEAD_DIM).transpose(1, 0, 2)]
    ppermute x8, waiting for transfers between devices: 92.3 us -> 88.6 us  [from_behind(): return lax.ppermute(block, axis, route)]
    unnamed x39 -> x30, local copies, waits for them, and re-layouts: 5.76 us -> 7.88 us
  transfers between devices with their start and end apart: 8 -> 8, of which waited for: 6 -> 6; matrix products, arithmetic and copies ran while one was open for 8% -> 14% of each run, Pallas kernels for 0% -> 0%
where the time goes in v2:
time: 285 us; the launch traced here: 284 us
  waiting for transfers between devices  88.6 us (31%)
  Pallas kernels  78.1 us (27%)
  local copies, waits for them, and re-layouts  48.3 us (17%)
  other arithmetic  28.6 us (10%)
  starting transfers between devices  25.7 us (9%)
  matrix products  12.9 us (5%)
    ppermute x8, waiting for transfers between devices, from_behind(): return lax.ppermute(block, axis, route)  88.6 us
    pallas_call x1, Pallas kernels, global_total(): pl.pallas_call(functools.partial(total_kernel, axes, stages), out_shape=j...  49.1 us
    pallas_call x1, Pallas kernels, attention_heads(): pl.pallas_call(attention_kernel, out_shape=(jax.ShapeDtypeStruct((heads,...  29 us
    ppermute x8, starting transfers between devices, from_behind(): return lax.ppermute(block, axis, route)  25.7 us
    transpose x3, local copies, waits for them, and re-layouts, from_heads(): stacked.transpose(1, 0, 2).reshape(stacked.shape[1], HEADS * HEAD_DIM)  14.5 us
    mul x1, other arithmetic, on_device(): token_weight = block_weight[local_block] * bits.astype(jnp.float32)  11.3 us
    unnamed x30, local copies, waits for them, and re-layouts  7.88 us
    another operation x2, local copies, waits for them, and re-layouts, to_heads(): return rows.reshape(rows.shape[0], HEADS, HEAD_DIM).transpose(1, 0, 2)  6.22 us
  transfers between devices with their start and end apart: 8, of which 6 were waited for; matrix products, arithmetic and copies ran while one was open for 14% of the time, Pallas kernels for 0%

profile of v2, /device:TPU:1, one launch (start us, length us, event | category | flops | bytes accessed | tf_op | source)
XLA Modules:
  0.0 283.9 jit_solution(8444113306764718207)
XLA Ops:
  4.9 5.4 %collective-permute-start = (bf16[2,256,768]{2,1,0:T(8,128)(2,1)}, bf16[2,256,768]{2,1,0:T(8,128)(2,1)}, u32[]{:S(2)}, u32[]{:S(2)}) collective-permute-start(bf16[2,256,768]{2,1,0:T(8,128)(2,1)} %pad_maximum_fusion.1), channel_id=1, source_target_pairs={{0,1},{1,2},{2,3},{3,4},{4,5},{5,6},{6,7},{7,8},{8,9},{9,10},{10,1... | collective-permute-start | bytes 2359304 | tf_op jit(solution)/shard_map/ppermute | solution.py:25
  10.6 8.9 %collective-permute-done = bf16[2,256,768]{2,1,0:T(8,128)(2,1)} collective-permute-done((bf16[2,256,768]{2,1,0:T(8,128)(2,1)}, bf16[2,256,768]{2,1,0:T(8,128)(2,1)}, u32[]{:S(2)}, u32[]{:S(2)}) %collective-permute-start) | collective-permute-done | bytes 786464 | tf_op jit(solution)/shard_map/ppermute | solution.py:25
  19.5 4.4 %collective-permute-start.1 = (bf16[2,256,768]{2,1,0:T(8,128)(2,1)}, bf16[2,256,768]{2,1,0:T(8,128)(2,1)}, u32[]{:S(2)}, u32[]{:S(2)}) collective-permute-start(bf16[2,256,768]{2,1,0:T(8,128)(2,1)} %collective-permute-done), channel_id=1, source_target_pairs={{0,1},{1,2},{2,3},{3,4},{4,5},{5,6},{6,7},{7,8},{8,9},{9,10},{10,1... | collective-permute-start | bytes 2359304 | tf_op jit(solution)/shard_map/ppermute | solution.py:25
  24.7 4.4 %compare_select_fusion.2 = f32[256,1]{0,1:T(1,128)S(1)} fusion(f32[]{:T(128)} %bitcast.44, f32[]{:T(128)} %bitcast.45, f32[]{:T(128)} %bitcast.46, f32[]{:T(128)} %bitcast.47, f32[]{:T(128)} %bitcast.48, f32[]{:T(128)} %bitcast.50, f32[]{:T(128)} %bitcast.49), kind=kLoop, calls=%fused_computation.53 | loop fusion | flops 5888 | bytes 1052 | tf_op jit(solution)/shard_map/gather | solution.py:252
  29.8 3.4 %collective-permute-done.1 = bf16[2,256,768]{2,1,0:T(8,128)(2,1)} collective-permute-done((bf16[2,256,768]{2,1,0:T(8,128)(2,1)}, bf16[2,256,768]{2,1,0:T(8,128)(2,1)}, u32[]{:S(2)}, u32[]{:S(2)}) %collective-permute-start.1) | collective-permute-done | bytes 786464 | tf_op jit(solution)/shard_map/ppermute | solution.py:25
  33.1 4.4 %collective-permute-start.2 = (bf16[2,256,768]{2,1,0:T(8,128)(2,1)}, bf16[2,256,768]{2,1,0:T(8,128)(2,1)}, u32[]{:S(2)}, u32[]{:S(2)}) collective-permute-start(bf16[2,256,768]{2,1,0:T(8,128)(2,1)} %collective-permute-done.1), channel_id=1, source_target_pairs={{0,1},{1,2},{2,3},{3,4},{4,5},{5,6},{6,7},{7,8},{8,9},{9,10},{10,1... | collective-permute-start | bytes 2359304 | tf_op jit(solution)/shard_map/ppermute | solution.py:25
  37.5 4.5 %compare_select_fusion.1 = s32[256,1]{0,1:T(1,128)S(1)} fusion(s32[]{:T(128)} %bitcast.10, s32[]{:T(128)} %bitcast.11, s32[]{:T(128)} %bitcast.12, s32[]{:T(128)} %bitcast.13, s32[]{:T(128)} %bitcast.14, s32[]{:T(128)} %bitcast.16, s32[]{:T(128)} %bitcast.15), kind=kLoop, calls=%fused_computation.52 | loop fusion | flops 5888 | bytes 1052 | tf_op jit(solution)/shard_map/gather | solution.py:220
  42.0 11.3 %select_multiply_fusion = (f32[256]{0:T(256)S(1)}, s32[256]{0:T(256)S(1)}) fusion(pred[256]{0:T(512)(128)(4,1)S(1)} %compare_reduce_fusion, pred[256]{0:T(512)(128)(4,1)S(1)} %compare_reduce_fusion.1, pred[256]{0:T(512)(128)(4,1)S(1)} %compare_reduce_fusion.2, pred[256]{0:T(512)(128)(4,1)S(1)} %compare_reduce_fusion.3, ...), kind=kLoop, calls=%fused_computation.69 | loop fusion | flops 7168 | bytes 6472 | tf_op jit(solution)/shard_map/mul | solution.py:252
  56.9 2.0 collective-permute-start.3
  59.0 2.3 convolution_convert_fusion
  62.4 2.5 convolution_convert_fusion.4
  76.7 2.1 fusion.17
  78.9 2.7 copy.31
  81.5 3.1 %copy.32 = bf16[1280,12,64]{2,0,1:T(8,128)(2,1)} copy(bf16[1280,12,64]{0,2,1:T(8,128)(2,1)S(1)} %bitcast.106) | data formatting | bytes 3932160 | tf_op jit(solution)/shard_map/reshape;squeeze | solution.py:106
  84.6 2.7 copy.29
  87.3 3.1 %copy.30 = bf16[1280,12,64]{2,0,1:T(8,128)(2,1)} copy(bf16[1280,12,64]{0,2,1:T(8,128)(2,1)S(1)} %bitcast.107) | data formatting | bytes 3932160 | tf_op jit(solution)/shard_map/reshape;squeeze | solution.py:106
  90.4 29.0 %shard_map.104 = (bf16[12,256,64]{2,1,0:T(8,128)(2,1)}, f32[12,1280,64]{2,1,0:T(8,128)}, f32[12,1280,64]{2,1,0:T(8,128)}) custom-call(s32[1]{0:T(128)} %bitcast.place_ref, bf16[12,256,64]{2,1,0:T(8,128)(2,1)} %bitcast.109, bf16[12,1280,64]{2,1,0:T(8,128)(2,1)} %bitcast.103, bf16[12,1280,64]{2,1,0:T(8,128)(2,1)} %bitcast.102, bf16[12,256,64]{2,1,0:T(8,128)(2,1)} %bitcast.108, ...), custom_call_target="tpu_custom_call" | custom-call | flops 2818572288 | bytes 13369344 | tf_op jit(solution)/shard_map/pallas_call | solution.py:188
  119.4 6.5 %copy.41 = f32[1280,12,64]{0,2,1:T(8,128)} copy(f32[1280,12,64]{2,0,1:T(8,128)} %bitcast.105) | data formatting | bytes 7864320 | tf_op jit(solution)/shard_map/transpose | solution.py:110
  126.0 6.5 %copy.42 = f32[1280,12,64]{0,2,1:T(8,128)} copy(f32[1280,12,64]{2,0,1:T(8,128)} %bitcast.104) | data formatting | bytes 7864320 | tf_op jit(solution)/shard_map/transpose | solution.py:110
  132.5 1.6 fusion.2
  134.2 3.6 %collective-permute-start.4 = (f32[2,256,768]{1,2,0:T(8,128)S(1)}, f32[2,256,768]{1,2,0:T(8,128)S(1)}, u32[]{:S(2)}, u32[]{:S(2)}) collective-permute-start(f32[2,256,768]{1,2,0:T(8,128)S(1)} %fusion.2), channel_id=1, source_target_pairs={{1,0},{2,1},{3,2},{4,3},{5,4},{6,5},{7,6},{8,7},{9,8},{10,9},{11,1... | collective-permute-start | bytes 4718600 | tf_op jit(solution)/shard_map/ppermute | solution.py:25
  137.8 19.2 %collective-permute-done.4 = f32[2,256,768]{1,2,0:T(8,128)S(1)} collective-permute-done((f32[2,256,768]{1,2,0:T(8,128)S(1)}, f32[2,256,768]{1,2,0:T(8,128)S(1)}, u32[]{:S(2)}, u32[]{:S(2)}) %collective-permute-start.4) | collective-permute-done | bytes 1572896 | tf_op jit(solution)/shard_map/ppermute | solution.py:25
  157.1 1.9 collective-permute-start.5
  159.1 19.8 %collective-permute-done.5 = f32[2,256,768]{1,2,0:T(8,128)S(1)} collective-permute-done((f32[2,256,768]{1,2,0:T(8,128)S(1)}, f32[2,256,768]{1,2,0:T(8,128)S(1)}, u32[]{:S(2)}, u32[]{:S(2)}) %collective-permute-start.5) | collective-permute-done | bytes 1572896 | tf_op jit(solution)/shard_map/ppermute | solution.py:25
  179.1 1.9 collective-permute-start.6
  181.0 19.8 %collective-permute-done.6 = f32[2,256,768]{1,2,0:T(8,128)S(1)} collective-permute-done((f32[2,256,768]{1,2,0:T(8,128)S(1)}, f32[2,256,768]{1,2,0:T(8,128)S(1)}, u32[]{:S(2)}, u32[]{:S(2)}) %collective-permute-start.6) | collective-permute-done | bytes 1572896 | tf_op jit(solution)/shard_map/ppermute | solution.py:25
  202.2 2.1 collective-permute-start.7
  206.7 17.5 %collective-permute-done.7 = f32[2,256,768]{1,2,0:T(8,128)S(1)} collective-permute-done((f32[2,256,768]{1,2,0:T(8,128)}, f32[2,256,768]{1,2,0:T(8,128)S(1)}, u32[]{:S(2)}, u32[]{:S(2)}) %collective-permute-start.7) | collective-permute-done | bytes 1572896 | tf_op jit(solution)/shard_map/ppermute | solution.py:25
  224.2 1.6 fusion.7
  225.8 2.1 fusion.11
  227.8 2.8 multiply_reduce_fusion
  232.0 49.1 %shard_map.105 = f32[8,128]{1,0:T(8,128)} custom-call(f32[8,128]{1,0:T(8,128)} %broadcast_in_dim.29.part_ref), custom_call_target="tpu_custom_call" | custom-call | tf_op jit(solution)/shard_map/pallas_call | solution.py:90
  (66 shorter events, 30.0 us)
Async XLA Ops:
  0.6 1.3 copy-start
  0.6 2.7 copy-start.5
  0.7 2.7 copy-start.3
  3.4 20.5 %copy-start.9 = (s32[1,16,2]{1,2,0:T(2,128)S(1)}, s32[1,16,2]{1,2,0:T(2,128)}, u32[]{:S(2)}) copy-start(s32[1,16,2]{1,2,0:T(2,128)} %param.13) | copy-start | bytes 388
  3.4 20.5 %copy-start.10 = (s32[1,16]{1,0:T(1,128)S(1)}, s32[1,16]{1,0:T(1,128)}, u32[]{:S(2)}) copy-start(s32[1,16]{1,0:T(1,128)} %param.12) | copy-start | bytes 196
  3.4 25.6 %copy-start.8 = (s32[1,16]{1,0:T(1,128)S(1)}, s32[1,16]{1,0:T(1,128)}, u32[]{:S(2)}) copy-start(s32[1,16]{1,0:T(1,128)} %param.11) | copy-start | bytes 196
  3.4 49.9 %copy-start.11 = (bf16[768]{0:T(1024)(128)(2,1)S(1)}, bf16[768]{0:T(1024)(128)(2,1)}, u32[]{:S(2)}) copy-start(bf16[768]{0:T(1024)(128)(2,1)} %param.17) | copy-start | bytes 4612
  4.9 14.6 %collective-permute-start = (bf16[2,256,768]{2,1,0:T(8,128)(2,1)}, bf16[2,256,768]{2,1,0:T(8,128)(2,1)}, u32[]{:S(2)}, u32[]{:S(2)}) collective-permute-start(bf16[2,256,768]{2,1,0:T(8,128)(2,1)} %pad_maximum_fusion.1), channel_id=1, source_target_pairs={{0,1},{1,2},{2,3},{3,4},{4,5},{5,6},{6,7},{7,8},{8,9},{9,10},{10,1... | collective-permute-start | bytes 2359304 | tf_op jit(solution)/shard_map/ppermute | solution.py:25
  19.5 13.6 %collective-permute-start.1 = (bf16[2,256,768]{2,1,0:T(8,128)(2,1)}, bf16[2,256,768]{2,1,0:T(8,128)(2,1)}, u32[]{:S(2)}, u32[]{:S(2)}) collective-permute-start(bf16[2,256,768]{2,1,0:T(8,128)(2,1)} %collective-permute-done), channel_id=1, source_target_pairs={{0,1},{1,2},{2,3},{3,4},{4,5},{5,6},{6,7},{7,8},{8,9},{9,10},{10,1... | collective-permute-start | bytes 2359304 | tf_op jit(solution)/shard_map/ppermute | solution.py:25
  33.1 23.8 %collective-permute-start.2 = (bf16[2,256,768]{2,1,0:T(8,128)(2,1)}, bf16[2,256,768]{2,1,0:T(8,128)(2,1)}, u32[]{:S(2)}, u32[]{:S(2)}) collective-permute-start(bf16[2,256,768]{2,1,0:T(8,128)(2,1)} %collective-permute-done.1), channel_id=1, source_target_pairs={{0,1},{1,2},{2,3},{3,4},{4,5},{5,6},{6,7},{7,8},{8,9},{9,10},{10,1... | collective-permute-start | bytes 2359304 | tf_op jit(solution)/shard_map/ppermute | solution.py:25
  56.9 5.5 %copy-start.6 = (bf16[1,256,768]{2,1,0:T(8,128)(2,1)S(1)}, bf16[1,256,768]{2,1,0:T(8,128)(2,1)}, u32[]{:S(2)}) copy-start(bf16[1,256,768]{2,1,0:T(8,128)(2,1)} %param.9) | copy-start | bytes 1179652
  56.9 14.9 %collective-permute-start.3 = (bf16[2,256,768]{2,1,0:T(8,128)(2,1)}, bf16[2,256,768]{2,1,0:T(8,128)(2,1)}, u32[]{:S(2)}, u32[]{:S(2)}) collective-permute-start(bf16[2,256,768]{2,1,0:T(8,128)(2,1)} %collective-permute-done.2), channel_id=1, source_target_pairs={{0,1},{1,2},{2,3},{3,4},{4,5},{5,6},{6,7},{7,8},{8,9},{9,10},{10,1... | collective-permute-start | bytes 2359304 | tf_op jit(solution)/shard_map/ppermute | solution.py:25
  65.0 3.5 %copy-start.7 = (bf16[1,256,768]{2,1,0:T(8,128)(2,1)S(1)}, bf16[1,256,768]{2,1,0:T(8,128)(2,1)}, u32[]{:S(2)}) copy-start(bf16[1,256,768]{2,1,0:T(8,128)(2,1)} %param.10) | copy-start | bytes 1179652
  132.5 24.4 %copy-start.1 = (f32[1280,12,64]{0,2,1:T(8,128)S(1)}, f32[1280,12,64]{0,2,1:T(8,128)}, u32[]{:S(2)}) copy-start(f32[1280,12,64]{0,2,1:T(8,128)} %copy.41) | copy-start | bytes 11796484
  132.5 24.4 %copy-start.2 = (f32[1280,12,64]{0,2,1:T(8,128)S(1)}, f32[1280,12,64]{0,2,1:T(8,128)}, u32[]{:S(2)}) copy-start(f32[1280,12,64]{0,2,1:T(8,128)} %copy.42) | copy-start | bytes 11796484
  134.2 22.8 %collective-permute-start.4 = (f32[2,256,768]{1,2,0:T(8,128)S(1)}, f32[2,256,768]{1,2,0:T(8,128)S(1)}, u32[]{:S(2)}, u32[]{:S(2)}) collective-permute-start(f32[2,256,768]{1,2,0:T(8,128)S(1)} %fusion.2), channel_id=1, source_target_pairs={{1,0},{2,1},{3,2},{4,3},{5,4},{6,5},{7,6},{8,7},{9,8},{10,9},{11,1... | collective-permute-start | bytes 4718600 | tf_op jit(solution)/shard_map/ppermute | solution.py:25
  157.1 21.7 %collective-permute-start.5 = (f32[2,256,768]{1,2,0:T(8,128)S(1)}, f32[2,256,768]{1,2,0:T(8,128)S(1)}, u32[]{:S(2)}, u32[]{:S(2)}) collective-permute-start(f32[2,256,768]{1,2,0:T(8,128)S(1)} %fusion.4), channel_id=1, source_target_pairs={{1,0},{2,1},{3,2},{4,3},{5,4},{6,5},{7,6},{8,7},{9,8},{10,9},{11,1... | collective-permute-start | bytes 4718600 | tf_op jit(solution)/shard_map/ppermute | solution.py:25
  179.1 21.7 %collective-permute-start.6 = (f32[2,256,768]{1,2,0:T(8,128)S(1)}, f32[2,256,768]{1,2,0:T(8,128)S(1)}, u32[]{:S(2)}, u32[]{:S(2)}) collective-permute-start(f32[2,256,768]{1,2,0:T(8,128)S(1)} %fusion.6), channel_id=1, source_target_pairs={{1,0},{2,1},{3,2},{4,3},{5,4},{6,5},{7,6},{8,7},{9,8},{10,9},{11,1... | collective-permute-start | bytes 4718600 | tf_op jit(solution)/shard_map/ppermute | solution.py:25
  202.2 21.9 %collective-permute-start.7 = (f32[2,256,768]{1,2,0:T(8,128)}, f32[2,256,768]{1,2,0:T(8,128)S(1)}, u32[]{:S(2)}, u32[]{:S(2)}) collective-permute-start(f32[2,256,768]{1,2,0:T(8,128)} %fusion.1), channel_id=1, source_target_pairs={{1,0},{2,1},{3,2},{4,3},{5,4},{6,5},{7,6},{8,7},{9,8},{10,9},{11,1... | collective-permute-start | bytes 4718600 | tf_op jit(solution)/shard_map/ppermute | solution.py:25
  206.7 19.1 %copy-start.4 = (bf16[768,768]{1,0:T(8,128)(2,1)S(1)}, bf16[768,768]{1,0:T(8,128)(2,1)}, u32[]{:S(2)}) copy-start(bf16[768,768]{1,0:T(8,128)(2,1)} %param.16) | copy-start | bytes 3538948

commit v3 on v2

--- a/solution.py
+++ b/solution.py
@@ -206,6 +206,14 @@
     )(place, query_h, key_h, value_h, nkey_h, nvalue_h, grad_h)
 
 
+def project(rows, weight):
+    high = rows.astype(jnp.bfloat16)
+    low = (rows - high.astype(jnp.float32)).astype(jnp.bfloat16)
+    contract = (((1,), (1,)), ((), ()))
+    product = lax.dot_general(high, weight, contract, preferred_element_type=jnp.float32)
+    return product + lax.dot_general(low, weight, contract, preferred_element_type=jnp.float32)
+
+
 def on_device(clean, out_cot, mask_bits, levels, importance, w_query, w_key, w_value, mask_embed):
     clean_rows = clean[0]
     cotangent = out_cot[0]
@@ -223,20 +231,16 @@
     query = jnp.dot(noisy, w_query, preferred_element_type=jnp.float32).astype(jnp.bfloat16)
     key_noisy = jnp.dot(noisy, w_key, preferred_element_type=jnp.float32).astype(jnp.bfloat16)
     value_noisy = jnp.dot(noisy, w_value, preferred_element_type=jnp.float32).astype(jnp.bfloat16)
-    key_wide = w_key.astype(jnp.float32).T
-    value_wide = w_value.astype(jnp.float32).T
-    key_mine = jnp.dot(clean_rows, w_key, preferred_element_type=jnp.float32).astype(jnp.bfloat16)
-    value_mine = jnp.dot(clean_rows, w_value, preferred_element_type=jnp.float32).astype(
-        jnp.bfloat16
-    )
-    carried = jnp.stack([key_mine, value_mine])
+    carried = clean_rows
     collected = [carried]
     for step in range(span):
         carried = from_behind(carried, "seq", 1)
         collected.insert(0, carried)
-    window_kv = jnp.concatenate(collected, axis=1)
-    key_clean = window_kv[0]
-    value_clean = window_kv[1]
+    window_rows = jnp.concatenate(collected, axis=0)
+    key_clean = jnp.dot(window_rows, w_key, preferred_element_type=jnp.float32).astype(jnp.bfloat16)
+    value_clean = jnp.dot(window_rows, w_value, preferred_element_type=jnp.float32).astype(
+        jnp.bfloat16
+    )
     context = key_clean.shape[0]
     ctx_pos = position - span * tok_count + jnp.arange(context, dtype=jnp.int32)
     q_start = (position + local) // BLOCK * BLOCK
@@ -262,13 +266,12 @@
 
     place = jnp.reshape(span * tok_count - position, (1,)).astype(jnp.int32)
     out_heads, dkey_heads, dvalue_heads = attention_heads(place, *head_inputs)
-    terms = jnp.stack([from_heads(dkey_heads), from_heads(dvalue_heads)])
-    running = terms[:, :tok_count]
+    terms = project(from_heads(dkey_heads), w_key) + project(from_heads(dvalue_heads), w_value)
+    running = terms[:tok_count]
     for step in range(span):
-        running = from_behind(running, "seq", -1)
-        running = running + terms[:, (step + 1) * tok_count : (step + 2) * tok_count]
-    raw = jnp.dot(running[0], key_wide, precision=lax.Precision.HIGHEST)
-    raw = raw + jnp.dot(running[1], value_wide, precision=lax.Precision.HIGHEST)
+        running = from_behind(running.astype(jnp.bfloat16), "seq", -1).astype(jnp.float32)
+        running = running + terms[(step + 1) * tok_count : (step + 2) * tok_count]
+    raw = running
     attn_rows = from_heads(out_heads)
     squares = jnp.sum(raw * raw)
     total_squares = global_total(squares, ("dp", "seq"))

time: 285 us -> 219 us (0.77)
  waiting for transfers between devices: 88.6 us -> 30.1 us
  local copies, waits for them, and re-layouts: 48.3 us -> 36.5 us
  matrix products: 12.9 us -> 18.5 us
  Pallas kernels: 78.1 us -> 74.1 us
  other arithmetic: 28.6 us -> 32.3 us
    ppermute x8, waiting for transfers between devices: 88.6 us -> 30.1 us  [from_behind(): return lax.ppermute(block, axis, route)]
    dot_general x4 -> x6, matrix products: 6.84 us -> 15.9 us  [the longest x2 5.57 us: project(): lax.dot_general(low, weight, contract, preferred_element_type=jnp.float32)]
    reshape x3 -> x5, local copies, waits for them, and re-layouts: 3.5 us -> 11.6 us  [to_heads(): return rows.reshape(rows.shape[0], HEADS, HEAD_DIM).transpose(1, 0, 2)]
    slice x3 -> x1, local copies, waits for them, and re-layouts: 7.49 us -> 0.04 us  [on_device(): running = terms[:tok_count]]
    another operation x2 -> x0, local copies, waits for them, and re-layouts: 6.22 us -> none  [to_heads(): return rows.reshape(rows.shape[0], HEADS, HEAD_DIM).transpose(1, 0, 2)]
    convert_element_type x0 -> x5, other arithmetic: none -> 5.41 us  [the longest x2 5.14 us: project(): low = (rows - high.astype(jnp.float32)).astype(jnp.bfloat16)]
    pallas_call x1, Pallas kernels: 49.1 us -> 45.1 us  [global_total(): pl.pallas_call(functools.partial(total_kernel, axes, stages), out_shape=j...]
    add x4 -> x0, other arithmetic: 3.41 us -> none  [on_device(): running = running + terms[:, (step + 1) * tok_count:(step + 2) * tok_count]]
  transfers between devices with their start and end apart: 8 -> 8, of which waited for: 6 -> 5; matrix products, arithmetic and copies ran while one was open for 14% -> 15% of each run, Pallas kernels for 0% -> 0%
where the time goes in v3:
time: 219 us; the launch traced here: 218 us
  Pallas kernels  74.1 us (34%)
  local copies, waits for them, and re-layouts  36.5 us (17%)
  other arithmetic  32.3 us (15%)
  waiting for transfers between devices  30.1 us (14%)
  starting transfers between devices  24.4 us (11%)
  matrix products  18.5 us (8%)
    pallas_call x1, Pallas kernels, global_total(): pl.pallas_call(functools.partial(total_kernel, axes, stages), out_shape=j...  45.1 us
    ppermute x8, waiting for transfers between devices, from_behind(): return lax.ppermute(block, axis, route)  30.1 us
    pallas_call x1, Pallas kernels, attention_heads(): pl.pallas_call(attention_kernel, out_shape=(jax.ShapeDtypeStruct((heads,...  29 us
    ppermute x8, starting transfers between devices, from_behind(): return lax.ppermute(block, axis, route)  24.4 us
    transpose x3, local copies, waits for them, and re-layouts, from_heads(): stacked.transpose(1, 0, 2).reshape(stacked.shape[1], HEADS * HEAD_DIM)  13.4 us
    reshape x5, local copies, waits for them, and re-layouts, to_heads(): return rows.reshape(rows.shape[0], HEADS, HEAD_DIM).transpose(1, 0, 2)  11.6 us
    mul x1, other arithmetic, on_device(): token_weight = block_weight[local_block] * bits.astype(jnp.float32)  11.4 us
    unnamed x38, local copies, waits for them, and re-layouts  5.63 us
  transfers between devices with their start and end apart: 8, of which 5 were waited for; matrix products, arithmetic and copies ran while one was open for 15% of the time, Pallas kernels for 0%

profile of v3, /device:TPU:1, one launch (start us, length us, event | category | flops | bytes accessed | tf_op | source)
XLA Modules:
  0.0 217.6 jit_solution(2692036133766077601)
XLA Ops:
  0.7 5.7 %collective-permute-start = (bf16[256,768]{1,0:T(8,128)(2,1)}, bf16[256,768]{1,0:T(8,128)(2,1)S(1)}, u32[]{:S(2)}, u32[]{:S(2)}) collective-permute-start(bf16[256,768]{1,0:T(8,128)(2,1)} %bitcast.110), channel_id=1, source_target_pairs={{0,1},{1,2},{2,3},{3,4},{4,5},{5,6},{6,7},{7,8},{8,9},{9,10},{10,1... | collective-permute-start | bytes 1179656 | tf_op jit(solution)/shard_map/ppermute | solution.py:25
  8.7 4.3 %compare_select_fusion.2 = f32[256,1]{0,1:T(1,128)S(1)} fusion(f32[]{:T(128)} %bitcast.42, f32[]{:T(128)} %bitcast.43, f32[]{:T(128)} %bitcast.44, f32[]{:T(128)} %bitcast.45, f32[]{:T(128)} %bitcast.46, f32[]{:T(128)} %bitcast.48, f32[]{:T(128)} %bitcast.47), kind=kLoop, calls=%fused_computation.42 | loop fusion | flops 5888 | bytes 1052 | tf_op jit(solution)/shard_map/gather | solution.py:256
  13.0 1.9 fusion.9
  15.0 4.3 %compare_select_fusion.1 = s32[256,1]{0,1:T(1,128)S(1)} fusion(s32[]{:T(128)} %bitcast.10, s32[]{:T(128)} %bitcast.11, s32[]{:T(128)} %bitcast.12, s32[]{:T(128)} %bitcast.13, s32[]{:T(128)} %bitcast.14, s32[]{:T(128)} %bitcast.16, s32[]{:T(128)} %bitcast.15), kind=kLoop, calls=%fused_computation.41 | loop fusion | flops 5888 | bytes 1052 | tf_op jit(solution)/shard_map/gather | solution.py:228
  20.0 1.9 collective-permute-start.1
  22.0 11.4 %select_multiply_fusion = (f32[256]{0:T(256)S(1)}, s32[256]{0:T(256)S(1)}) fusion(pred[256]{0:T(512)(128)(4,1)S(1)} %compare_reduce_fusion, pred[256]{0:T(512)(128)(4,1)S(1)} %compare_reduce_fusion.1, pred[256]{0:T(512)(128)(4,1)S(1)} %compare_reduce_fusion.2, pred[256]{0:T(512)(128)(4,1)S(1)} %compare_reduce_fusion.3, ...), kind=kLoop, calls=%fused_computation.58 | loop fusion | flops 7168 | bytes 6472 | tf_op jit(solution)/shard_map/mul | solution.py:256
  33.4 4.5 %collective-permute-start.2 = (bf16[256,768]{1,0:T(8,128)(2,1)S(1)}, bf16[256,768]{1,0:T(8,128)(2,1)}, u32[]{:S(2)}, u32[]{:S(2)}) collective-permute-start(bf16[256,768]{1,0:T(8,128)(2,1)S(1)} %collective-permute-done.1), channel_id=1, source_target_pairs={{0,1},{1,2},{2,3},{3,4},{4,5},{5,6},{6,7},{7,8},{8,9},{9,10},{10,1... | collective-permute-start | bytes 1179656 | tf_op jit(solution)/shard_map/ppermute | solution.py:25
  40.0 2.6 %collective-permute-done.2 = bf16[256,768]{1,0:T(8,128)(2,1)} collective-permute-done((bf16[256,768]{1,0:T(8,128)(2,1)S(1)}, bf16[256,768]{1,0:T(8,128)(2,1)}, u32[]{:S(2)}, u32[]{:S(2)}) %collective-permute-start.2) | collective-permute-done | bytes 393248 | tf_op jit(solution)/shard_map/ppermute | solution.py:25
  42.6 4.5 %collective-permute-start.3 = (bf16[256,768]{1,0:T(8,128)(2,1)}, bf16[256,768]{1,0:T(8,128)(2,1)}, u32[]{:S(2)}, u32[]{:S(2)}) collective-permute-start(bf16[256,768]{1,0:T(8,128)(2,1)} %collective-permute-done.2), channel_id=1, source_target_pairs={{0,1},{1,2},{2,3},{3,4},{4,5},{5,6},{6,7},{7,8},{8,9},{9,10},{10,1... | collective-permute-start | bytes 1179656 | tf_op jit(solution)/shard_map/ppermute | solution.py:25
  55.6 3.1 %convolution_convert_fusion = bf16[1280,768]{0,1:T(8,128)(2,1)} fusion(bf16[1280,768]{1,0:T(8,128)(2,1)S(1)} %constant_dynamic-update-slice_fusion, bf16[768,768]{1,0:T(8,128)(2,1)S(1)} %copy-done.5), kind=kOutput, calls=%fused_computation.7 | convolution fusion | flops 1510932480 | bytes 5111808 | tf_op jit(solution)/shard_map/dot_general | solution.py:241
  58.7 1.8 convolution_convert_fusion.1
  60.5 4.9 %copy.28 = bf16[1280,12,64]{2,0,1:T(8,128)(2,1)} copy(bf16[1280,12,64]{0,2,1:T(8,128)(2,1)} %bitcast.103) | data formatting | bytes 3932160 | tf_op jit(solution)/shard_map/reshape | solution.py:106
  65.4 3.1 %copy.27 = bf16[1280,12,64]{2,0,1:T(8,128)(2,1)} copy(bf16[1280,12,64]{0,2,1:T(8,128)(2,1)S(1)} %bitcast.102) | data formatting | bytes 3932160 | tf_op jit(solution)/shard_map/reshape | solution.py:106
  68.5 29.0 %shard_map.104 = (bf16[12,256,64]{2,1,0:T(8,128)(2,1)}, f32[12,1280,64]{2,1,0:T(8,128)}, f32[12,1280,64]{2,1,0:T(8,128)}) custom-call(s32[1]{0:T(128)} %bitcast.place_ref, bf16[12,256,64]{2,1,0:T(8,128)(2,1)} %bitcast.100, bf16[12,1280,64]{2,1,0:T(8,128)(2,1)} %bitcast.96, bf16[12,1280,64]{2,1,0:T(8,128)(2,1)} %bitcast.95, bf16[12,256,64]{2,1,0:T(8,128)(2,1)} %bitcast.99, ...), custom_call_target="tpu_custom_call" | custom-call | flops 2818572288 | bytes 13369344 | tf_op jit(solution)/shard_map/pallas_call | solution.py:188
  97.5 6.6 %copy.37 = f32[1280,12,64]{0,2,1:T(8,128)} copy(f32[1280,12,64]{2,0,1:T(8,128)} %bitcast.98) | data formatting | bytes 7864320 | tf_op jit(solution)/shard_map/transpose | solution.py:110
  104.1 2.5 %fusion.1 = (bf16[1280,768]{0,1:T(8,128)(2,1)S(1)}, bf16[1280,768]{0,1:T(8,128)(2,1)S(1)}) fusion(f32[1280,12,64]{0,2,1:T(8,128)} %copy.37), kind=kLoop, calls=%fused_computation.5 | loop fusion | flops 3932160 | bytes 7864320 | tf_op jit(solution)/shard_map/convert_element_type | solution.py:211
  106.6 3.7 %fusion.12 = f32[1280,768]{1,0:T(8,128)} fusion(bf16[1280,768]{0,1:T(8,128)(2,1)S(1)} %get-tuple-element.14, bf16[768,768]{1,0:T(8,128)(2,1)S(1)} %copy-done), kind=kOutput, calls=%fused_computation.67 | convolution fusion | flops 1509949440 | bytes 7077888 | tf_op jit(solution)/shard_map/dot_general | solution.py:214
  110.4 3.8 %fusion.11 = f32[1280,768]{1,0:T(8,128)} fusion(bf16[1280,768]{0,1:T(8,128)(2,1)S(1)} %get-tuple-element.15, bf16[768,768]{1,0:T(8,128)(2,1)S(1)} %copy-done), kind=kOutput, calls=%fused_computation.66 | convolution fusion | flops 1509949440 | bytes 7077888 | tf_op jit(solution)/shard_map/dot_general | solution.py:213
  114.1 6.6 %copy.38 = f32[1280,12,64]{0,2,1:T(8,128)} copy(f32[1280,12,64]{2,0,1:T(8,128)} %bitcast.97) | data formatting | bytes 7864320 | tf_op jit(solution)/shard_map/transpose | solution.py:110
  120.7 2.6 %fusion = (bf16[1280,768]{0,1:T(8,128)(2,1)S(1)}, bf16[1280,768]{0,1:T(8,128)(2,1)S(1)}) fusion(f32[1280,12,64]{0,2,1:T(8,128)} %copy.38), kind=kLoop, calls=%fused_computation.2 | loop fusion | flops 3932160 | bytes 7864320 | tf_op jit(solution)/shard_map/convert_element_type | solution.py:211
  126.6 1.8 add_add_fusion
  128.5 1.9 collective-permute-start.4
  130.5 7.2 %collective-permute-done.4 = bf16[256,768]{1,0:T(8,128)(2,1)S(1)} collective-permute-done((bf16[256,768]{1,0:T(8,128)(2,1)S(1)}, bf16[256,768]{1,0:T(8,128)(2,1)S(1)}, u32[]{:S(2)}, u32[]{:S(2)}) %collective-permute-start.4) | collective-permute-done | bytes 393248 | tf_op jit(solution)/shard_map/ppermute | solution.py:25
  137.7 2.1 collective-permute-start.5
  139.8 7.2 %collective-permute-done.5 = bf16[256,768]{1,0:T(8,128)(2,1)S(1)} collective-permute-done((bf16[256,768]{1,0:T(8,128)(2,1)S(1)}, bf16[256,768]{1,0:T(8,128)(2,1)S(1)}, u32[]{:S(2)}, u32[]{:S(2)}) %collective-permute-start.5) | collective-permute-done | bytes 393248 | tf_op jit(solution)/shard_map/ppermute | solution.py:25
  147.1 1.9 collective-permute-start.6
  149.0 7.2 %collective-permute-done.6 = bf16[256,768]{1,0:T(8,128)(2,1)S(1)} collective-permute-done((bf16[256,768]{1,0:T(8,128)(2,1)S(1)}, bf16[256,768]{1,0:T(8,128)(2,1)S(1)}, u32[]{:S(2)}, u32[]{:S(2)}) %collective-permute-start.6) | collective-permute-done | bytes 393248 | tf_op jit(solution)/shard_map/ppermute | solution.py:25
  156.2 1.9 collective-permute-start.7
  159.4 6.0 %collective-permute-done.7 = bf16[256,768]{1,0:T(8,128)(2,1)S(1)} collective-permute-done((bf16[256,768]{1,0:T(8,128)(2,1)S(1)}, bf16[256,768]{1,0:T(8,128)(2,1)S(1)}, u32[]{:S(2)}, u32[]{:S(2)}) %collective-permute-start.7) | collective-permute-done | bytes 393248 | tf_op jit(solution)/shard_map/ppermute | solution.py:25
  165.3 2.0 multiply_reduce_fusion
  168.5 45.1 %shard_map.105 = f32[8,128]{1,0:T(8,128)} custom-call(f32[8,128]{1,0:T(8,128)} %broadcast_in_dim.29.part_ref), custom_call_target="tpu_custom_call" | custom-call | tf_op jit(solution)/shard_map/pallas_call | solution.py:90
  215.5 2.1 multiply_bitcast_fusion
  (74 shorter events, 20.8 us)
Async XLA Ops:
  0.6 37.3 %copy-start = (bf16[768,768]{1,0:T(8,128)(2,1)S(1)}, bf16[768,768]{1,0:T(8,128)(2,1)}, u32[]{:S(2)}) copy-start(bf16[768,768]{1,0:T(8,128)(2,1)} %param.15) | copy-start | bytes 3538948
  0.6 38.8 %copy-start.9 = (bf16[1,256,768]{2,1,0:T(8,128)(2,1)S(1)}, bf16[1,256,768]{2,1,0:T(8,128)(2,1)}, u32[]{:S(2)}) copy-start(bf16[1,256,768]{2,1,0:T(8,128)(2,1)} %param.9) | copy-start | bytes 1179652
  0.7 38.8 %copy-start.15 = (bf16[768]{0:T(1024)(128)(2,1)S(1)}, bf16[768]{0:T(1024)(128)(2,1)}, u32[]{:S(2)}) copy-start(bf16[768]{0:T(1024)(128)(2,1)} %param.17) | copy-start | bytes 4612
  0.7 38.8 %copy-start.4 = (bf16[768,768]{1,0:T(8,128)(2,1)S(1)}, bf16[768,768]{1,0:T(8,128)(2,1)}, u32[]{:S(2)}) copy-start(bf16[768,768]{1,0:T(8,128)(2,1)} %param.16) | copy-start | bytes 3538948
  0.7 18.6 %collective-permute-start = (bf16[256,768]{1,0:T(8,128)(2,1)}, bf16[256,768]{1,0:T(8,128)(2,1)S(1)}, u32[]{:S(2)}, u32[]{:S(2)}) collective-permute-start(bf16[256,768]{1,0:T(8,128)(2,1)} %bitcast.110), channel_id=1, source_target_pairs={{0,1},{1,2},{2,3},{3,4},{4,5},{5,6},{6,7},{7,8},{8,9},{9,10},{10,1... | collective-permute-start | bytes 1179656 | tf_op jit(solution)/shard_map/ppermute | solution.py:25
  19.3 0.7 copy-start.10
  20.0 13.3 %collective-permute-start.1 = (bf16[256,768]{1,0:T(8,128)(2,1)S(1)}, bf16[256,768]{1,0:T(8,128)(2,1)S(1)}, u32[]{:S(2)}, u32[]{:S(2)}) collective-permute-start(bf16[256,768]{1,0:T(8,128)(2,1)S(1)} %collective-permute-done), channel_id=1, source_target_pairs={{0,1},{1,2},{2,3},{3,4},{4,5},{5,6},{6,7},{7,8},{8,9},{9,10},{10,1... | collective-permute-start | bytes 1179656 | tf_op jit(solution)/shard_map/ppermute | solution.py:25
  33.4 13.8 %copy-start.14 = (bf16[768,768]{1,0:T(8,128)(2,1)S(1)}, bf16[768,768]{1,0:T(8,128)(2,1)}, u32[]{:S(2)}) copy-start(bf16[768,768]{1,0:T(8,128)(2,1)} %param.14) | copy-start | bytes 3538948
  33.4 6.6 %copy-start.12 = (bf16[256,768]{1,0:T(8,128)(2,1)}, bf16[256,768]{1,0:T(8,128)(2,1)S(1)}, u32[]{:S(2)}) copy-start(bf16[256,768]{1,0:T(8,128)(2,1)S(1)} %collective-permute-done.1) | copy-start | bytes 1179652
  33.4 9.2 %collective-permute-start.2 = (bf16[256,768]{1,0:T(8,128)(2,1)S(1)}, bf16[256,768]{1,0:T(8,128)(2,1)}, u32[]{:S(2)}, u32[]{:S(2)}) collective-permute-start(bf16[256,768]{1,0:T(8,128)(2,1)S(1)} %collective-permute-done.1), channel_id=1, source_target_pairs={{0,1},{1,2},{2,3},{3,4},{4,5},{5,6},{6,7},{7,8},{8,9},{9,10},{10,1... | collective-permute-start | bytes 1179656 | tf_op jit(solution)/shard_map/ppermute | solution.py:25
  42.6 10.7 %collective-permute-start.3 = (bf16[256,768]{1,0:T(8,128)(2,1)}, bf16[256,768]{1,0:T(8,128)(2,1)}, u32[]{:S(2)}, u32[]{:S(2)}) collective-permute-start(bf16[256,768]{1,0:T(8,128)(2,1)} %collective-permute-done.2), channel_id=1, source_target_pairs={{0,1},{1,2},{2,3},{3,4},{4,5},{5,6},{6,7},{7,8},{8,9},{9,10},{10,1... | collective-permute-start | bytes 1179656 | tf_op jit(solution)/shard_map/ppermute | solution.py:25
  49.0 2.7 %copy-start.8 = (bf16[1,256,768]{2,1,0:T(8,128)(2,1)S(1)}, bf16[1,256,768]{2,1,0:T(8,128)(2,1)}, u32[]{:S(2)}) copy-start(bf16[1,256,768]{2,1,0:T(8,128)(2,1)} %param.10) | copy-start | bytes 1179652
  52.2 3.3 %copy-start.13 = (bf16[256,768]{1,0:T(8,128)(2,1)S(1)}, bf16[256,768]{1,0:T(8,128)(2,1)}, u32[]{:S(2)}) copy-start(bf16[256,768]{1,0:T(8,128)(2,1)} %copy-done.12) | copy-start | bytes 1179652
  52.2 3.3 %copy-start.11 = (bf16[256,768]{1,0:T(8,128)(2,1)S(1)}, bf16[256,768]{1,0:T(8,128)(2,1)}, u32[]{:S(2)}) copy-start(bf16[256,768]{1,0:T(8,128)(2,1)} %copy-done.10) | copy-start | bytes 1179652
  53.3 2.3 %copy-start.5 = (bf16[768,768]{1,0:T(8,128)(2,1)S(1)}, bf16[768,768]{1,0:T(8,128)(2,1)}, u32[]{:S(2)}) copy-start(bf16[768,768]{1,0:T(8,128)(2,1)} %param.16) | copy-start | bytes 3538948
  120.7 2.6 %copy-start.6 = (bf16[768,768]{1,0:T(8,128)(2,1)S(1)}, bf16[768,768]{1,0:T(8,128)(2,1)}, u32[]{:S(2)}) copy-start(bf16[768,768]{1,0:T(8,128)(2,1)} %param.16) | copy-start | bytes 3538948
  123.3 2.1 copy-start.2
  123.3 3.3 %copy-start.3 = (f32[1280,768]{1,0:T(8,128)S(1)}, f32[1280,768]{1,0:T(8,128)}, u32[]{:S(2)}) copy-start(f32[1280,768]{1,0:T(8,128)} %fusion.11) | copy-start | bytes 11796484
  128.5 27.7 %copy-start.1 = (f32[1280,768]{1,0:T(8,128)}, f32[1280,768]{1,0:T(8,128)S(1)}, u32[]{:S(2)}) copy-start(f32[1280,768]{1,0:T(8,128)S(1)} %add_add_fusion) | copy-start | bytes 11796484
  128.5 9.1 %collective-permute-start.4 = (bf16[256,768]{1,0:T(8,128)(2,1)S(1)}, bf16[256,768]{1,0:T(8,128)(2,1)S(1)}, u32[]{:S(2)}, u32[]{:S(2)}) collective-permute-start(bf16[256,768]{1,0:T(8,128)(2,1)S(1)} %slice.108), channel_id=1, source_target_pairs={{1,0},{2,1},{3,2},{4,3},{5,4},{6,5},{7,6},{8,7},{9,8},{10,9},{11,1... | collective-permute-start | bytes 1179656 | tf_op jit(solution)/shard_map/ppermute | solution.py:25
  137.7 20.5 %copy-start.7 = (bf16[12,256,64]{2,1,0:T(8,128)(2,1)S(1)}, bf16[12,256,64]{2,1,0:T(8,128)(2,1)}, u32[]{:S(2)}) copy-start(bf16[12,256,64]{2,1,0:T(8,128)(2,1)} %get-tuple-element.5) | copy-start | bytes 1179652
  137.7 9.2 %collective-permute-start.5 = (bf16[256,768]{1,0:T(8,128)(2,1)S(1)}, bf16[256,768]{1,0:T(8,128)(2,1)S(1)}, u32[]{:S(2)}, u32[]{:S(2)}) collective-permute-start(bf16[256,768]{1,0:T(8,128)(2,1)S(1)} %fusion.5), channel_id=1, source_target_pairs={{1,0},{2,1},{3,2},{4,3},{5,4},{6,5},{7,6},{8,7},{9,8},{10,9},{11,1... | collective-permute-start | bytes 1179656 | tf_op jit(solution)/shard_map/ppermute | solution.py:25
  147.1 9.1 %collective-permute-start.6 = (bf16[256,768]{1,0:T(8,128)(2,1)S(1)}, bf16[256,768]{1,0:T(8,128)(2,1)S(1)}, u32[]{:S(2)}, u32[]{:S(2)}) collective-permute-start(bf16[256,768]{1,0:T(8,128)(2,1)S(1)} %fusion.4), channel_id=1, source_target_pairs={{1,0},{2,1},{3,2},{4,3},{5,4},{6,5},{7,6},{8,7},{9,8},{10,9},{11,1... | collective-permute-start | bytes 1179656 | tf_op jit(solution)/shard_map/ppermute | solution.py:25
  156.2 9.1 %collective-permute-start.7 = (bf16[256,768]{1,0:T(8,128)(2,1)S(1)}, bf16[256,768]{1,0:T(8,128)(2,1)S(1)}, u32[]{:S(2)}, u32[]{:S(2)}) collective-permute-start(bf16[256,768]{1,0:T(8,128)(2,1)S(1)} %fusion.3), channel_id=1, source_target_pairs={{1,0},{2,1},{3,2},{4,3},{5,4},{6,5},{7,6},{8,7},{9,8},{10,9},{11,1... | collective-permute-start | bytes 1179656 | tf_op jit(solution)/shard_map/ppermute | solution.py:25

commit v4 on v3

v4 whole, which is shorter than its diff:
```python
import functools
import math

import jax
import jax.numpy as jnp
from jax import lax
from jax.sharding import PartitionSpec as P
from jax.experimental import pallas as pl
from jax.experimental.pallas import tpu as pltpu

HEADS = 12
HEAD_DIM = 64
BLOCK = 16
WINDOW = 1024
LEVELS = 16


EPS = 1e-06
CLIP = 0.25


def from_behind(block, axis, distance):
    devices = range(lax.axis_size(axis))
    route = [(i - distance, i) for i in devices if i - distance in devices]
    return lax.ppermute(block, axis, route)


def group_stages(axes):
    stages = []
    for axis in axes:
        rest, stride = lax.axis_size(axis), 1
        while rest > 1:
            size = max(g for g in range(1, 9) if rest % g == 0)
            stages.append((axis, stride, size))
            stride, rest = stride * size, rest // size
    return stages


def stage_peer(axis, stride, size, offset):
    index = lax.axis_index(axis)
    digit = (index // stride) % size
    return index + ((digit + offset) % size - digit) * stride


def device_of(axes, axis, peer):
    return tuple(peer if name == axis else lax.axis_index(name) for name in axes)


def total_kernel(axes, stages, part_ref, out_ref, slots, send_sems, recv_sems):
    barrier = pltpu.get_barrier_semaphore()
    greeted = 0
    for axis, stride, size in stages:
        for offset in range(1, size):
            peer = stage_peer(axis, stride, size, offset)
            pl.semaphore_signal(
                barrier, 1, device_id=device_of(axes, axis, peer),
                device_id_type=pl.DeviceIdType.MESH,
            )
            greeted += 1
    pl.semaphore_wait(barrier, greeted)
    current = part_ref[...]
    for number, (axis, stride, size) in enumerate(stages):
        digit = (lax.axis_index(axis) // stride) % size
        slots[number, digit] = current
        copies = []
        for offset in range(1, size):
            peer = stage_peer(axis, stride, size, offset)
            copy = pltpu.make_async_remote_copy(
                src_ref=slots.at[number, digit],
                dst_ref=slots.at[number, digit],
                send_sem=send_sems.at[number, offset],
                recv_sem=recv_sems.at[number, offset],
                device_id=device_of(axes, axis, peer),
                device_id_type=pl.DeviceIdType.MESH,
            )
            copy.start()
            copies.append(copy)
        for copy in copies:
            copy.wait()
        current = slots[number, 0]
        for member in range(1, size):
            current = current + slots[number, member]
    out_ref[...] = current


def global_total(value, axes):
    stages = group_stages(axes)
    widest = max(size for _, _, size in stages)
    part = jnp.broadcast_to(value.astype(jnp.float32), (8, 128))
    summed = pl.pallas_call(
        functools.partial(total_kernel, axes, stages),
        out_shape=jax.ShapeDtypeStruct((8, 128), jnp.float32),
        in_specs=[pl.BlockSpec(memory_space=pltpu.VMEM)],
        out_specs=pl.BlockSpec(memory_space=pltpu.VMEM),
        scratch_shapes=[
            pltpu.VMEM((len(stages), widest, 8, 128), jnp.float32),
            pltpu.SemaphoreType.DMA((len(stages), widest)),
            pltpu.SemaphoreType.DMA((len(stages), widest)),
        ],
        compiler_params=pltpu.CompilerParams(collective_id=0, has_side_effects=True),
    )(part)
    return summed[0, 0]


def attention_kernel(place_ref, q_ref, kc_ref, vc_ref, kn_ref, vn_ref, g_ref,
                     out_ref, dk_ref, dv_ref):
    scale = 1.0 / math.sqrt(HEAD_DIM)
    query = q_ref[...]
    key_clean = kc_ref[...]
    value_clean = vc_ref[...]
    key_noisy = kn_ref[...]
    value_noisy = vn_ref[...]
    grad = g_ref[...]
    rows, lanes = query.shape
    context = key_clean.shape[0]
    row_block = lax.broadcasted_iota(jnp.int32, (rows, context), 0) // BLOCK * BLOCK
    col = lax.broadcasted_iota(jnp.int32, (rows, context), 1)
    allow_clean = (col >= row_block) & (col < row_block + WINDOW) & (col >= place_ref[0])
    own_row = lax.broadcasted_iota(jnp.int32, (rows, rows), 0) // BLOCK
    own_col = lax.broadcasted_iota(jnp.int32, (rows, rows), 1) // BLOCK
    allow_noisy = own_row == own_col
    lane = lax.broadcasted_iota(jnp.int32, (1, lanes), 1) // HEAD_DIM
    contract = (((1,), (1,)), ((), ()))
    lead = (((0,), (0,)), ((), ()))
    zero = jnp.zeros((), jnp.bfloat16)
    outs, dks, dvs = [], [], []
    for head in range(lanes // HEAD_DIM):
        mine = lane == head
        query_h = jnp.where(mine, query, zero)
        grad_h = jnp.where(mine, grad, zero)
        score_clean = lax.dot_general(query_h, key_clean, contract, preferred_element_type=jnp.float32) * scale
        score_noisy = lax.dot_general(query_h, key_noisy, contract, preferred_element_type=jnp.float32) * scale
        score_clean = jnp.where(allow_clean, score_clean, -jnp.inf)
        score_noisy = jnp.where(allow_noisy, score_noisy, -jnp.inf)
        peak = jnp.maximum(
            jnp.max(score_clean, axis=-1, keepdims=True), jnp.max(score_noisy, axis=-1, keepdims=True)
        )
        exp_clean = jnp.where(allow_clean, jnp.exp(score_clean - peak), 0.0)
        exp_noisy = jnp.where(allow_noisy, jnp.exp(score_noisy - peak), 0.0)
        denom = jnp.sum(exp_clean, axis=-1, keepdims=True) + jnp.sum(exp_noisy, axis=-1, keepdims=True)
        inverse = 1.0 / denom
        prob_clean = exp_clean * inverse
        weight_clean = prob_clean.astype(jnp.bfloat16)
        weight_noisy = (exp_noisy * inverse).astype(jnp.bfloat16)
        mixed = jnp.dot(weight_clean, value_clean, preferred_element_type=jnp.float32)
        mixed = mixed + jnp.dot(weight_noisy, value_noisy, preferred_element_type=jnp.float32)
        out_h = mixed.astype(jnp.bfloat16)
        delta = jnp.sum(
            jnp.where(mine, grad.astype(jnp.float32) * out_h.astype(jnp.float32), 0.0),
            axis=-1, keepdims=True,
        )
        dprob = lax.dot_general(grad_h, value_clean, contract, preferred_element_type=jnp.float32)
        dscore = (prob_clean * (dprob - delta) * scale).astype(jnp.bfloat16)
        outs.append(out_h)
        dks.append(lax.dot_general(dscore, query, lead, preferred_element_type=jnp.float32))
        dvs.append(lax.dot_general(weight_clean, grad, lead, preferred_element_type=jnp.float32))
    out, dk, dv = outs[0], dks[0], dvs[0]
    for head in range(1, len(outs)):
        mine = lane == head
        out = jnp.where(mine, outs[head], out)
        dk = jnp.where(mine, dks[head], dk)
        dv = jnp.where(mine, dvs[head], dv)
    out_ref[...] = out
    dk_ref[...] = dk
    dv_ref[...] = dv


def attention_heads(place, query, key_clean, value_clean, key_noisy, value_noisy, grad):
    rows, width = query.shape
    context = key_clean.shape[0]
    lanes = 2 * HEAD_DIM
    pairs = width // lanes
    row_spec = pl.BlockSpec((rows, lanes), lambda p, place: (0, p))
    ctx_spec = pl.BlockSpec((context, lanes), lambda p, place: (0, p))
    flops = pairs * 2 * 2 * lanes * (5 * rows * context + 3 * rows * rows)
    return pl.pallas_call(
        attention_kernel,
        out_shape=(
            jax.ShapeDtypeStruct((rows, width), jnp.bfloat16),
            jax.ShapeDtypeStruct((context, width), jnp.float32),
            jax.ShapeDtypeStruct((context, width), jnp.float32),
        ),
        grid_spec=pltpu.PrefetchScalarGridSpec(
            num_scalar_prefetch=1,
            grid=(pairs,),
            in_specs=[row_spec, ctx_spec, ctx_spec, row_spec, row_spec, row_spec],
            out_specs=[row_spec, ctx_spec, ctx_spec],
        ),
        cost_estimate=pl.CostEstimate(
            flops=flops,
            transcendentals=width // HEAD_DIM * rows * (context + rows),
            bytes_accessed=width * (8 * rows + 4 * context + 8 * context),
        ),
    )(place, query, key_clean, value_clean, key_noisy, value_noisy, grad)


def project(rows, weight):
    high = rows.astype(jnp.bfloat16)
    low = (rows - high.astype(jnp.float32)).astype(jnp.bfloat16)
    contract = (((1,), (1,)), ((), ()))
    product = lax.dot_general(high, weight, contract, preferred_element_type=jnp.float32)
    return product + lax.dot_general(low, weight, contract, preferred_element_type=jnp.float32)


def on_device(clean, out_cot, mask_bits, levels, importance, w_query, w_key, w_value, mask_embed):
    clean_rows = clean[0]
    cotangent = out_cot[0]
    tok_count = clean_rows.shape[0]
    width = clean_rows.shape[1]
    span = WINDOW // tok_count
    scale = 1.0 / math.sqrt(HEAD_DIM)
    position = lax.axis_index("seq") * tok_count
    within = jnp.arange(BLOCK, dtype=jnp.int32)
    block_bits = jnp.right_shift(mask_bits[0][:, None], within[None, :]) & 1
    bits = block_bits.reshape(tok_count)
    masked = bits == 1
    noisy = jnp.where(masked[:, None], mask_embed[None, :], clean_rows)
    query = jnp.dot(noisy, w_query, preferred_element_type=jnp.float32).astype(jnp.bfloat16)
    key_noisy = jnp.dot(noisy, w_key, preferred_element_type=jnp.float32).astype(jnp.bfloat16)
    value_noisy = jnp.dot(noisy, w_value, preferred_element_type=jnp.float32).astype(jnp.bfloat16)
    carried = clean_rows
    collected = [carried]
    for step in range(span):
        carried = from_behind(carried, "seq", 1)
        collected.insert(0, carried)
    window_rows = jnp.concatenate(collected, axis=0)
    key_clean = jnp.dot(window_rows, w_key, preferred_element_type=jnp.float32).astype(jnp.bfloat16)
    value_clean = jnp.dot(window_rows, w_value, preferred_element_type=jnp.float32).astype(
        jnp.bfloat16
    )
    level_f = levels[0].astype(jnp.float32)
    ratio_f = importance[0].astype(jnp.float32)
    block_weight = LEVELS / level_f * (ratio_f[:, 0] / ratio_f[:, 1])
    token_weight = (block_weight[:, None] * block_bits.astype(jnp.float32)).reshape(tok_count)
    grad_out = (cotangent.astype(jnp.float32) * token_weight[:, None]).astype(jnp.bfloat16)
    place = jnp.reshape(span * tok_count - position, (1,)).astype(jnp.int32)
    attn_rows, dkey_rows, dvalue_rows = attention_heads(
        place, query, key_clean, value_clean, key_noisy, value_noisy, grad_out
    )
    terms = project(dkey_rows, w_key) + project(dvalue_rows, w_value)
    running = terms[:tok_count]
    for step in range(span):
        running = from_behind(running.astype(jnp.bfloat16), "seq", -1).astype(jnp.float32)
        running = running + terms[(step + 1) * tok_count : (step + 2) * tok_count]
    raw = running
    squares = jnp.sum(raw * raw)
    total_squares = global_total(squares, ("dp", "seq"))
    entries = float(tok_count * width * lax.axis_size("dp") * lax.axis_size("seq"))
    rms = jnp.sqrt(total_squares / entries + EPS)
    factor = jnp.minimum(1.0, CLIP / rms)
    return (attn_rows[None], (raw * factor)[None])


def solution(mesh):
    in_specs = (
        P("dp", "seq", None),
        P("dp", "seq", None),
        P("dp", "seq"),
        P("dp", "seq"),
        P("dp", "seq", None),
        P(),
        P(),
        P(),
        P(),
    )
    out_specs = (P("dp", "seq", None), P("dp", "seq", None))
    return jax.shard_map(
        on_device, mesh=mesh, in_specs=in_specs, out_specs=out_specs, check_vma=False
    )
```

time: 219 us -> 184 us (0.84)
  local copies, waits for them, and re-layouts: 36.5 us -> 6.04 us
  other arithmetic: 32.3 us -> 6.25 us
  waiting for transfers between devices: 30.1 us -> 39 us
  Pallas kernels: 74.1 us -> 80.1 us
  matrix products: 18.5 us -> 23.6 us
    transpose x3 -> x0, local copies, waits for them, and re-layouts: 13.4 us -> none  [from_heads(): stacked.transpose(1, 0, 2).reshape(stacked.shape[1], HEADS * HEAD_DIM)]
    reshape x5 -> x0, local copies, waits for them, and re-layouts: 11.6 us -> none  [to_heads(): return rows.reshape(rows.shape[0], HEADS, HEAD_DIM).transpose(1, 0, 2)]
    mul x2, other arithmetic: 12 us -> 0.74 us  [on_device(): block_weight[:, None] * block_bits.astype(jnp.float32)]
    ppermute x8, waiting for transfers between devices: 30.1 us -> 39 us  [from_behind(): return lax.ppermute(block, axis, route)]
    gather x11 -> x0, other arithmetic: 8.92 us -> none  [the longest x10 4.61 us: on_device(): bits = jnp.right_shift(mask_bits[0][local_block], within) & 1]
    pallas_call x1, Pallas kernels: 45.1 us -> 53.8 us  [global_total(): pl.pallas_call(functools.partial(total_kernel, axes, stages), out_shape=j...]
    convert_element_type x2 -> x1, other arithmetic: 5.14 us -> 0.91 us  [on_device(): (cotangent.astype(jnp.float32) * token_weight[:, None]).astype(jnp.bfloat16)]
    pallas_call x1, Pallas kernels: 29 us -> 26.3 us  [attention_heads(): pl.pallas_call(attention_kernel, out_shape=(jax.ShapeDtypeStruct((rows, w...]
  transfers between devices with their start and end apart: 8 -> 8, of which waited for: 5 -> 8; matrix products, arithmetic and copies ran while one was open for 15% -> 6% of each run, Pallas kernels for 0% -> 0%
where the time goes in v4:
time: 184 us; the launch traced here: 183 us
  Pallas kernels  80.1 us (44%)
  waiting for transfers between devices  39 us (21%)
  starting transfers between devices  26.5 us (14%)
  matrix products  23.6 us (13%)
  other arithmetic  6.25 us (3%)
  local copies, waits for them, and re-layouts  6.04 us (3%)
    pallas_call x1, Pallas kernels, global_total(): pl.pallas_call(functools.partial(total_kernel, axes, stages), out_shape=j...  53.8 us
    ppermute x8, waiting for transfers between devices, from_behind(): return lax.ppermute(block, axis, route)  39 us
    ppermute x8, starting transfers between devices, from_behind(): return lax.ppermute(block, axis, route)  26.5 us
    pallas_call x1, Pallas kernels, attention_heads(): pl.pallas_call(attention_kernel, out_shape=(jax.ShapeDtypeStruct((rows, w...  26.3 us
    dot_general x2, matrix products, project(): lax.dot_general(low, weight, contract, preferred_element_type=jnp.float32)  7.15 us
  transfers between devices with their start and end apart: 8, of which 8 were waited for; matrix products, arithmetic and copies ran while one was open for 6% of the time, Pallas kernels for 0%

profile of v4, /device:TPU:1, one launch (start us, length us, event | category | flops | bytes accessed | tf_op | source)
XLA Modules:
  0.0 183.0 jit_solution(7465293532191579324)
XLA Ops:
  0.7 5.7 %collective-permute-start = (bf16[256,768]{1,0:T(8,128)(2,1)}, bf16[256,768]{1,0:T(8,128)(2,1)S(1)}, u32[]{:S(2)}, u32[]{:S(2)}) collective-permute-start(bf16[256,768]{1,0:T(8,128)(2,1)} %bitcast.34), channel_id=1, source_target_pairs={{0,1},{1,2},{2,3},{3,4},{4,5},{5,6},{6,7},{7,8},{8,9},{9,10},{10,1... | collective-permute-start | bytes 1179656 | tf_op jit(solution)/shard_map/ppermute | solution.py:25
  7.8 3.5 %collective-permute-done = bf16[256,768]{1,0:T(8,128)(2,1)S(1)} collective-permute-done((bf16[256,768]{1,0:T(8,128)(2,1)}, bf16[256,768]{1,0:T(8,128)(2,1)S(1)}, u32[]{:S(2)}, u32[]{:S(2)}) %collective-permute-start) | collective-permute-done | bytes 393248 | tf_op jit(solution)/shard_map/ppermute | solution.py:25
  11.4 4.3 %collective-permute-start.1 = (bf16[256,768]{1,0:T(8,128)(2,1)S(1)}, bf16[256,768]{1,0:T(8,128)(2,1)}, u32[]{:S(2)}, u32[]{:S(2)}) collective-permute-start(bf16[256,768]{1,0:T(8,128)(2,1)S(1)} %collective-permute-done), channel_id=1, source_target_pairs={{0,1},{1,2},{2,3},{3,4},{4,5},{5,6},{6,7},{7,8},{8,9},{9,10},{10,1... | collective-permute-start | bytes 1179656 | tf_op jit(solution)/shard_map/ppermute | solution.py:25
  16.3 2.3 %convolution_convert_fusion.3.kn_ref = bf16[256,768]{1,0:T(8,128)(2,1)} fusion(bf16[768,768]{1,0:T(8,128)(2,1)S(1)} %copy-done, pred[256]{0:T(512)(128)(4,1)S(1)} %eq.12, bf16[768]{0:T(1024)(128)(2,1)} %param.17, bf16[1,256,768]{2,1,0:T(8,128)(2,1)} %param.9), kind=kOutput, calls=%fused_computation.7 | convolution fusion | flops 302383104 | bytes 1967872 | tf_op jit(solution)/shard_map/dot_general | solution.py:219
  18.6 1.7 collective-permute-done.1
  20.3 4.5 %collective-permute-start.2 = (bf16[256,768]{1,0:T(8,128)(2,1)}, bf16[256,768]{1,0:T(8,128)(2,1)}, u32[]{:S(2)}, u32[]{:S(2)}) collective-permute-start(bf16[256,768]{1,0:T(8,128)(2,1)} %collective-permute-done.1), channel_id=1, source_target_pairs={{0,1},{1,2},{2,3},{3,4},{4,5},{5,6},{6,7},{7,8},{8,9},{9,10},{10,1... | collective-permute-start | bytes 1179656 | tf_op jit(solution)/shard_map/ppermute | solution.py:25
  25.0 2.0 %convolution_convert_fusion.2.vn_ref = bf16[256,768]{1,0:T(8,128)(2,1)} fusion(bf16[768,768]{1,0:T(8,128)(2,1)S(1)} %copy-done.3, pred[256]{0:T(512)(128)(4,1)S(1)} %eq.12, bf16[768]{0:T(1024)(128)(2,1)} %param.17, bf16[1,256,768]{2,1,0:T(8,128)(2,1)S(1)} %copy-done.5), kind=kOutput, calls=%fused_computation.6 | convolution fusion | flops 302383104 | bytes 1967872 | tf_op jit(solution)/shard_map/dot_general | solution.py:220
  27.0 2.9 %collective-permute-done.2 = bf16[256,768]{1,0:T(8,128)(2,1)} collective-permute-done((bf16[256,768]{1,0:T(8,128)(2,1)}, bf16[256,768]{1,0:T(8,128)(2,1)}, u32[]{:S(2)}, u32[]{:S(2)}) %collective-permute-start.2) | collective-permute-done | bytes 393248 | tf_op jit(solution)/shard_map/ppermute | solution.py:25
  29.8 4.4 %collective-permute-start.3 = (bf16[256,768]{1,0:T(8,128)(2,1)}, bf16[256,768]{1,0:T(8,128)(2,1)}, u32[]{:S(2)}, u32[]{:S(2)}) collective-permute-start(bf16[256,768]{1,0:T(8,128)(2,1)} %collective-permute-done.2), channel_id=1, source_target_pairs={{0,1},{1,2},{2,3},{3,4},{4,5},{5,6},{6,7},{7,8},{8,9},{9,10},{10,1... | collective-permute-start | bytes 1179656 | tf_op jit(solution)/shard_map/ppermute | solution.py:25
  35.2 2.5 %convolution_convert_fusion.4.q_ref = bf16[256,768]{1,0:T(8,128)(2,1)} fusion(bf16[768,768]{1,0:T(8,128)(2,1)} %param.14, pred[256]{0:T(512)(128)(4,1)S(1)} %eq.12, bf16[768]{0:T(1024)(128)(2,1)} %param.17, bf16[1,256,768]{2,1,0:T(8,128)(2,1)S(1)} %copy-done.5), kind=kOutput, calls=%fused_computation.8 | convolution fusion | flops 302383104 | bytes 1967872 | tf_op jit(solution)/shard_map/dot_general | solution.py:218
  37.7 1.5 collective-permute-done.3
  40.3 1.0 constant_dynamic-update-slice_fusion.3
  41.3 1.0 constant_dynamic-update-slice_fusion.2
  42.4 3.0 %convolution_convert_fusion.vc_ref = bf16[1280,768]{1,0:T(8,128)(2,1)} fusion(bf16[1280,768]{1,0:T(8,128)(2,1)S(1)} %constant_dynamic-update-slice_fusion, bf16[768,768]{1,0:T(8,128)(2,1)S(1)} %copy-done.3), kind=kOutput, calls=%fused_computation.3 | convolution fusion | flops 1510932480 | bytes 5111808 | tf_op jit(solution)/shard_map/dot_general | solution.py:228
  45.4 3.1 %convolution_convert_fusion.1.kc_ref = bf16[1280,768]{1,0:T(8,128)(2,1)} fusion(bf16[1280,768]{1,0:T(8,128)(2,1)S(1)} %constant_dynamic-update-slice_fusion, bf16[768,768]{1,0:T(8,128)(2,1)S(1)} %copy-done), kind=kOutput, calls=%fused_computation.4 | convolution fusion | flops 1510932480 | bytes 5111808 | tf_op jit(solution)/shard_map/dot_general | solution.py:227
  48.5 26.3 %shard_map.104 = (bf16[256,768]{1,0:T(8,128)(2,1)}, f32[1280,768]{1,0:T(8,128)}, f32[1280,768]{1,0:T(8,128)}) custom-call(s32[1]{0:T(128)} %bitcast.place_ref, bf16[256,768]{1,0:T(8,128)(2,1)} %convolution_convert_fusion.4.q_ref, bf16[1280,768]{1,0:T(8,128)(2,1)} %convolution_convert_fusion.1.kc_ref, bf16[1280,768]{1,0:T(8,128)(2,1)} %convolution_convert_fusion.vc_ref, ...), custom_call_target="tpu_custom_call" | custom-call | flops 5637144576 | bytes 13369344 | tf_op jit(solution)/shard_map/pallas_call | solution.py:176
  74.8 5.2 %fusion = f32[1280,768]{1,0:T(8,128)S(1)} fusion(bf16[768,768]{1,0:T(8,128)(2,1)S(1)} %copy-done, f32[1280,768]{1,0:T(8,128)} %get-tuple-element.6), kind=kOutput, calls=%fused_computation.5 | convolution fusion | flops 1513881600 | bytes 9043968 | tf_op jit(solution)/shard_map/dot_general | solution.py:202
  80.1 1.8 fusion.5
  82.2 1.8 fusion.2
  83.9 1.9 %add_add_fusion = f32[1280,768]{1,0:T(8,128)S(1)} fusion(f32[1280,768]{1,0:T(8,128)S(1)} %fusion.2, f32[1280,768]{1,0:T(8,128)S(1)} %fusion.5, f32[1280,768]{1,0:T(8,128)S(1)} %fusion, bf16[768,768]{1,0:T(8,128)(2,1)S(1)} %copy-done.3, f32[1280,768]{1,0:T(8,128)S(1)} %copy-done.2), kind=kOutput, calls=%fused_computation | convolution fusion | flops 1516830720 | bytes 20840448 | tf_op jit(solution)/shard_map/dot_general | solution.py:202
  85.9 1.9 %collective-permute-start.4 = (bf16[256,768]{1,0:T(8,128)(2,1)S(1)}, bf16[256,768]{1,0:T(8,128)(2,1)S(1)}, u32[]{:S(2)}, u32[]{:S(2)}) collective-permute-start(bf16[256,768]{1,0:T(8,128)(2,1)S(1)} %slice.55), channel_id=1, source_target_pairs={{1,0},{2,1},{3,2},{4,3},{5,4},{6,5},{7,6},{8,7},{9,8},{10,9},{11,1... | collective-permute-start | bytes 1179656 | tf_op jit(solution)/shard_map/ppermute | solution.py:25
  87.8 7.9 %collective-permute-done.4 = bf16[256,768]{1,0:T(8,128)(2,1)S(1)} collective-permute-done((bf16[256,768]{1,0:T(8,128)(2,1)S(1)}, bf16[256,768]{1,0:T(8,128)(2,1)S(1)}, u32[]{:S(2)}, u32[]{:S(2)}) %collective-permute-start.4) | collective-permute-done | bytes 393248 | tf_op jit(solution)/shard_map/ppermute | solution.py:25
  95.8 1.9 %collective-permute-start.5 = (bf16[256,768]{1,0:T(8,128)(2,1)S(1)}, bf16[256,768]{1,0:T(8,128)(2,1)S(1)}, u32[]{:S(2)}, u32[]{:S(2)}) collective-permute-start(bf16[256,768]{1,0:T(8,128)(2,1)S(1)} %fusion.9), channel_id=1, source_target_pairs={{1,0},{2,1},{3,2},{4,3},{5,4},{6,5},{7,6},{8,7},{9,8},{10,9},{11,1... | collective-permute-start | bytes 1179656 | tf_op jit(solution)/shard_map/ppermute | solution.py:25
  97.8 7.2 %collective-permute-done.5 = bf16[256,768]{1,0:T(8,128)(2,1)S(1)} collective-permute-done((bf16[256,768]{1,0:T(8,128)(2,1)S(1)}, bf16[256,768]{1,0:T(8,128)(2,1)S(1)}, u32[]{:S(2)}, u32[]{:S(2)}) %collective-permute-start.5) | collective-permute-done | bytes 393248 | tf_op jit(solution)/shard_map/ppermute | solution.py:25
  105.0 1.9 %collective-permute-start.6 = (bf16[256,768]{1,0:T(8,128)(2,1)S(1)}, bf16[256,768]{1,0:T(8,128)(2,1)S(1)}, u32[]{:S(2)}, u32[]{:S(2)}) collective-permute-start(bf16[256,768]{1,0:T(8,128)(2,1)S(1)} %fusion.8), channel_id=1, source_target_pairs={{1,0},{2,1},{3,2},{4,3},{5,4},{6,5},{7,6},{8,7},{9,8},{10,9},{11,1... | collective-permute-start | bytes 1179656 | tf_op jit(solution)/shard_map/ppermute | solution.py:25
  106.9 7.2 %collective-permute-done.6 = bf16[256,768]{1,0:T(8,128)(2,1)S(1)} collective-permute-done((bf16[256,768]{1,0:T(8,128)(2,1)S(1)}, bf16[256,768]{1,0:T(8,128)(2,1)S(1)}, u32[]{:S(2)}, u32[]{:S(2)}) %collective-permute-start.6) | collective-permute-done | bytes 393248 | tf_op jit(solution)/shard_map/ppermute | solution.py:25
  114.2 1.9 %collective-permute-start.7 = (bf16[256,768]{1,0:T(8,128)(2,1)S(1)}, bf16[256,768]{1,0:T(8,128)(2,1)S(1)}, u32[]{:S(2)}, u32[]{:S(2)}) collective-permute-start(bf16[256,768]{1,0:T(8,128)(2,1)S(1)} %fusion.7), channel_id=1, source_target_pairs={{1,0},{2,1},{3,2},{4,3},{5,4},{6,5},{7,6},{8,7},{9,8},{10,9},{11,1... | collective-permute-start | bytes 1179656 | tf_op jit(solution)/shard_map/ppermute | solution.py:25
  116.1 7.2 %collective-permute-done.7 = bf16[256,768]{1,0:T(8,128)(2,1)S(1)} collective-permute-done((bf16[256,768]{1,0:T(8,128)(2,1)S(1)}, bf16[256,768]{1,0:T(8,128)(2,1)S(1)}, u32[]{:S(2)}, u32[]{:S(2)}) %collective-permute-start.7) | collective-permute-done | bytes 393248 | tf_op jit(solution)/shard_map/ppermute | solution.py:25
  124.1 1.2 broadcast_in_dim.32.part_ref
  125.3 53.8 %shard_map.105 = f32[8,128]{1,0:T(8,128)} custom-call(f32[8,128]{1,0:T(8,128)} %broadcast_in_dim.32.part_ref), custom_call_target="tpu_custom_call" | custom-call | tf_op jit(solution)/shard_map/pallas_call | solution.py:90
  179.1 1.2 slice.32
  180.9 2.1 %multiply_bitcast_fusion = f32[1,256,768]{2,1,0:T(8,128)} fusion(f32[1280,768]{1,0:T(8,128)} %copy-done.1, bf16[256,768]{1,0:T(8,128)(2,1)S(1)} %collective-permute-done.7, f32[]{:T(128)} %bitcast.8), kind=kLoop, calls=%fused_computation.25 | loop fusion | flops 589824 | bytes 1966084 | tf_op jit(solution)/shard_map/broadcast_in_dim | solution.py:251
  (31 shorter events, 5.8 us)
Async XLA Ops:
  0.6 15.7 %copy-start = (bf16[768,768]{1,0:T(8,128)(2,1)S(1)}, bf16[768,768]{1,0:T(8,128)(2,1)}, u32[]{:S(2)}) copy-start(bf16[768,768]{1,0:T(8,128)(2,1)} %param.15) | copy-start | bytes 3538948
  0.6 24.4 %copy-start.5 = (bf16[1,256,768]{2,1,0:T(8,128)(2,1)S(1)}, bf16[1,256,768]{2,1,0:T(8,128)(2,1)}, u32[]{:S(2)}) copy-start(bf16[1,256,768]{2,1,0:T(8,128)(2,1)} %param.9) | copy-start | bytes 1179652
  0.7 24.2 %copy-start.6 = (s32[1,16]{1,0:T(1,128)S(1)}, s32[1,16]{1,0:T(1,128)}, u32[]{:S(2)}) copy-start(s32[1,16]{1,0:T(1,128)} %param.11) | copy-start | bytes 196
  0.7 24.3 %copy-start.3 = (bf16[768,768]{1,0:T(8,128)(2,1)S(1)}, bf16[768,768]{1,0:T(8,128)(2,1)}, u32[]{:S(2)}) copy-start(bf16[768,768]{1,0:T(8,128)(2,1)} %param.16) | copy-start | bytes 3538948
  0.7 10.7 %collective-permute-start = (bf16[256,768]{1,0:T(8,128)(2,1)}, bf16[256,768]{1,0:T(8,128)(2,1)S(1)}, u32[]{:S(2)}, u32[]{:S(2)}) collective-permute-start(bf16[256,768]{1,0:T(8,128)(2,1)} %bitcast.34), channel_id=1, source_target_pairs={{0,1},{1,2},{2,3},{3,4},{4,5},{5,6},{6,7},{7,8},{8,9},{9,10},{10,1... | collective-permute-start | bytes 1179656 | tf_op jit(solution)/shard_map/ppermute | solution.py:25
  11.4 9.0 %collective-permute-start.1 = (bf16[256,768]{1,0:T(8,128)(2,1)S(1)}, bf16[256,768]{1,0:T(8,128)(2,1)}, u32[]{:S(2)}, u32[]{:S(2)}) collective-permute-start(bf16[256,768]{1,0:T(8,128)(2,1)S(1)} %collective-permute-done), channel_id=1, source_target_pairs={{0,1},{1,2},{2,3},{3,4},{4,5},{5,6},{6,7},{7,8},{8,9},{9,10},{10,1... | collective-permute-start | bytes 1179656 | tf_op jit(solution)/shard_map/ppermute | solution.py:25
  16.3 17.9 %copy-start.4 = (bf16[1,256,768]{2,1,0:T(8,128)(2,1)S(1)}, bf16[1,256,768]{2,1,0:T(8,128)(2,1)}, u32[]{:S(2)}) copy-start(bf16[1,256,768]{2,1,0:T(8,128)(2,1)} %param.10) | copy-start | bytes 1179652
  20.3 9.5 %collective-permute-start.2 = (bf16[256,768]{1,0:T(8,128)(2,1)}, bf16[256,768]{1,0:T(8,128)(2,1)}, u32[]{:S(2)}, u32[]{:S(2)}) collective-permute-start(bf16[256,768]{1,0:T(8,128)(2,1)} %collective-permute-done.1), channel_id=1, source_target_pairs={{0,1},{1,2},{2,3},{3,4},{4,5},{5,6},{6,7},{7,8},{8,9},{9,10},{10,1... | collective-permute-start | bytes 1179656 | tf_op jit(solution)/shard_map/ppermute | solution.py:25
  29.8 9.4 %collective-permute-start.3 = (bf16[256,768]{1,0:T(8,128)(2,1)}, bf16[256,768]{1,0:T(8,128)(2,1)}, u32[]{:S(2)}, u32[]{:S(2)}) collective-permute-start(bf16[256,768]{1,0:T(8,128)(2,1)} %collective-permute-done.2), channel_id=1, source_target_pairs={{0,1},{1,2},{2,3},{3,4},{4,5},{5,6},{6,7},{7,8},{8,9},{9,10},{10,1... | collective-permute-start | bytes 1179656 | tf_op jit(solution)/shard_map/ppermute | solution.py:25
  74.8 5.3 %copy-start.7 = (f32[1280,768]{1,0:T(8,128)S(1)}, f32[1280,768]{1,0:T(8,128)}, u32[]{:S(2)}) copy-start(f32[1280,768]{1,0:T(8,128)} %get-tuple-element.6) | copy-start | bytes 11796484
  80.0 2.1 %copy-start.2 = (f32[1280,768]{1,0:T(8,128)S(1)}, f32[1280,768]{1,0:T(8,128)}, u32[]{:S(2)}) copy-start(f32[1280,768]{1,0:T(8,128)} %get-tuple-element.7) | copy-start | bytes 11796484
  85.8 37.5 %copy-start.1 = (f32[1280,768]{1,0:T(8,128)}, f32[1280,768]{1,0:T(8,128)S(1)}, u32[]{:S(2)}) copy-start(f32[1280,768]{1,0:T(8,128)S(1)} %add_add_fusion) | copy-start | bytes 11796484
  85.9 9.8 %collective-permute-start.4 = (bf16[256,768]{1,0:T(8,128)(2,1)S(1)}, bf16[256,768]{1,0:T(8,128)(2,1)S(1)}, u32[]{:S(2)}, u32[]{:S(2)}) collective-permute-start(bf16[256,768]{1,0:T(8,128)(2,1)S(1)} %slice.55), channel_id=1, source_target_pairs={{1,0},{2,1},{3,2},{4,3},{5,4},{6,5},{7,6},{8,7},{9,8},{10,9},{11,1... | collective-permute-start | bytes 1179656 | tf_op jit(solution)/shard_map/ppermute | solution.py:25
  95.8 9.1 %collective-permute-start.5 = (bf16[256,768]{1,0:T(8,128)(2,1)S(1)}, bf16[256,768]{1,0:T(8,128)(2,1)S(1)}, u32[]{:S(2)}, u32[]{:S(2)}) collective-permute-start(bf16[256,768]{1,0:T(8,128)(2,1)S(1)} %fusion.9), channel_id=1, source_target_pairs={{1,0},{2,1},{3,2},{4,3},{5,4},{6,5},{7,6},{8,7},{9,8},{10,9},{11,1... | collective-permute-start | bytes 1179656 | tf_op jit(solution)/shard_map/ppermute | solution.py:25
  105.0 9.1 %collective-permute-start.6 = (bf16[256,768]{1,0:T(8,128)(2,1)S(1)}, bf16[256,768]{1,0:T(8,128)(2,1)S(1)}, u32[]{:S(2)}, u32[]{:S(2)}) collective-permute-start(bf16[256,768]{1,0:T(8,128)(2,1)S(1)} %fusion.8), channel_id=1, source_target_pairs={{1,0},{2,1},{3,2},{4,3},{5,4},{6,5},{7,6},{8,7},{9,8},{10,9},{11,1... | collective-permute-start | bytes 1179656 | tf_op jit(solution)/shard_map/ppermute | solution.py:25
  114.2 9.1 %collective-permute-start.7 = (bf16[256,768]{1,0:T(8,128)(2,1)S(1)}, bf16[256,768]{1,0:T(8,128)(2,1)S(1)}, u32[]{:S(2)}, u32[]{:S(2)}) collective-permute-start(bf16[256,768]{1,0:T(8,128)(2,1)S(1)} %fusion.7), channel_id=1, source_target_pairs={{1,0},{2,1},{3,2},{4,3},{5,4},{6,5},{7,6},{8,7},{9,8},{10,9},{11,1... | collective-permute-start | bytes 1179656 | tf_op jit(solution)/shard_map/ppermute | solution.py:25

commit v5 on v4

--- a/solution.py
+++ b/solution.py
@@ -194,6 +194,143 @@
     )(place, query, key_clean, value_clean, key_noisy, value_noisy, grad)
 
 
+def chain_barrier(axes, left, right, has_left, has_right):
+    barrier = pltpu.get_barrier_semaphore()
+    for peer, present in ((left, has_left), (right, has_right)):
+        @pl.when(present)
+        def _():
+            pl.semaphore_signal(
+                barrier, 1, device_id=device_of(axes, "seq", peer),
+                device_id_type=pl.DeviceIdType.MESH,
+            )
+    pl.semaphore_wait(barrier, has_left.astype(jnp.int32) + has_right.astype(jnp.int32))
+
+
+def chain_ends(axes):
+    me = lax.axis_index("seq")
+    size = lax.axis_size("seq")
+    left = jnp.maximum(me - 1, 0)
+    right = jnp.minimum(me + 1, size - 1)
+    return me, left, right, me > 0, me < size - 1
+
+
+def sum_back_kernel(axes, span, chunks, terms_ref, raw_ref, sent, got, send_sems, recv_sems):
+    me, left, right, has_left, has_right = chain_ends(axes)
+    chain_barrier(axes, left, right, has_left, has_right)
+    rows = raw_ref.shape[0]
+    piece = rows // chunks
+
+    @pl.when(jnp.logical_not(has_right))
+    def _():
+        got[...] = jnp.zeros(got.shape, got.dtype)
+
+    def copy(step, chunk):
+        return pltpu.make_async_remote_copy(
+            src_ref=sent.at[step, chunk], dst_ref=got.at[step, chunk],
+            send_sem=send_sems.at[step, chunk], recv_sem=recv_sems.at[step, chunk],
+            device_id=device_of(axes, "seq", left), device_id_type=pl.DeviceIdType.MESH,
+        )
+
+    for step in range(span + 1):
+        for chunk in range(chunks):
+            value = terms_ref[pl.ds(step * rows + chunk * piece, piece), :]
+            if step > 0:
+                @pl.when(has_right)
+                def _():
+                    copy(step - 1, chunk).wait_recv()
+
+                value = value + got[step - 1, chunk].astype(jnp.float32)
+            if step < span:
+                sent[step, chunk] = value.astype(jnp.bfloat16)
+
+                @pl.when(has_left)
+                def _():
+                    copy(step, chunk).start()
+            else:
+                raw_ref[pl.ds(chunk * piece, piece), :] = value
+    for step in range(span):
+        for chunk in range(chunks):
+            @pl.when(has_left)
+            def _():
+                copy(step, chunk).wait_send()
+
+
+def sum_back(terms, span, rows, axes, chunks=4):
+    width = terms.shape[1]
+    piece = rows // chunks
+    return pl.pallas_call(
+        functools.partial(sum_back_kernel, axes, span, chunks),
+        out_shape=jax.ShapeDtypeStruct((rows, width), jnp.float32),
+        in_specs=[pl.BlockSpec(memory_space=pltpu.VMEM)],
+        out_specs=pl.BlockSpec(memory_space=pltpu.VMEM),
+        scratch_shapes=[
+            pltpu.VMEM((span, chunks, piece, width), jnp.bfloat16),
+            pltpu.VMEM((span, chunks, piece, width), jnp.bfloat16),
+            pltpu.SemaphoreType.DMA((span, chunks)),
+            pltpu.SemaphoreType.DMA((span, chunks)),
+        ],
+        compiler_params=pltpu.CompilerParams(collective_id=1, has_side_effects=True),
+    )(terms)
+
+
+def gather_front_kernel(axes, span, chunks, own_ref, window_ref, got, send_sems, recv_sems):
+    me, left, right, has_left, has_right = chain_ends(axes)
+    chain_barrier(axes, left, right, has_left, has_right)
+    rows = own_ref.shape[0]
+    piece = rows // chunks
+    for step in range(span):
+        @pl.when(step >= me)
+        def _():
+            got[step] = jnp.zeros(got.shape[1:], got.dtype)
+
+    def copy(step, chunk):
+        if step == 0:
+            source = own_ref.at[pl.ds(chunk * piece, piece)]
+        else:
+            source = got.at[step - 1, chunk]
+        return pltpu.make_async_remote_copy(
+            src_ref=source, dst_ref=got.at[step, chunk],
+            send_sem=send_sems.at[step, chunk], recv_sem=recv_sems.at[step, chunk],
+            device_id=device_of(axes, "seq", right), device_id_type=pl.DeviceIdType.MESH,
+        )
+
+    for step in range(span + 1):
+        for chunk in range(chunks):
+            if step > 0:
+                @pl.when(step <= me)
+                def _():
+                    copy(step - 1, chunk).wait_recv()
+            if step < span:
+                @pl.when(has_right & (step <= me))
+                def _():
+                    copy(step, chunk).start()
+    for step in range(span):
+        window_ref[pl.ds((span - 1 - step) * rows, rows), :] = got[step].reshape(rows, -1)
+    window_ref[pl.ds(span * rows, rows), :] = own_ref[...]
+    for step in range(span):
+        for chunk in range(chunks):
+            @pl.when(has_right & (step <= me))
+            def _():
+                copy(step, chunk).wait_send()
+
+
+def gather_front(own, span, axes, chunks=4):
+    rows, width = own.shape
+    piece = rows // chunks
+    return pl.pallas_call(
+        functools.partial(gather_front_kernel, axes, span, chunks),
+        out_shape=jax.ShapeDtypeStruct(((span + 1) * rows, width), own.dtype),
+        in_specs=[pl.BlockSpec(memory_space=pltpu.VMEM)],
+        out_specs=pl.BlockSpec(memory_space=pltpu.VMEM),
+        scratch_shapes=[
+            pltpu.VMEM((span, chunks, piece, width), own.dtype),
+            pltpu.SemaphoreType.DMA((span, chunks)),
+            pltpu.SemaphoreType.DMA((span, chunks)),
+        ],
+        compiler_params=pltpu.CompilerParams(collective_id=2, has_side_effects=True),
+    )(own)
+
+
 def project(rows, weight):
     high = rows.astype(jnp.bfloat16)
     low = (rows - high.astype(jnp.float32)).astype(jnp.bfloat16)
@@ -218,12 +355,7 @@
     query = jnp.dot(noisy, w_query, preferred_element_type=jnp.float32).astype(jnp.bfloat16)
     key_noisy = jnp.dot(noisy, w_key, preferred_element_type=jnp.float32).astype(jnp.bfloat16)
     value_noisy = jnp.dot(noisy, w_value, preferred_element_type=jnp.float32).astype(jnp.bfloat16)
-    carried = clean_rows
-    collected = [carried]
-    for step in range(span):
-        carried = from_behind(carried, "seq", 1)
-        collected.insert(0, carried)
-    window_rows = jnp.concatenate(collected, axis=0)
+    window_rows = gather_front(clean_rows, span, ("dp", "seq"))
     key_clean = jnp.dot(window_rows, w_key, preferred_element_type=jnp.float32).astype(jnp.bfloat16)
     value_clean = jnp.dot(window_rows, w_value, preferred_element_type=jnp.float32).astype(
         jnp.bfloat16
@@ -238,11 +370,7 @@
         place, query, key_clean, value_clean, key_noisy, value_noisy, grad_out
     )
     terms = project(dkey_rows, w_key) + project(dvalue_rows, w_value)
-    running = terms[:tok_count]
-    for step in range(span):
-        running = from_behind(running.astype(jnp.bfloat16), "seq", -1).astype(jnp.float32)
-        running = running + terms[(step + 1) * tok_count : (step + 2) * tok_count]
-    raw = running
+    raw = sum_back(terms, span, tok_count, ("dp", "seq"))
     squares = jnp.sum(raw * raw)
     total_squares = global_total(squares, ("dp", "seq"))
     entries = float(tok_count * width * lax.axis_size("dp") * lax.axis_size("seq"))

time: 184 us -> 145 us (0.79)
  waiting for transfers between devices: 39 us -> 0 us
  starting transfers between devices: 26.5 us -> 0 us
  Pallas kernels: 80.1 us -> 105 us
  local copies, waits for them, and re-layouts: 6.04 us -> 3.01 us
  other arithmetic: 6.25 us -> 8.94 us
    pallas_call x0 -> x2, Pallas kernels: none -> 48.8 us  [the longest x1 29.6 us: sum_back(): pl.pallas_call(functools.partial(sum_back_kernel, axes, span, chunks), ou...]
    ppermute x8 -> x0, waiting for transfers between devices: 39 us -> none  [from_behind(): return lax.ppermute(block, axis, route)]
    ppermute x8 -> x0, starting transfers between devices: 26.5 us -> none  [from_behind(): return lax.ppermute(block, axis, route)]
    pallas_call x1, Pallas kernels: 53.8 us -> 30.4 us  [global_total(): pl.pallas_call(functools.partial(total_kernel, axes, stages), out_shape=j...]
    unnamed x20 -> x16, local copies, waits for them, and re-layouts: 3.45 us -> 0.36 us
    dot_general x2, matrix products: 7.15 us -> 9.19 us  [project(): lax.dot_general(low, weight, contract, preferred_element_type=jnp.float32)]
  transfers between devices with their start and end apart: 8 -> 0, of which waited for: 8 -> 0; matrix products, arithmetic and copies ran while one was open for 6% -> 0% of each run, Pallas kernels for 0% -> 0%
where the time goes in v5:
time: 145 us; the launch traced here: 144 us
  Pallas kernels  105 us (72%)
  matrix products  25.4 us (18%)
  other arithmetic  8.94 us (6%)
  local copies, waits for them, and re-layouts  3.01 us (2%)
  between operations  1.45 us (1%)
    pallas_call x1, Pallas kernels, global_total(): pl.pallas_call(functools.partial(total_kernel, axes, stages), out_shape=j...  30.4 us
    pallas_call x1, Pallas kernels, sum_back(): pl.pallas_call(functools.partial(sum_back_kernel, axes, span, chunks), ou...  29.6 us
    pallas_call x1, Pallas kernels, attention_heads(): pl.pallas_call(attention_kernel, out_shape=(jax.ShapeDtypeStruct((rows, w...  26.2 us
    pallas_call x1, Pallas kernels, gather_front(): pl.pallas_call(functools.partial(gather_front_kernel, axes, span, chunks)...  19.2 us
    dot_general x2, matrix products, project(): lax.dot_general(low, weight, contract, preferred_element_type=jnp.float32)  9.19 us
    dot_general x1, matrix products, on_device(): jnp.dot(window_rows, w_value, preferred_element_type=jnp.float32)  4.75 us
    dot_general x2, matrix products, project(): lax.dot_general(high, weight, contract, preferred_element_type=jnp.float32)  3.53 us
    dot_general x1, matrix products, on_device(): jnp.dot(window_rows, w_key, preferred_element_type=jnp.float32)  2.98 us

profile of v5, /device:TPU:1, one launch (start us, length us, event | category | flops | bytes accessed | tf_op | source)
XLA Modules:
  0.0 144.3 jit_solution(2883991216466997771)
XLA Ops:
  0.6 0.0 copy-start
  0.6 0.0 copy-start.3
  0.7 0.0 copy-start.4
  0.7 0.0 copy-start.6
  0.7 0.8 convert_bitcast_fusion
  1.5 0.7 fusion.9
  2.2 0.7 fusion.8
  2.9 0.1 eq.12
  3.0 0.7 convert_multiply_fusion.1
  3.7 0.1 mul.46
  3.8 1.9 %fusion.7.g_ref = bf16[256,768]{1,0:T(8,128)(2,1)} fusion(bf16[1,256,768]{2,1,0:T(8,128)(2,1)} %param.10, f32[256]{0:T(256)S(1)} %mul.46), kind=kLoop, calls=%fused_computation.16 | loop fusion | flops 589824 | bytes 787456 | tf_op jit(solution)/shard_map/convert_element_type | solution.py:367
  5.7 2.4 %convolution_convert_fusion.3.kn_ref = bf16[256,768]{1,0:T(8,128)(2,1)} fusion(bf16[768,768]{1,0:T(8,128)(2,1)S(1)} %copy-done, pred[256]{0:T(512)(128)(4,1)S(1)} %eq.12, bf16[768]{0:T(1024)(128)(2,1)} %param.17, bf16[1,256,768]{2,1,0:T(8,128)(2,1)} %param.9), kind=kOutput, calls=%fused_computation.7 | convolution fusion | flops 302383104 | bytes 1967872 | tf_op jit(solution)/shard_map/dot_general | solution.py:356
  8.1 1.3 convolution_convert_fusion.2.vn_ref
  9.4 0.0 copy-done.5
  9.4 1.3 convolution_convert_fusion.4.q_ref
  10.7 19.2 %shard_map.104 = bf16[1280,768]{1,0:T(8,128)(2,1)} custom-call(bf16[256,768]{1,0:T(8,128)(2,1)} %bitcast.33), custom_call_target="tpu_custom_call" | custom-call | tf_op jit(solution)/shard_map/pallas_call | solution.py:320
  29.9 4.7 %convolution_convert_fusion.vc_ref = bf16[1280,768]{1,0:T(8,128)(2,1)} fusion(bf16[1280,768]{1,0:T(8,128)(2,1)} %shard_map.104, bf16[768,768]{1,0:T(8,128)(2,1)S(1)} %copy-done.3), kind=kOutput, calls=%fused_computation.3 | convolution fusion | flops 1510932480 | bytes 5111808 | tf_op jit(solution)/shard_map/dot_general | solution.py:360
  34.6 3.0 %convolution_convert_fusion.1.kc_ref = bf16[1280,768]{1,0:T(8,128)(2,1)} fusion(bf16[1280,768]{1,0:T(8,128)(2,1)S(1)} %copy-done.2, bf16[768,768]{1,0:T(8,128)(2,1)S(1)} %copy-done), kind=kOutput, calls=%fused_computation.4 | convolution fusion | flops 1510932480 | bytes 5111808 | tf_op jit(solution)/shard_map/dot_general | solution.py:359
  37.6 26.2 %shard_map.105 = (bf16[256,768]{1,0:T(8,128)(2,1)}, f32[1280,768]{1,0:T(8,128)}, f32[1280,768]{1,0:T(8,128)}) custom-call(s32[1]{0:T(128)} %bitcast.place_ref, bf16[256,768]{1,0:T(8,128)(2,1)} %convolution_convert_fusion.4.q_ref, bf16[1280,768]{1,0:T(8,128)(2,1)} %convolution_convert_fusion.1.kc_ref, bf16[1280,768]{1,0:T(8,128)(2,1)} %convolution_convert_fusion.vc_ref, ...), custom_call_target="tpu_custom_call" | custom-call | flops 5637144576 | bytes 13369344 | tf_op jit(solution)/shard_map/pallas_call | solution.py:176
  63.9 5.2 %fusion = f32[1280,768]{1,0:T(8,128)S(1)} fusion(bf16[768,768]{1,0:T(8,128)(2,1)S(1)} %copy-done, f32[1280,768]{1,0:T(8,128)} %get-tuple-element.6), kind=kOutput, calls=%fused_computation.5 | convolution fusion | flops 1513881600 | bytes 9043968 | tf_op jit(solution)/shard_map/dot_general | solution.py:339
  69.1 0.0 copy-done.7
  69.1 0.0 copy-start.1
  69.1 1.8 %fusion.5 = f32[1280,768]{1,0:T(8,128)S(1)} fusion(bf16[768,768]{1,0:T(8,128)(2,1)S(1)} %copy-done, f32[1280,768]{1,0:T(8,128)S(1)} %copy-done.7), kind=kOutput, calls=%fused_computation.13 | convolution fusion | flops 1510932480 | bytes 9043968 | tf_op jit(solution)/shard_map/dot_general | solution.py:338
  70.9 0.3 copy-done.1
  71.2 1.8 %fusion.2 = f32[1280,768]{1,0:T(8,128)S(1)} fusion(bf16[768,768]{1,0:T(8,128)(2,1)S(1)} %copy-done.3, f32[1280,768]{1,0:T(8,128)S(1)} %copy-done.1), kind=kOutput, calls=%fused_computation.10 | convolution fusion | flops 1510932480 | bytes 9043968 | tf_op jit(solution)/shard_map/dot_general | solution.py:338
  73.0 3.9 %add_add_fusion.terms_ref = f32[1280,768]{1,0:T(8,128)} fusion(f32[1280,768]{1,0:T(8,128)S(1)} %fusion.2, f32[1280,768]{1,0:T(8,128)S(1)} %fusion.5, f32[1280,768]{1,0:T(8,128)S(1)} %fusion, bf16[768,768]{1,0:T(8,128)(2,1)S(1)} %copy-done.3, f32[1280,768]{1,0:T(8,128)S(1)} %copy-done.1), kind=kOutput, calls=%fused_computation | convolution fusion | flops 1516830720 | bytes 20840448 | tf_op jit(solution)/shard_map/dot_general | solution.py:339
  76.9 29.6 %shard_map.106 = f32[256,768]{1,0:T(8,128)} custom-call(f32[1280,768]{1,0:T(8,128)} %add_add_fusion.terms_ref), custom_call_target="tpu_custom_call" | custom-call | tf_op jit(solution)/shard_map/pallas_call | solution.py:261
  106.6 2.0 %multiply_reduce_fusion = f32[]{:T(128)} fusion(f32[256,768]{1,0:T(8,128)} %shard_map.106), kind=kLoop, calls=%fused_computation.18 | loop fusion | flops 393215 | bytes 786436 | tf_op jit(solution)/shard_map/reduce_sum | solution.py:374
  108.6 1.3 broadcast_in_dim.32.part_ref
  109.9 30.4 %shard_map.107 = f32[8,128]{1,0:T(8,128)} custom-call(f32[8,128]{1,0:T(8,128)} %broadcast_in_dim.32.part_ref), custom_call_target="tpu_custom_call" | custom-call | tf_op jit(solution)/shard_map/pallas_call | solution.py:90
  140.3 1.2 slice.11
  142.2 2.1 %multiply_bitcast_fusion = f32[1,256,768]{2,1,0:T(8,128)} fusion(f32[256,768]{1,0:T(8,128)} %shard_map.106, f32[]{:T(128)} %bitcast.8), kind=kLoop, calls=%fused_computation.17 | loop fusion | flops 196608 | bytes 1572868 | tf_op jit(solution)/shard_map/broadcast_in_dim | solution.py:379
  (8 shorter events, 0.0 us)
Async XLA Ops:
  0.6 5.1 %copy-start = (bf16[768,768]{1,0:T(8,128)(2,1)S(1)}, bf16[768,768]{1,0:T(8,128)(2,1)}, u32[]{:S(2)}) copy-start(bf16[768,768]{1,0:T(8,128)(2,1)} %param.15) | copy-start | bytes 3538948
  0.6 7.5 %copy-start.3 = (bf16[768,768]{1,0:T(8,128)(2,1)S(1)}, bf16[768,768]{1,0:T(8,128)(2,1)}, u32[]{:S(2)}) copy-start(bf16[768,768]{1,0:T(8,128)(2,1)} %param.16) | copy-start | bytes 3538948
  0.7 7.5 %copy-start.4 = (bf16[1,256,768]{2,1,0:T(8,128)(2,1)S(1)}, bf16[1,256,768]{2,1,0:T(8,128)(2,1)}, u32[]{:S(2)}) copy-start(bf16[1,256,768]{2,1,0:T(8,128)(2,1)} %param.9) | copy-start | bytes 1179652
  0.7 7.5 %copy-start.6 = (bf16[768]{0:T(1024)(128)(2,1)S(1)}, bf16[768]{0:T(1024)(128)(2,1)}, u32[]{:S(2)}) copy-start(bf16[768]{0:T(1024)(128)(2,1)} %param.17) | copy-start | bytes 4612
  5.7 3.7 %copy-start.5 = (bf16[768,768]{1,0:T(8,128)(2,1)S(1)}, bf16[768,768]{1,0:T(8,128)(2,1)}, u32[]{:S(2)}) copy-start(bf16[768,768]{1,0:T(8,128)(2,1)} %param.14) | copy-start | bytes 3538948
  29.9 4.8 %copy-start.2 = (bf16[1280,768]{1,0:T(8,128)(2,1)S(1)}, bf16[1280,768]{1,0:T(8,128)(2,1)}, u32[]{:S(2)}) copy-start(bf16[1280,768]{1,0:T(8,128)(2,1)} %shard_map.104) | copy-start | bytes 5898244
  63.9 5.3 %copy-start.7 = (f32[1280,768]{1,0:T(8,128)S(1)}, f32[1280,768]{1,0:T(8,128)}, u32[]{:S(2)}) copy-start(f32[1280,768]{1,0:T(8,128)} %get-tuple-element.6) | copy-start | bytes 11796484
  69.1 2.1 %copy-start.1 = (f32[1280,768]{1,0:T(8,128)S(1)}, f32[1280,768]{1,0:T(8,128)}, u32[]{:S(2)}) copy-start(f32[1280,768]{1,0:T(8,128)} %get-tuple-element.7) | copy-start | bytes 11796484

commit v6 on v5

--- a/solution.py
+++ b/solution.py
@@ -273,7 +273,8 @@
     )(terms)
 
 
-def gather_front_kernel(axes, span, chunks, own_ref, window_ref, got, send_sems, recv_sems):
+def gather_front_kernel(axes, span, chunks, own_ref, noisy_ref, wq_ref, wk_ref, wv_ref,
+                        kc_ref, vc_ref, q_ref, kn_ref, vn_ref, got, send_sems, recv_sems):
     me, left, right, has_left, has_right = chain_ends(axes)
     chain_barrier(axes, left, right, has_left, has_right)
     rows = own_ref.shape[0]
@@ -294,19 +295,35 @@
             device_id=device_of(axes, "seq", right), device_id_type=pl.DeviceIdType.MESH,
         )
 
-    for step in range(span + 1):
+    def project_rows(rows_in, weight_ref):
+        return jnp.dot(rows_in, weight_ref[...], preferred_element_type=jnp.float32).astype(
+            jnp.bfloat16
+        )
+
+    for chunk in range(chunks):
+        @pl.when(has_right)
+        def _():
+            copy(0, chunk).start()
+    noisy = noisy_ref[...]
+    q_ref[...] = project_rows(noisy, wq_ref)
+    kn_ref[...] = project_rows(noisy, wk_ref)
+    vn_ref[...] = project_rows(noisy, wv_ref)
+    own = own_ref[...]
+    kc_ref[pl.ds(span * rows, rows), :] = project_rows(own, wk_ref)
+    vc_ref[pl.ds(span * rows, rows), :] = project_rows(own, wv_ref)
+    for step in range(1, span + 1):
         for chunk in range(chunks):
-            if step > 0:
-                @pl.when(step <= me)
-                def _():
-                    copy(step - 1, chunk).wait_recv()
+            @pl.when(step <= me)
+            def _():
+                copy(step - 1, chunk).wait_recv()
             if step < span:
                 @pl.when(has_right & (step <= me))
                 def _():
                     copy(step, chunk).start()
-    for step in range(span):
-        window_ref[pl.ds((span - 1 - step) * rows, rows), :] = got[step].reshape(rows, -1)
-    window_ref[pl.ds(span * rows, rows), :] = own_ref[...]
+            arrived = got[step - 1, chunk]
+            start = (span - step) * rows + chunk * piece
+            kc_ref[pl.ds(start, piece), :] = project_rows(arrived, wk_ref)
+            vc_ref[pl.ds(start, piece), :] = project_rows(arrived, wv_ref)
     for step in range(span):
         for chunk in range(chunks):
             @pl.when(has_right & (step <= me))
@@ -314,22 +331,29 @@
                 copy(step, chunk).wait_send()
 
 
-def gather_front(own, span, axes, chunks=4):
+def gather_front(own, noisy, w_query, w_key, w_value, span, axes, chunks=4):
     rows, width = own.shape
     piece = rows // chunks
+    vmem = pl.BlockSpec(memory_space=pltpu.VMEM)
+    context = jax.ShapeDtypeStruct(((span + 1) * rows, width), jnp.bfloat16)
+    local = jax.ShapeDtypeStruct((rows, width), jnp.bfloat16)
+    flops = 2 * width * width * rows * (2 * (span + 1) + 3)
     return pl.pallas_call(
         functools.partial(gather_front_kernel, axes, span, chunks),
-        out_shape=jax.ShapeDtypeStruct(((span + 1) * rows, width), own.dtype),
-        in_specs=[pl.BlockSpec(memory_space=pltpu.VMEM)],
-        out_specs=pl.BlockSpec(memory_space=pltpu.VMEM),
+        out_shape=(context, context, local, local, local),
+        in_specs=[vmem] * 5,
+        out_specs=[vmem] * 5,
         scratch_shapes=[
             pltpu.VMEM((span, chunks, piece, width), own.dtype),
             pltpu.SemaphoreType.DMA((span, chunks)),
             pltpu.SemaphoreType.DMA((span, chunks)),
         ],
+        cost_estimate=pl.CostEstimate(
+            flops=flops, transcendentals=0,
+            bytes_accessed=2 * width * (3 * width + (2 * span + 7) * rows),
+        ),
         compiler_params=pltpu.CompilerParams(collective_id=2, has_side_effects=True),
-    )(own)
-
+    )(own, noisy, w_query, w_key, w_value)
 
 def project(rows, weight):
     high = rows.astype(jnp.bfloat16)
@@ -352,13 +376,8 @@
     bits = block_bits.reshape(tok_count)
     masked = bits == 1
     noisy = jnp.where(masked[:, None], mask_embed[None, :], clean_rows)
-    query = jnp.dot(noisy, w_query, preferred_element_type=jnp.float32).astype(jnp.bfloat16)
-    key_noisy = jnp.dot(noisy, w_key, preferred_element_type=jnp.float32).astype(jnp.bfloat16)
-    value_noisy = jnp.dot(noisy, w_value, preferred_element_type=jnp.float32).astype(jnp.bfloat16)
-    window_rows = gather_front(clean_rows, span, ("dp", "seq"))
-    key_clean = jnp.dot(window_rows, w_key, preferred_element_type=jnp.float32).astype(jnp.bfloat16)
-    value_clean = jnp.dot(window_rows, w_value, preferred_element_type=jnp.float32).astype(
-        jnp.bfloat16
+    key_clean, value_clean, query, key_noisy, value_noisy = gather_front(
+        clean_rows, noisy, w_query, w_key, w_value, span, ("dp", "seq")
     )
     level_f = levels[0].astype(jnp.float32)
     ratio_f = importance[0].astype(jnp.float32)

time: 145 us -> 137 us (0.945)
  matrix products: 25.4 us -> 12.7 us
  Pallas kernels: 105 us -> 108 us
  other arithmetic: 8.94 us -> 10.6 us
    dot_general x5 -> x0, matrix products: 12.7 us -> none  [the longest x1 4.75 us: on_device(): jnp.dot(window_rows, w_value, preferred_element_type=jnp.float32)]
    pallas_call x1, Pallas kernels: 19.2 us -> 22.9 us  [gather_front(): pl.pallas_call(functools.partial(gather_front_kernel, axes, span, chunks)...]
    select_n x0 -> x1, other arithmetic: none -> 1.86 us  [on_device(): noisy = jnp.where(masked[:, None], mask_embed[None, :], clean_rows)]
    pallas_call x1, Pallas kernels: 29.6 us -> 28 us  [sum_back(): pl.pallas_call(functools.partial(sum_back_kernel, axes, span, chunks), ou...]
where the time goes in v6:
time: 137 us; the launch traced here: 136 us
  Pallas kernels  108 us (79%)
  matrix products  12.7 us (9%)
  other arithmetic  10.6 us (8%)
  local copies, waits for them, and re-layouts  3.22 us (2%)
  between operations  1.43 us (1%)
    pallas_call x1, Pallas kernels, global_total(): pl.pallas_call(functools.partial(total_kernel, axes, stages), out_shape=j...  30.9 us
    pallas_call x1, Pallas kernels, sum_back(): pl.pallas_call(functools.partial(sum_back_kernel, axes, span, chunks), ou...  28 us
    pallas_call x1, Pallas kernels, attention_heads(): pl.pallas_call(attention_kernel, out_shape=(jax.ShapeDtypeStruct((rows, w...  26.5 us
    pallas_call x1, Pallas kernels, gather_front(): pl.pallas_call(functools.partial(gather_front_kernel, axes, span, chunks)...  22.9 us
    dot_general x2, matrix products, project(): lax.dot_general(low, weight, contract, preferred_element_type=jnp.float32)  9.16 us
    dot_general x2, matrix products, project(): lax.dot_general(high, weight, contract, preferred_element_type=jnp.float32)  3.52 us

profile of v6, /device:TPU:1, one launch (start us, length us, event | category | flops | bytes accessed | tf_op | source)
XLA Modules:
  0.0 136.3 jit_solution(16776522840334742723)
XLA Ops:
  0.6 0.7 convert_bitcast_fusion
  1.3 0.7 fusion.9
  2.0 0.7 fusion.8
  2.7 0.1 eq.12
  2.8 0.7 convert_multiply_fusion.1
  3.5 0.1 mul.46
  3.6 1.9 %fusion.7.g_ref = bf16[256,768]{1,0:T(8,128)(2,1)} fusion(bf16[1,256,768]{2,1,0:T(8,128)(2,1)} %param.10, f32[256]{0:T(256)S(1)} %mul.46), kind=kLoop, calls=%fused_computation.11 | loop fusion | flops 589824 | bytes 787456 | tf_op jit(solution)/shard_map/convert_element_type | solution.py:386
  5.5 1.9 %broadcast_select_fusion.noisy_ref = bf16[256,768]{1,0:T(8,128)(2,1)} fusion(pred[256]{0:T(512)(128)(4,1)S(1)} %eq.12, bf16[768]{0:T(1024)(128)(2,1)} %param.17, bf16[1,256,768]{2,1,0:T(8,128)(2,1)} %param.9), kind=kLoop, calls=%fused_computation.14 | loop fusion | flops 196608 | bytes 788224 | tf_op jit(solution)/shard_map/jit(_where)/select_n | solution.py:378
  7.4 22.9 %shard_map.104 = (bf16[1280,768]{1,0:T(8,128)(2,1)}, bf16[1280,768]{1,0:T(8,128)(2,1)}, bf16[256,768]{1,0:T(8,128)(2,1)}, bf16[256,768]{1,0:T(8,128)(2,1)}, bf16[256,768]{1,0:T(8,128)(2,1)}) custom-call(bf16[256,768]{1,0:T(8,128)(2,1)} %bitcast.23, bf16[256,768]{1,0:T(8,128)(2,1)} %broadcast_select_fusion.noisy_ref, bf16[768,768]{1,0:T(8,128)(2,1)} %wq_ref.1, ...), custom_call_target="tpu_custom_call" | custom-call | flops 3925868544 | bytes 9437184 | tf_op jit(solution)/shard_map/pallas_call | solution.py:341
  30.3 0.0 copy-start.2
  30.3 26.5 %shard_map.105 = (bf16[256,768]{1,0:T(8,128)(2,1)}, f32[1280,768]{1,0:T(8,128)}, f32[1280,768]{1,0:T(8,128)}) custom-call(s32[1]{0:T(128)} %bitcast.place_ref, bf16[256,768]{1,0:T(8,128)(2,1)} %get-tuple-element.10.q_ref, bf16[1280,768]{1,0:T(8,128)(2,1)} %get-tuple-element.11.kc_ref, bf16[1280,768]{1,0:T(8,128)(2,1)} %get-tuple-element.12.vc_ref, ...), custom_call_target="tpu_custom_call" | custom-call | flops 5637144576 | bytes 13369344 | tf_op jit(solution)/shard_map/pallas_call | solution.py:176
  56.9 0.0 copy-done.2
  56.9 0.0 copy-start.3
  56.9 5.2 %fusion = f32[1280,768]{1,0:T(8,128)S(1)} fusion(bf16[768,768]{1,0:T(8,128)(2,1)S(1)} %copy-done.2, f32[1280,768]{1,0:T(8,128)} %get-tuple-element.16), kind=kOutput, calls=%fused_computation.3 | convolution fusion | flops 1513881600 | bytes 9043968 | tf_op jit(solution)/shard_map/dot_general | solution.py:363
  62.1 0.0 copy-done.3
  62.1 0.0 copy-start
  62.1 0.0 copy-start.1
  62.2 1.8 %fusion.5 = f32[1280,768]{1,0:T(8,128)S(1)} fusion(bf16[768,768]{1,0:T(8,128)(2,1)S(1)} %copy-done.2, f32[1280,768]{1,0:T(8,128)S(1)} %copy-done.3), kind=kOutput, calls=%fused_computation.8 | convolution fusion | flops 1510932480 | bytes 9043968 | tf_op jit(solution)/shard_map/dot_general | solution.py:362
  63.9 0.3 copy-done
  64.2 0.3 copy-done.1
  64.6 1.8 %fusion.2 = f32[1280,768]{1,0:T(8,128)S(1)} fusion(bf16[768,768]{1,0:T(8,128)(2,1)S(1)} %copy-done.1, f32[1280,768]{1,0:T(8,128)S(1)} %copy-done), kind=kOutput, calls=%fused_computation.5 | convolution fusion | flops 1510932480 | bytes 9043968 | tf_op jit(solution)/shard_map/dot_general | solution.py:362
  66.3 3.9 %add_add_fusion.terms_ref = f32[1280,768]{1,0:T(8,128)} fusion(f32[1280,768]{1,0:T(8,128)S(1)} %fusion.2, f32[1280,768]{1,0:T(8,128)S(1)} %fusion.5, f32[1280,768]{1,0:T(8,128)S(1)} %fusion, bf16[768,768]{1,0:T(8,128)(2,1)S(1)} %copy-done.1, f32[1280,768]{1,0:T(8,128)S(1)} %copy-done), kind=kOutput, calls=%fused_computation | convolution fusion | flops 1516830720 | bytes 20840448 | tf_op jit(solution)/shard_map/dot_general | solution.py:363
  70.3 28.0 %shard_map.106 = f32[256,768]{1,0:T(8,128)} custom-call(f32[1280,768]{1,0:T(8,128)} %add_add_fusion.terms_ref), custom_call_target="tpu_custom_call" | custom-call | tf_op jit(solution)/shard_map/pallas_call | solution.py:261
  98.3 2.0 %multiply_reduce_fusion = f32[]{:T(128)} fusion(f32[256,768]{1,0:T(8,128)} %shard_map.106), kind=kLoop, calls=%fused_computation.13 | loop fusion | flops 393215 | bytes 786436 | tf_op jit(solution)/shard_map/reduce_sum | solution.py:393
  100.3 1.2 broadcast_in_dim.32.part_ref
  101.5 30.9 %shard_map.107 = f32[8,128]{1,0:T(8,128)} custom-call(f32[8,128]{1,0:T(8,128)} %broadcast_in_dim.32.part_ref), custom_call_target="tpu_custom_call" | custom-call | tf_op jit(solution)/shard_map/pallas_call | solution.py:90
  132.3 1.2 slice.11
  134.2 2.1 %multiply_bitcast_fusion = f32[1,256,768]{2,1,0:T(8,128)} fusion(f32[256,768]{1,0:T(8,128)} %shard_map.106, f32[]{:T(128)} %bitcast.8), kind=kLoop, calls=%fused_computation.12 | loop fusion | flops 196608 | bytes 1572868 | tf_op jit(solution)/shard_map/broadcast_in_dim | solution.py:398
Async XLA Ops:
  30.3 26.6 %copy-start.2 = (bf16[768,768]{1,0:T(8,128)(2,1)S(1)}, bf16[768,768]{1,0:T(8,128)(2,1)}, u32[]{:S(2)}) copy-start(bf16[768,768]{1,0:T(8,128)(2,1)} %wk_ref.1) | copy-start | bytes 3538948
  56.9 5.3 %copy-start.3 = (f32[1280,768]{1,0:T(8,128)S(1)}, f32[1280,768]{1,0:T(8,128)}, u32[]{:S(2)}) copy-start(f32[1280,768]{1,0:T(8,128)} %get-tuple-element.16) | copy-start | bytes 11796484
  62.1 2.1 %copy-start = (f32[1280,768]{1,0:T(8,128)S(1)}, f32[1280,768]{1,0:T(8,128)}, u32[]{:S(2)}) copy-start(f32[1280,768]{1,0:T(8,128)} %get-tuple-element.17) | copy-start | bytes 11796484
  62.1 2.4 %copy-start.1 = (bf16[768,768]{1,0:T(8,128)(2,1)S(1)}, bf16[768,768]{1,0:T(8,128)(2,1)}, u32[]{:S(2)}) copy-start(bf16[768,768]{1,0:T(8,128)(2,1)} %wv_ref.1) | copy-start | bytes 3538948

commit v7 on v6

--- a/solution.py
+++ b/solution.py
@@ -214,7 +214,8 @@
     return me, left, right, me > 0, me < size - 1
 
 
-def sum_back_kernel(axes, span, chunks, terms_ref, raw_ref, sent, got, send_sems, recv_sems):
+def sum_back_kernel(axes, span, chunks, dk_ref, dv_ref, wk_ref, wv_ref, raw_ref, sent, got,
+                    send_sems, recv_sems):
     me, left, right, has_left, has_right = chain_ends(axes)
     chain_barrier(axes, left, right, has_left, has_right)
     rows = raw_ref.shape[0]
@@ -233,7 +234,8 @@
 
     for step in range(span + 1):
         for chunk in range(chunks):
-            value = terms_ref[pl.ds(step * rows + chunk * piece, piece), :]
+            at = pl.ds(step * rows + chunk * piece, piece)
+            value = project(dk_ref[at, :], wk_ref[...]) + project(dv_ref[at, :], wv_ref[...])
             if step > 0:
                 @pl.when(has_right)
                 def _():
@@ -255,22 +257,27 @@
                 copy(step, chunk).wait_send()
 
 
-def sum_back(terms, span, rows, axes, chunks=4):
-    width = terms.shape[1]
+def sum_back(dk, dv, w_key, w_value, span, rows, axes, chunks=4):
+    width = dk.shape[1]
     piece = rows // chunks
+    vmem = pl.BlockSpec(memory_space=pltpu.VMEM)
     return pl.pallas_call(
         functools.partial(sum_back_kernel, axes, span, chunks),
         out_shape=jax.ShapeDtypeStruct((rows, width), jnp.float32),
-        in_specs=[pl.BlockSpec(memory_space=pltpu.VMEM)],
-        out_specs=pl.BlockSpec(memory_space=pltpu.VMEM),
+        in_specs=[vmem] * 4,
+        out_specs=vmem,
         scratch_shapes=[
             pltpu.VMEM((span, chunks, piece, width), jnp.bfloat16),
             pltpu.VMEM((span, chunks, piece, width), jnp.bfloat16),
             pltpu.SemaphoreType.DMA((span, chunks)),
             pltpu.SemaphoreType.DMA((span, chunks)),
         ],
+        cost_estimate=pl.CostEstimate(
+            flops=8 * width * width * rows * (span + 1), transcendentals=0,
+            bytes_accessed=4 * width * (2 * (span + 1) * rows + rows + width),
+        ),
         compiler_params=pltpu.CompilerParams(collective_id=1, has_side_effects=True),
-    )(terms)
+    )(dk, dv, w_key, w_value)
 
 
 def gather_front_kernel(axes, span, chunks, own_ref, noisy_ref, wq_ref, wk_ref, wv_ref,
@@ -388,8 +395,7 @@
     attn_rows, dkey_rows, dvalue_rows = attention_heads(
         place, query, key_clean, value_clean, key_noisy, value_noisy, grad_out
     )
-    terms = project(dkey_rows, w_key) + project(dvalue_rows, w_value)
-    raw = sum_back(terms, span, tok_count, ("dp", "seq"))
+    raw = sum_back(dkey_rows, dvalue_rows, w_key, w_value, span, tok_count, ("dp", "seq"))
     squares = jnp.sum(raw * raw)
     total_squares = global_total(squares, ("dp", "seq"))
     entries = float(tok_count * width * lax.axis_size("dp") * lax.axis_size("seq"))

time: 137 us -> 159 us (1.16)
  Pallas kernels: 108 us -> 144 us
  matrix products: 12.7 us -> 0 us
    pallas_call x1, Pallas kernels: 28 us -> 63.5 us  [sum_back(): pl.pallas_call(functools.partial(sum_back_kernel, axes, span, chunks), ou...]
    dot_general x4 -> x0, matrix products: 12.7 us -> none  [the longest x2 9.16 us: project(): lax.dot_general(low, weight, contract, preferred_element_type=jnp.float32)]
where the time goes in v7:
time: 159 us; the launch traced here: 158 us
  Pallas kernels  144 us (91%)
  other arithmetic  10.6 us (7%)
  local copies, waits for them, and re-layouts  2.65 us (2%)
    pallas_call x1, Pallas kernels, sum_back(): pl.pallas_call(functools.partial(sum_back_kernel, axes, span, chunks), ou...  63.5 us
    pallas_call x1, Pallas kernels, global_total(): pl.pallas_call(functools.partial(total_kernel, axes, stages), out_shape=j...  31 us
    pallas_call x1, Pallas kernels, attention_heads(): pl.pallas_call(attention_kernel, out_shape=(jax.ShapeDtypeStruct((rows, w...  26.3 us
    pallas_call x1, Pallas kernels, gather_front(): pl.pallas_call(functools.partial(gather_front_kernel, axes, span, chunks)...  22.9 us

profile of v7, /device:TPU:1, one launch (start us, length us, event | category | flops | bytes accessed | tf_op | source)
XLA Modules:
  0.0 158.4 jit_solution(7674001800461021989)
XLA Ops:
  0.6 0.7 convert_bitcast_fusion
  1.3 0.7 fusion.2
  2.0 0.7 fusion.1
  2.7 0.1 eq.12
  2.8 0.7 convert_multiply_fusion.1
  3.5 0.1 mul.46
  3.6 1.9 %fusion.g_ref = bf16[256,768]{1,0:T(8,128)(2,1)} fusion(bf16[1,256,768]{2,1,0:T(8,128)(2,1)} %param.10, f32[256]{0:T(256)S(1)} %mul.46), kind=kLoop, calls=%fused_computation.1 | loop fusion | flops 589824 | bytes 787456 | tf_op jit(solution)/shard_map/convert_element_type | solution.py:393
  5.5 1.9 %broadcast_select_fusion.noisy_ref = bf16[256,768]{1,0:T(8,128)(2,1)} fusion(pred[256]{0:T(512)(128)(4,1)S(1)} %eq.12, bf16[768]{0:T(1024)(128)(2,1)} %param.17, bf16[1,256,768]{2,1,0:T(8,128)(2,1)} %param.9), kind=kLoop, calls=%fused_computation.4 | loop fusion | flops 196608 | bytes 788224 | tf_op jit(solution)/shard_map/jit(_where)/select_n | solution.py:385
  7.4 22.9 %shard_map.104 = (bf16[1280,768]{1,0:T(8,128)(2,1)}, bf16[1280,768]{1,0:T(8,128)(2,1)}, bf16[256,768]{1,0:T(8,128)(2,1)}, bf16[256,768]{1,0:T(8,128)(2,1)}, bf16[256,768]{1,0:T(8,128)(2,1)}) custom-call(bf16[256,768]{1,0:T(8,128)(2,1)} %bitcast.19, bf16[256,768]{1,0:T(8,128)(2,1)} %broadcast_select_fusion.noisy_ref, bf16[768,768]{1,0:T(8,128)(2,1)} %wq_ref.1, ...), custom_call_target="tpu_custom_call" | custom-call | flops 3925868544 | bytes 9437184 | tf_op jit(solution)/shard_map/pallas_call | solution.py:348
  30.3 26.3 %shard_map.105 = (bf16[256,768]{1,0:T(8,128)(2,1)}, f32[1280,768]{1,0:T(8,128)}, f32[1280,768]{1,0:T(8,128)}) custom-call(s32[1]{0:T(128)} %bitcast.place_ref, bf16[256,768]{1,0:T(8,128)(2,1)} %get-tuple-element.10.q_ref, bf16[1280,768]{1,0:T(8,128)(2,1)} %get-tuple-element.11.kc_ref, bf16[1280,768]{1,0:T(8,128)(2,1)} %get-tuple-element.12.vc_ref, ...), custom_call_target="tpu_custom_call" | custom-call | flops 5637144576 | bytes 13369344 | tf_op jit(solution)/shard_map/pallas_call | solution.py:176
  56.6 63.5 %shard_map.106 = f32[256,768]{1,0:T(8,128)} custom-call(f32[1280,768]{1,0:T(8,128)} %get-tuple-element.16.dk_ref, f32[1280,768]{1,0:T(8,128)} %get-tuple-element.17.dv_ref, bf16[768,768]{1,0:T(8,128)(2,1)} %wk_ref.3, bf16[768,768]{1,0:T(8,128)(2,1)} %wv_ref.3), custom_call_target="tpu_custom_call" | custom-call | flops 6039797760 | bytes 11010048 | tf_op jit(solution)/shard_map/pallas_call | solution.py:264
  120.1 2.0 %multiply_reduce_fusion = f32[]{:T(128)} fusion(f32[256,768]{1,0:T(8,128)} %shard_map.106), kind=kLoop, calls=%fused_computation.3 | loop fusion | flops 393215 | bytes 786436 | tf_op jit(solution)/shard_map/reduce_sum | solution.py:399
  122.1 1.3 broadcast_in_dim.32.part_ref
  123.4 31.0 %shard_map.107 = f32[8,128]{1,0:T(8,128)} custom-call(f32[8,128]{1,0:T(8,128)} %broadcast_in_dim.32.part_ref), custom_call_target="tpu_custom_call" | custom-call | tf_op jit(solution)/shard_map/pallas_call | solution.py:90
  154.4 1.2 slice.11
  156.3 2.1 %multiply_bitcast_fusion = f32[1,256,768]{2,1,0:T(8,128)} fusion(f32[256,768]{1,0:T(8,128)} %shard_map.106, f32[]{:T(128)} %bitcast.8), kind=kLoop, calls=%fused_computation.2 | loop fusion | flops 196608 | bytes 1572868 | tf_op jit(solution)/shard_map/broadcast_in_dim | solution.py:404

commit v8 on v7

--- a/solution.py
+++ b/solution.py
@@ -214,6 +214,13 @@
     return me, left, right, me > 0, me < size - 1
 
 
+def project_plain(rows, weight_ref):
+    high = rows.astype(jnp.bfloat16)
+    low = (rows - high.astype(jnp.float32)).astype(jnp.bfloat16)
+    product = jnp.dot(high, weight_ref[...], preferred_element_type=jnp.float32)
+    return product + jnp.dot(low, weight_ref[...], preferred_element_type=jnp.float32)
+
+
 def sum_back_kernel(axes, span, chunks, dk_ref, dv_ref, wk_ref, wv_ref, raw_ref, sent, got,
                     send_sems, recv_sems):
     me, left, right, has_left, has_right = chain_ends(axes)
@@ -235,7 +242,7 @@
     for step in range(span + 1):
         for chunk in range(chunks):
             at = pl.ds(step * rows + chunk * piece, piece)
-            value = project(dk_ref[at, :], wk_ref[...]) + project(dv_ref[at, :], wv_ref[...])
+            value = project_plain(dk_ref[at, :], wk_ref) + project_plain(dv_ref[at, :], wv_ref)
             if step > 0:
                 @pl.when(has_right)
                 def _():
@@ -395,7 +402,7 @@
     attn_rows, dkey_rows, dvalue_rows = attention_heads(
         place, query, key_clean, value_clean, key_noisy, value_noisy, grad_out
     )
-    raw = sum_back(dkey_rows, dvalue_rows, w_key, w_value, span, tok_count, ("dp", "seq"))
+    raw = sum_back(dkey_rows, dvalue_rows, w_key.T, w_value.T, span, tok_count, ("dp", "seq"))
     squares = jnp.sum(raw * raw)
     total_squares = global_total(squares, ("dp", "seq"))
     entries = float(tok_count * width * lax.axis_size("dp") * lax.axis_size("seq"))

time: 159 us -> 136 us (0.86)
  Pallas kernels: 144 us -> 122 us
  other arithmetic: 10.6 us -> 6.6 us
  local copies, waits for them, and re-layouts: 2.65 us -> 5.62 us
    pallas_call x1, Pallas kernels: 63.5 us -> 41.4 us  [sum_back(): pl.pallas_call(functools.partial(sum_back_kernel, axes, span, chunks), ou...]
    unnamed x0 -> x16, local copies, waits for them, and re-layouts: none -> 2.97 us
where the time goes in v8:
time: 136 us; the launch traced here: 135 us
  Pallas kernels  122 us (90%)
  other arithmetic  6.6 us (5%)
  local copies, waits for them, and re-layouts  5.62 us (4%)
  between operations  1.43 us (1%)
    pallas_call x1, Pallas kernels, sum_back(): pl.pallas_call(functools.partial(sum_back_kernel, axes, span, chunks), ou...  41.4 us
    pallas_call x1, Pallas kernels, global_total(): pl.pallas_call(functools.partial(total_kernel, axes, stages), out_shape=j...  31 us
    pallas_call x1, Pallas kernels, attention_heads(): pl.pallas_call(attention_kernel, out_shape=(jax.ShapeDtypeStruct((rows, w...  26.3 us
    pallas_call x1, Pallas kernels, gather_front(): pl.pallas_call(functools.partial(gather_front_kernel, axes, span, chunks)...  23 us
    unnamed x16, local copies, waits for them, and re-layouts  2.97 us

profile of v8, /device:TPU:1, one launch (start us, length us, event | category | flops | bytes accessed | tf_op | source)
XLA Modules:
  0.0 135.4 jit_solution(11006121759185519078)
XLA Ops:
  0.6 0.7 fusion.1
  1.4 0.1 eq.12
  1.5 1.9 %broadcast_select_fusion.noisy_ref = bf16[256,768]{1,0:T(8,128)(2,1)} fusion(pred[256]{0:T(512)(128)(4,1)S(1)} %eq.12, bf16[768]{0:T(1024)(128)(2,1)} %param.17, bf16[1,256,768]{2,1,0:T(8,128)(2,1)} %param.9), kind=kLoop, calls=%fused_computation.4 | loop fusion | flops 196608 | bytes 788224 | tf_op jit(solution)/shard_map/jit(_where)/select_n | solution.py:392
  3.3 0.0 copy-start.5
  3.3 0.0 copy-start.6
  3.3 0.0 copy-start.4
  3.3 0.0 copy-start.3
  3.3 23.0 %shard_map.104 = (bf16[1280,768]{1,0:T(8,128)(2,1)}, bf16[1280,768]{1,0:T(8,128)(2,1)}, bf16[256,768]{1,0:T(8,128)(2,1)}, bf16[256,768]{1,0:T(8,128)(2,1)}, bf16[256,768]{1,0:T(8,128)(2,1)}) custom-call(bf16[256,768]{1,0:T(8,128)(2,1)} %bitcast.23, bf16[256,768]{1,0:T(8,128)(2,1)} %broadcast_select_fusion.noisy_ref, bf16[768,768]{1,0:T(8,128)(2,1)} %wq_ref.1, ...), custom_call_target="tpu_custom_call" | custom-call | flops 3925868544 | bytes 9437184 | tf_op jit(solution)/shard_map/pallas_call | solution.py:355
  26.4 0.0 copy-done.5
  26.4 0.0 copy-done.6
  26.4 0.0 copy-done.4
  26.4 0.1 convert_multiply_fusion.1
  26.5 0.1 mul.46
  26.6 0.0 copy-done.3
  26.6 0.9 fusion.g_ref
  27.5 0.0 copy-start.1
  27.5 26.3 %shard_map.105 = (bf16[256,768]{1,0:T(8,128)(2,1)}, f32[1280,768]{1,0:T(8,128)}, f32[1280,768]{1,0:T(8,128)}) custom-call(s32[1]{0:T(128)} %bitcast.place_ref, bf16[256,768]{1,0:T(8,128)(2,1)} %get-tuple-element.10.q_ref, bf16[1280,768]{1,0:T(8,128)(2,1)} %get-tuple-element.11.kc_ref, bf16[1280,768]{1,0:T(8,128)(2,1)} %get-tuple-element.12.vc_ref, ...), custom_call_target="tpu_custom_call" | custom-call | flops 5637144576 | bytes 13369344 | tf_op jit(solution)/shard_map/pallas_call | solution.py:176
  53.8 0.0 copy-done.1
  53.8 0.0 copy-start.2
  53.8 1.5 %copy.11 = bf16[768,768]{0,1:T(8,128)(2,1)} copy(bf16[768,768]{1,0:T(8,128)(2,1)S(1)} %copy-done.1) | data formatting | bytes 2359296 | tf_op args[6]
  55.3 0.0 copy-done.2
  55.3 1.5 %copy.12 = bf16[768,768]{0,1:T(8,128)(2,1)} copy(bf16[768,768]{1,0:T(8,128)(2,1)S(1)} %copy-done.2) | data formatting | bytes 2359296 | tf_op args[7]
  56.8 41.4 %shard_map.106 = f32[256,768]{1,0:T(8,128)} custom-call(f32[1280,768]{1,0:T(8,128)} %get-tuple-element.16.dk_ref, f32[1280,768]{1,0:T(8,128)} %get-tuple-element.17.dv_ref, bf16[768,768]{1,0:T(8,128)(2,1)} %bitcast.21, bf16[768,768]{1,0:T(8,128)(2,1)} %bitcast.22), custom_call_target="tpu_custom_call" | custom-call | flops 6039797760 | bytes 11010048 | tf_op jit(solution)/shard_map/pallas_call | solution.py:271
  98.2 0.0 copy-start
  98.2 2.1 %multiply_reduce_fusion = f32[]{:T(128)} fusion(f32[256,768]{1,0:T(8,128)} %shard_map.106), kind=kLoop, calls=%fused_computation.3 | loop fusion | flops 393215 | bytes 786436 | tf_op jit(solution)/shard_map/reduce_sum | solution.py:406
  100.3 1.3 broadcast_in_dim.32.part_ref
  101.6 31.0 %shard_map.107 = f32[8,128]{1,0:T(8,128)} custom-call(f32[8,128]{1,0:T(8,128)} %broadcast_in_dim.32.part_ref), custom_call_target="tpu_custom_call" | custom-call | tf_op jit(solution)/shard_map/pallas_call | solution.py:90
  132.6 1.2 slice.11
  134.5 0.0 copy-done
  134.5 0.9 multiply_bitcast_fusion
  (2 shorter events, 0.0 us)
Async XLA Ops:
  3.3 23.1 %copy-start.5 = (s32[1,16,2]{1,2,0:T(2,128)S(1)}, s32[1,16,2]{1,2,0:T(2,128)}, u32[]{:S(2)}) copy-start(s32[1,16,2]{1,2,0:T(2,128)} %param.13) | copy-start | bytes 388
  3.3 23.1 %copy-start.6 = (s32[1,16]{1,0:T(1,128)S(1)}, s32[1,16]{1,0:T(1,128)}, u32[]{:S(2)}) copy-start(s32[1,16]{1,0:T(1,128)} %param.12) | copy-start | bytes 196
  3.3 23.1 %copy-start.4 = (s32[1,16]{1,0:T(1,128)S(1)}, s32[1,16]{1,0:T(1,128)}, u32[]{:S(2)}) copy-start(s32[1,16]{1,0:T(1,128)} %param.11) | copy-start | bytes 196
  3.3 23.3 %copy-start.3 = (bf16[1,256,768]{2,1,0:T(8,128)(2,1)S(1)}, bf16[1,256,768]{2,1,0:T(8,128)(2,1)}, u32[]{:S(2)}) copy-start(bf16[1,256,768]{2,1,0:T(8,128)(2,1)} %param.10) | copy-start | bytes 1179652
  27.5 26.3 %copy-start.1 = (bf16[768,768]{1,0:T(8,128)(2,1)S(1)}, bf16[768,768]{1,0:T(8,128)(2,1)}, u32[]{:S(2)}) copy-start(bf16[768,768]{1,0:T(8,128)(2,1)} %wk_ref.1) | copy-start | bytes 3538948
  53.8 1.5 %copy-start.2 = (bf16[768,768]{1,0:T(8,128)(2,1)S(1)}, bf16[768,768]{1,0:T(8,128)(2,1)}, u32[]{:S(2)}) copy-start(bf16[768,768]{1,0:T(8,128)(2,1)} %wv_ref.1) | copy-start | bytes 3538948
  98.2 36.3 %copy-start = (f32[256,768]{1,0:T(8,128)S(1)}, f32[256,768]{1,0:T(8,128)}, u32[]{:S(2)}) copy-start(f32[256,768]{1,0:T(8,128)} %shard_map.106) | copy-start | bytes 2359300

commit v9 on v8

--- a/solution.py
+++ b/solution.py
@@ -46,9 +46,8 @@
     return tuple(peer if name == axis else lax.axis_index(name) for name in axes)
 
 
-def total_kernel(axes, stages, part_ref, out_ref, slots, send_sems, recv_sems):
-    barrier = pltpu.get_barrier_semaphore()
-    greeted = 0
+def greet_groups(axes, stages, barrier):
+    count = 0
     for axis, stride, size in stages:
         for offset in range(1, size):
             peer = stage_peer(axis, stride, size, offset)
@@ -56,9 +55,11 @@
                 barrier, 1, device_id=device_of(axes, axis, peer),
                 device_id_type=pl.DeviceIdType.MESH,
             )
-            greeted += 1
-    pl.semaphore_wait(barrier, greeted)
-    current = part_ref[...]
+            count += 1
+    return count
+
+
+def stage_total(axes, stages, current, slots, send_sems, recv_sems):
     for number, (axis, stride, size) in enumerate(stages):
         digit = (lax.axis_index(axis) // stride) % size
         slots[number, digit] = current
@@ -80,7 +81,13 @@
         current = slots[number, 0]
         for member in range(1, size):
             current = current + slots[number, member]
-    out_ref[...] = current
+    return current
+
+
+def total_kernel(axes, stages, part_ref, out_ref, slots, send_sems, recv_sems):
+    barrier = pltpu.get_barrier_semaphore()
+    pl.semaphore_wait(barrier, greet_groups(axes, stages, barrier))
+    out_ref[...] = stage_total(axes, stages, part_ref[...], slots, send_sems, recv_sems)
 
 
 def global_total(value, axes):
@@ -194,8 +201,9 @@
     )(place, query, key_clean, value_clean, key_noisy, value_noisy, grad)
 
 
-def chain_barrier(axes, left, right, has_left, has_right):
+def chain_barrier(axes, left, right, has_left, has_right, stages=()):
     barrier = pltpu.get_barrier_semaphore()
+    greeted = greet_groups(axes, stages, barrier)
     for peer, present in ((left, has_left), (right, has_right)):
         @pl.when(present)
         def _():
@@ -203,7 +211,7 @@
                 barrier, 1, device_id=device_of(axes, "seq", peer),
                 device_id_type=pl.DeviceIdType.MESH,
             )
-    pl.semaphore_wait(barrier, has_left.astype(jnp.int32) + has_right.astype(jnp.int32))
+    pl.semaphore_wait(barrier, has_left.astype(jnp.int32) + has_right.astype(jnp.int32) + greeted)
 
 
 def chain_ends(axes):
@@ -221,10 +229,11 @@
     return product + jnp.dot(low, weight_ref[...], preferred_element_type=jnp.float32)
 
 
-def sum_back_kernel(axes, span, chunks, dk_ref, dv_ref, wk_ref, wv_ref, raw_ref, sent, got,
-                    send_sems, recv_sems):
+def sum_back_kernel(axes, span, chunks, stages, dk_ref, dv_ref, wk_ref, wv_ref, raw_ref, total_ref,
+                    sent, got, send_sems, recv_sems, slots, total_send, total_recv):
     me, left, right, has_left, has_right = chain_ends(axes)
-    chain_barrier(axes, left, right, has_left, has_right)
+    chain_barrier(axes, left, right, has_left, has_right, stages)
+    squares = jnp.zeros((1, 1), jnp.float32)
     rows = raw_ref.shape[0]
     piece = rows // chunks
 
@@ -257,6 +266,10 @@
                     copy(step, chunk).start()
             else:
                 raw_ref[pl.ds(chunk * piece, piece), :] = value
+                squares = squares + jnp.sum(value * value, axis=(0, 1), keepdims=True)
+    total_ref[...] = stage_total(
+        axes, stages, jnp.broadcast_to(squares, total_ref.shape), slots, total_send, total_recv
+    )
     for step in range(span):
         for chunk in range(chunks):
             @pl.when(has_left)
@@ -267,17 +280,25 @@
 def sum_back(dk, dv, w_key, w_value, span, rows, axes, chunks=4):
     width = dk.shape[1]
     piece = rows // chunks
+    stages = group_stages(axes)
+    widest = max(size for _, _, size in stages)
     vmem = pl.BlockSpec(memory_space=pltpu.VMEM)
     return pl.pallas_call(
-        functools.partial(sum_back_kernel, axes, span, chunks),
-        out_shape=jax.ShapeDtypeStruct((rows, width), jnp.float32),
+        functools.partial(sum_back_kernel, axes, span, chunks, stages),
+        out_shape=(
+            jax.ShapeDtypeStruct((rows, width), jnp.float32),
+            jax.ShapeDtypeStruct((8, 128), jnp.float32),
+        ),
         in_specs=[vmem] * 4,
-        out_specs=vmem,
+        out_specs=[vmem, vmem],
         scratch_shapes=[
             pltpu.VMEM((span, chunks, piece, width), jnp.bfloat16),
             pltpu.VMEM((span, chunks, piece, width), jnp.bfloat16),
             pltpu.SemaphoreType.DMA((span, chunks)),
             pltpu.SemaphoreType.DMA((span, chunks)),
+            pltpu.VMEM((len(stages), widest, 8, 128), jnp.float32),
+            pltpu.SemaphoreType.DMA((len(stages), widest)),
+            pltpu.SemaphoreType.DMA((len(stages), widest)),
         ],
         cost_estimate=pl.CostEstimate(
             flops=8 * width * width * rows * (span + 1), transcendentals=0,
@@ -402,9 +423,8 @@
     attn_rows, dkey_rows, dvalue_rows = attention_heads(
         place, query, key_clean, value_clean, key_noisy, value_noisy, grad_out
     )
-    raw = sum_back(dkey_rows, dvalue_rows, w_key.T, w_value.T, span, tok_count, ("dp", "seq"))
-    squares = jnp.sum(raw * raw)
-    total_squares = global_total(squares, ("dp", "seq"))
+    raw, total = sum_back(dkey_rows, dvalue_rows, w_key.T, w_value.T, span, tok_count, ("dp", "seq"))
+    total_squares = total[0, 0]
     entries = float(tok_count * width * lax.axis_size("dp") * lax.axis_size("seq"))
     rms = jnp.sqrt(total_squares / entries + EPS)
     factor = jnp.minimum(1.0, CLIP / rms)

time: 136 us -> 130 us (0.956)
  Pallas kernels: 122 us -> 119 us
    pallas_call x2 -> x1, Pallas kernels: 72.4 us -> 69.3 us  [sum_back(): pl.pallas_call(functools.partial(sum_back_kernel, axes, span, chunks, sta...]
    reduce_sum x1 -> x0, other arithmetic: 2.09 us -> none  [on_device(): squares = jnp.sum(raw * raw)]
    unnamed x16 -> x14, local copies, waits for them, and re-layouts: 2.97 us -> 2.97 us
where the time goes in v9:
time: 130 us
  Pallas kernels  119 us (92%)
  other arithmetic  5.64 us (4%)
  local copies, waits for them, and re-layouts  4.33 us (3%)
  between operations  1.4 us (1%)
    pallas_call x1, Pallas kernels, sum_back(): pl.pallas_call(functools.partial(sum_back_kernel, axes, span, chunks, sta...  69.3 us
    pallas_call x1, Pallas kernels, attention_heads(): pl.pallas_call(attention_kernel, out_shape=(jax.ShapeDtypeStruct((rows, w...  26.4 us
    pallas_call x1, Pallas kernels, gather_front(): pl.pallas_call(functools.partial(gather_front_kernel, axes, span, chunks)...  23.1 us
    unnamed x14, local copies, waits for them, and re-layouts  2.97 us

profile of v9, /device:TPU:1, one launch (start us, length us, event | category | flops | bytes accessed | tf_op | source)
XLA Modules:
  0.0 130.2 jit_solution(14677531090569438379)
XLA Ops:
  0.6 0.7 fusion.1
  1.4 0.1 eq.12
  1.5 1.9 %broadcast_select_fusion.noisy_ref = bf16[256,768]{1,0:T(8,128)(2,1)} fusion(pred[256]{0:T(512)(128)(4,1)S(1)} %eq.12, bf16[768]{0:T(1024)(128)(2,1)} %param.17, bf16[1,256,768]{2,1,0:T(8,128)(2,1)} %param.9), kind=kLoop, calls=%fused_computation.3 | loop fusion | flops 196608 | bytes 788224 | tf_op jit(solution)/shard_map/jit(_where)/select_n | solution.py:413
  3.3 0.0 copy-start.4
  3.3 0.0 copy-start.5
  3.3 0.0 copy-start.3
  3.3 0.0 copy-start.2
  3.3 23.1 %shard_map.104 = (bf16[1280,768]{1,0:T(8,128)(2,1)}, bf16[1280,768]{1,0:T(8,128)(2,1)}, bf16[256,768]{1,0:T(8,128)(2,1)}, bf16[256,768]{1,0:T(8,128)(2,1)}, bf16[256,768]{1,0:T(8,128)(2,1)}) custom-call(bf16[256,768]{1,0:T(8,128)(2,1)} %bitcast.23, bf16[256,768]{1,0:T(8,128)(2,1)} %broadcast_select_fusion.noisy_ref, bf16[768,768]{1,0:T(8,128)(2,1)} %wq_ref.1, ...), custom_call_target="tpu_custom_call" | custom-call | flops 3925868544 | bytes 9437184 | tf_op jit(solution)/shard_map/pallas_call | solution.py:376
  26.4 0.0 copy-done.4
  26.4 0.0 copy-done.5
  26.5 0.0 copy-done.3
  26.5 0.1 convert_multiply_fusion.1
  26.5 0.1 mul.43
  26.6 0.0 copy-done.2
  26.6 0.9 fusion.g_ref
  27.5 0.0 copy-start
  27.5 26.4 %shard_map.105 = (bf16[256,768]{1,0:T(8,128)(2,1)}, f32[1280,768]{1,0:T(8,128)}, f32[1280,768]{1,0:T(8,128)}) custom-call(s32[1]{0:T(128)} %bitcast.place_ref, bf16[256,768]{1,0:T(8,128)(2,1)} %get-tuple-element.12.q_ref, bf16[1280,768]{1,0:T(8,128)(2,1)} %get-tuple-element.13.kc_ref, bf16[1280,768]{1,0:T(8,128)(2,1)} %get-tuple-element.14.vc_ref, ...), custom_call_target="tpu_custom_call" | custom-call | flops 5637144576 | bytes 13369344 | tf_op jit(solution)/shard_map/pallas_call | solution.py:183
  53.9 0.0 copy-done
  53.9 0.0 copy-start.1
  53.9 1.5 %copy.11 = bf16[768,768]{0,1:T(8,128)(2,1)} copy(bf16[768,768]{1,0:T(8,128)(2,1)S(1)} %copy-done) | data formatting | bytes 2359296 | tf_op args[6]
  55.4 0.0 copy-done.1
  55.4 1.4 %copy.12 = bf16[768,768]{0,1:T(8,128)(2,1)} copy(bf16[768,768]{1,0:T(8,128)(2,1)S(1)} %copy-done.1) | data formatting | bytes 2359296 | tf_op args[7]
  56.9 69.3 %shard_map.106 = (f32[256,768]{1,0:T(8,128)}, f32[8,128]{1,0:T(8,128)}) custom-call(f32[1280,768]{1,0:T(8,128)} %get-tuple-element.18.dk_ref, f32[1280,768]{1,0:T(8,128)} %get-tuple-element.19.dv_ref, bf16[768,768]{1,0:T(8,128)(2,1)} %bitcast.21, bf16[768,768]{1,0:T(8,128)(2,1)} %bitcast.22), custom_call_target="tpu_custom_call" | custom-call | flops 6039797760 | bytes 11010048 | tf_op jit(solution)/shard_map/pallas_call | solution.py:286
  126.2 1.2 slice.11
  128.1 2.1 %multiply_bitcast_fusion = f32[1,256,768]{2,1,0:T(8,128)} fusion(f32[256,768]{1,0:T(8,128)} %get-tuple-element.20, f32[]{:T(128)} %bitcast.10), kind=kLoop, calls=%fused_computation.2 | loop fusion | flops 196608 | bytes 1572868 | tf_op jit(solution)/shard_map/broadcast_in_dim | solution.py:431
  (2 shorter events, 0.0 us)
Async XLA Ops:
  3.3 23.1 %copy-start.4 = (s32[1,16,2]{1,2,0:T(2,128)S(1)}, s32[1,16,2]{1,2,0:T(2,128)}, u32[]{:S(2)}) copy-start(s32[1,16,2]{1,2,0:T(2,128)} %param.13) | copy-start | bytes 388
  3.3 23.1 %copy-start.5 = (s32[1,16]{1,0:T(1,128)S(1)}, s32[1,16]{1,0:T(1,128)}, u32[]{:S(2)}) copy-start(s32[1,16]{1,0:T(1,128)} %param.12) | copy-start | bytes 196
  3.3 23.1 %copy-start.3 = (s32[1,16]{1,0:T(1,128)S(1)}, s32[1,16]{1,0:T(1,128)}, u32[]{:S(2)}) copy-start(s32[1,16]{1,0:T(1,128)} %param.11) | copy-start | bytes 196
  3.3 23.3 %copy-start.2 = (bf16[1,256,768]{2,1,0:T(8,128)(2,1)S(1)}, bf16[1,256,768]{2,1,0:T(8,128)(2,1)}, u32[]{:S(2)}) copy-start(bf16[1,256,768]{2,1,0:T(8,128)(2,1)} %param.10) | copy-start | bytes 1179652
  27.5 26.4 %copy-start = (bf16[768,768]{1,0:T(8,128)(2,1)S(1)}, bf16[768,768]{1,0:T(8,128)(2,1)}, u32[]{:S(2)}) copy-start(bf16[768,768]{1,0:T(8,128)(2,1)} %wk_ref.1) | copy-start | bytes 3538948
  53.9 1.5 %copy-start.1 = (bf16[768,768]{1,0:T(8,128)(2,1)S(1)}, bf16[768,768]{1,0:T(8,128)(2,1)}, u32[]{:S(2)}) copy-start(bf16[768,768]{1,0:T(8,128)(2,1)} %wv_ref.1) | copy-start | bytes 3538948

commit v10 on v9

--- a/solution.py
+++ b/solution.py
@@ -249,9 +249,10 @@
         )
 
     for step in range(span + 1):
+        at = pl.ds(step * rows, rows)
+        term = project_plain(dk_ref[at, :], wk_ref) + project_plain(dv_ref[at, :], wv_ref)
         for chunk in range(chunks):
-            at = pl.ds(step * rows + chunk * piece, piece)
-            value = project_plain(dk_ref[at, :], wk_ref) + project_plain(dv_ref[at, :], wv_ref)
+            value = term[chunk * piece:(chunk + 1) * piece]
             if step > 0:
                 @pl.when(has_right)
                 def _():
@@ -355,10 +356,9 @@
                 @pl.when(has_right & (step <= me))
                 def _():
                     copy(step, chunk).start()
-            arrived = got[step - 1, chunk]
-            start = (span - step) * rows + chunk * piece
-            kc_ref[pl.ds(start, piece), :] = project_rows(arrived, wk_ref)
-            vc_ref[pl.ds(start, piece), :] = project_rows(arrived, wv_ref)
+        arrived = got[step - 1].reshape(rows, -1)
+        kc_ref[pl.ds((span - step) * rows, rows), :] = project_rows(arrived, wk_ref)
+        vc_ref[pl.ds((span - step) * rows, rows), :] = project_rows(arrived, wv_ref)
     for step in range(span):
         for chunk in range(chunks):
             @pl.when(has_right & (step <= me))

time: 130 us -> 121 us (0.931)
  Pallas kernels: 119 us -> 109 us
    pallas_call x1, Pallas kernels: 69.3 us -> 61.5 us  [sum_back(): pl.pallas_call(functools.partial(sum_back_kernel, axes, span, chunks, sta...]
    pallas_call x1, Pallas kernels: 23.1 us -> 21.5 us  [gather_front(): pl.pallas_call(functools.partial(gather_front_kernel, axes, span, chunks)...]
where the time goes in v10:
time: 121 us
  Pallas kernels  109 us (90%)
  other arithmetic  5.64 us (5%)
  local copies, waits for them, and re-layouts  4.33 us (4%)
  between operations  1.4 us (1%)
    pallas_call x1, Pallas kernels, sum_back(): pl.pallas_call(functools.partial(sum_back_kernel, axes, span, chunks, sta...  61.5 us
    pallas_call x1, Pallas kernels, attention_heads(): pl.pallas_call(attention_kernel, out_shape=(jax.ShapeDtypeStruct((rows, w...  26.4 us
    pallas_call x1, Pallas kernels, gather_front(): pl.pallas_call(functools.partial(gather_front_kernel, axes, span, chunks)...  21.5 us
    unnamed x14, local copies, waits for them, and re-layouts  2.97 us

profile of v10, /device:TPU:1, one launch (start us, length us, event | category | flops | bytes accessed | tf_op | source)
XLA Modules:
  0.0 120.8 jit_solution(11783368725877931800)
XLA Ops:
  0.6 0.7 fusion.1
  1.4 0.1 eq.12
  1.5 1.9 %broadcast_select_fusion.noisy_ref = bf16[256,768]{1,0:T(8,128)(2,1)} fusion(pred[256]{0:T(512)(128)(4,1)S(1)} %eq.12, bf16[768]{0:T(1024)(128)(2,1)} %param.17, bf16[1,256,768]{2,1,0:T(8,128)(2,1)} %param.9), kind=kLoop, calls=%fused_computation.3 | loop fusion | flops 196608 | bytes 788224 | tf_op jit(solution)/shard_map/jit(_where)/select_n | solution.py:413
  3.3 0.0 copy-start.4
  3.3 0.0 copy-start.5
  3.3 0.0 copy-start.3
  3.3 0.0 copy-start.2
  3.3 21.5 %shard_map.104 = (bf16[1280,768]{1,0:T(8,128)(2,1)}, bf16[1280,768]{1,0:T(8,128)(2,1)}, bf16[256,768]{1,0:T(8,128)(2,1)}, bf16[256,768]{1,0:T(8,128)(2,1)}, bf16[256,768]{1,0:T(8,128)(2,1)}) custom-call(bf16[256,768]{1,0:T(8,128)(2,1)} %bitcast.23, bf16[256,768]{1,0:T(8,128)(2,1)} %broadcast_select_fusion.noisy_ref, bf16[768,768]{1,0:T(8,128)(2,1)} %wq_ref.1, ...), custom_call_target="tpu_custom_call" | custom-call | flops 3925868544 | bytes 9437184 | tf_op jit(solution)/shard_map/pallas_call | solution.py:376
  24.8 0.0 copy-done.4
  24.9 0.0 copy-done.5
  24.9 0.0 copy-done.3
  24.9 0.1 convert_multiply_fusion.1
  25.0 0.1 mul.43
  25.1 0.0 copy-done.2
  25.1 0.9 fusion.g_ref
  25.9 0.0 copy-start
  25.9 26.4 %shard_map.105 = (bf16[256,768]{1,0:T(8,128)(2,1)}, f32[1280,768]{1,0:T(8,128)}, f32[1280,768]{1,0:T(8,128)}) custom-call(s32[1]{0:T(128)} %bitcast.place_ref, bf16[256,768]{1,0:T(8,128)(2,1)} %get-tuple-element.12.q_ref, bf16[1280,768]{1,0:T(8,128)(2,1)} %get-tuple-element.13.kc_ref, bf16[1280,768]{1,0:T(8,128)(2,1)} %get-tuple-element.14.vc_ref, ...), custom_call_target="tpu_custom_call" | custom-call | flops 5637144576 | bytes 13369344 | tf_op jit(solution)/shard_map/pallas_call | solution.py:183
  52.4 0.0 copy-done
  52.4 0.0 copy-start.1
  52.4 1.5 %copy.11 = bf16[768,768]{0,1:T(8,128)(2,1)} copy(bf16[768,768]{1,0:T(8,128)(2,1)S(1)} %copy-done) | data formatting | bytes 2359296 | tf_op args[6]
  53.9 0.0 copy-done.1
  53.9 1.4 %copy.12 = bf16[768,768]{0,1:T(8,128)(2,1)} copy(bf16[768,768]{1,0:T(8,128)(2,1)S(1)} %copy-done.1) | data formatting | bytes 2359296 | tf_op args[7]
  55.3 61.5 %shard_map.106 = (f32[256,768]{1,0:T(8,128)}, f32[8,128]{1,0:T(8,128)}) custom-call(f32[1280,768]{1,0:T(8,128)} %get-tuple-element.18.dk_ref, f32[1280,768]{1,0:T(8,128)} %get-tuple-element.19.dv_ref, bf16[768,768]{1,0:T(8,128)(2,1)} %bitcast.21, bf16[768,768]{1,0:T(8,128)(2,1)} %bitcast.22), custom_call_target="tpu_custom_call" | custom-call | flops 6039797760 | bytes 11010048 | tf_op jit(solution)/shard_map/pallas_call | solution.py:287
  116.9 1.2 slice.11
  118.7 2.1 %multiply_bitcast_fusion = f32[1,256,768]{2,1,0:T(8,128)} fusion(f32[256,768]{1,0:T(8,128)} %get-tuple-element.20, f32[]{:T(128)} %bitcast.10), kind=kLoop, calls=%fused_computation.2 | loop fusion | flops 196608 | bytes 1572868 | tf_op jit(solution)/shard_map/broadcast_in_dim | solution.py:431
  (2 shorter events, 0.0 us)
Async XLA Ops:
  3.3 21.5 %copy-start.4 = (s32[1,16,2]{1,2,0:T(2,128)S(1)}, s32[1,16,2]{1,2,0:T(2,128)}, u32[]{:S(2)}) copy-start(s32[1,16,2]{1,2,0:T(2,128)} %param.13) | copy-start | bytes 388
  3.3 21.5 %copy-start.5 = (s32[1,16]{1,0:T(1,128)S(1)}, s32[1,16]{1,0:T(1,128)}, u32[]{:S(2)}) copy-start(s32[1,16]{1,0:T(1,128)} %param.12) | copy-start | bytes 196
  3.3 21.6 %copy-start.3 = (s32[1,16]{1,0:T(1,128)S(1)}, s32[1,16]{1,0:T(1,128)}, u32[]{:S(2)}) copy-start(s32[1,16]{1,0:T(1,128)} %param.11) | copy-start | bytes 196
  3.3 21.7 %copy-start.2 = (bf16[1,256,768]{2,1,0:T(8,128)(2,1)S(1)}, bf16[1,256,768]{2,1,0:T(8,128)(2,1)}, u32[]{:S(2)}) copy-start(bf16[1,256,768]{2,1,0:T(8,128)(2,1)} %param.10) | copy-start | bytes 1179652
  25.9 26.4 %copy-start = (bf16[768,768]{1,0:T(8,128)(2,1)S(1)}, bf16[768,768]{1,0:T(8,128)(2,1)}, u32[]{:S(2)}) copy-start(bf16[768,768]{1,0:T(8,128)(2,1)} %wk_ref.1) | copy-start | bytes 3538948
  52.4 1.5 %copy-start.1 = (bf16[768,768]{1,0:T(8,128)(2,1)S(1)}, bf16[768,768]{1,0:T(8,128)(2,1)}, u32[]{:S(2)}) copy-start(bf16[768,768]{1,0:T(8,128)(2,1)} %wv_ref.1) | copy-start | bytes 3538948

commit v11 on v10

--- a/solution.py
+++ b/solution.py
@@ -278,7 +278,7 @@
                 copy(step, chunk).wait_send()
 
 
-def sum_back(dk, dv, w_key, w_value, span, rows, axes, chunks=4):
+def sum_back(dk, dv, w_key, w_value, span, rows, axes, chunks=8):
     width = dk.shape[1]
     piece = rows // chunks
     stages = group_stages(axes)
@@ -366,7 +366,7 @@
                 copy(step, chunk).wait_send()
 
 
-def gather_front(own, noisy, w_query, w_key, w_value, span, axes, chunks=4):
+def gather_front(own, noisy, w_query, w_key, w_value, span, axes, chunks=8):
     rows, width = own.shape
     piece = rows // chunks
     vmem = pl.BlockSpec(memory_space=pltpu.VMEM)

time: 121 us -> 122 us (level)
  no operation moved by 1% of the time
where the time goes in v11:
time: 122 us; the launch traced here: 121 us
  Pallas kernels  110 us (90%)
  other arithmetic  5.64 us (5%)
  local copies, waits for them, and re-layouts  4.33 us (4%)
  between operations  1.4 us (1%)
    pallas_call x1, Pallas kernels, sum_back(): pl.pallas_call(functools.partial(sum_back_kernel, axes, span, chunks, sta...  61.8 us
    pallas_call x1, Pallas kernels, attention_heads(): pl.pallas_call(attention_kernel, out_shape=(jax.ShapeDtypeStruct((rows, w...  26.4 us
    pallas_call x1, Pallas kernels, gather_front(): pl.pallas_call(functools.partial(gather_front_kernel, axes, span, chunks)...  21.8 us
    unnamed x14, local copies, waits for them, and re-layouts  2.97 us

profile of v11, /device:TPU:1, one launch (start us, length us, event | category | flops | bytes accessed | tf_op | source)
XLA Modules:
  0.0 121.4 jit_solution(14784002388491590119)
XLA Ops:
  0.6 0.7 fusion.1
  1.4 0.1 eq.12
  1.5 1.9 %broadcast_select_fusion.noisy_ref = bf16[256,768]{1,0:T(8,128)(2,1)} fusion(pred[256]{0:T(512)(128)(4,1)S(1)} %eq.12, bf16[768]{0:T(1024)(128)(2,1)} %param.17, bf16[1,256,768]{2,1,0:T(8,128)(2,1)} %param.9), kind=kLoop, calls=%fused_computation.3 | loop fusion | flops 196608 | bytes 788224 | tf_op jit(solution)/shard_map/jit(_where)/select_n | solution.py:413
  3.3 0.0 copy-start.4
  3.3 0.0 copy-start.5
  3.3 0.0 copy-start.3
  3.3 0.0 copy-start.2
  3.3 21.8 %shard_map.104 = (bf16[1280,768]{1,0:T(8,128)(2,1)}, bf16[1280,768]{1,0:T(8,128)(2,1)}, bf16[256,768]{1,0:T(8,128)(2,1)}, bf16[256,768]{1,0:T(8,128)(2,1)}, bf16[256,768]{1,0:T(8,128)(2,1)}) custom-call(bf16[256,768]{1,0:T(8,128)(2,1)} %bitcast.23, bf16[256,768]{1,0:T(8,128)(2,1)} %broadcast_select_fusion.noisy_ref, bf16[768,768]{1,0:T(8,128)(2,1)} %wq_ref.1, ...), custom_call_target="tpu_custom_call" | custom-call | flops 3925868544 | bytes 9437184 | tf_op jit(solution)/shard_map/pallas_call | solution.py:376
  25.1 0.0 copy-done.4
  25.2 0.0 copy-done.5
  25.2 0.0 copy-done.3
  25.2 0.1 convert_multiply_fusion.1
  25.3 0.1 mul.43
  25.3 0.0 copy-done.2
  25.4 0.9 fusion.g_ref
  26.2 0.0 copy-start
  26.2 26.4 %shard_map.105 = (bf16[256,768]{1,0:T(8,128)(2,1)}, f32[1280,768]{1,0:T(8,128)}, f32[1280,768]{1,0:T(8,128)}) custom-call(s32[1]{0:T(128)} %bitcast.place_ref, bf16[256,768]{1,0:T(8,128)(2,1)} %get-tuple-element.12.q_ref, bf16[1280,768]{1,0:T(8,128)(2,1)} %get-tuple-element.13.kc_ref, bf16[1280,768]{1,0:T(8,128)(2,1)} %get-tuple-element.14.vc_ref, ...), custom_call_target="tpu_custom_call" | custom-call | flops 5637144576 | bytes 13369344 | tf_op jit(solution)/shard_map/pallas_call | solution.py:183
  52.6 0.0 copy-done
  52.7 0.0 copy-start.1
  52.7 1.5 %copy.11 = bf16[768,768]{0,1:T(8,128)(2,1)} copy(bf16[768,768]{1,0:T(8,128)(2,1)S(1)} %copy-done) | data formatting | bytes 2359296 | tf_op args[6]
  54.2 0.0 copy-done.1
  54.2 1.4 %copy.12 = bf16[768,768]{0,1:T(8,128)(2,1)} copy(bf16[768,768]{1,0:T(8,128)(2,1)S(1)} %copy-done.1) | data formatting | bytes 2359296 | tf_op args[7]
  55.6 61.8 %shard_map.106 = (f32[256,768]{1,0:T(8,128)}, f32[8,128]{1,0:T(8,128)}) custom-call(f32[1280,768]{1,0:T(8,128)} %get-tuple-element.18.dk_ref, f32[1280,768]{1,0:T(8,128)} %get-tuple-element.19.dv_ref, bf16[768,768]{1,0:T(8,128)(2,1)} %bitcast.21, bf16[768,768]{1,0:T(8,128)(2,1)} %bitcast.22), custom_call_target="tpu_custom_call" | custom-call | flops 6039797760 | bytes 11010048 | tf_op jit(solution)/shard_map/pallas_call | solution.py:287
  117.4 1.2 slice.11
  119.3 2.1 %multiply_bitcast_fusion = f32[1,256,768]{2,1,0:T(8,128)} fusion(f32[256,768]{1,0:T(8,128)} %get-tuple-element.20, f32[]{:T(128)} %bitcast.10), kind=kLoop, calls=%fused_computation.2 | loop fusion | flops 196608 | bytes 1572868 | tf_op jit(solution)/shard_map/broadcast_in_dim | solution.py:431
  (2 shorter events, 0.0 us)
Async XLA Ops:
  3.3 21.8 %copy-start.4 = (s32[1,16,2]{1,2,0:T(2,128)S(1)}, s32[1,16,2]{1,2,0:T(2,128)}, u32[]{:S(2)}) copy-start(s32[1,16,2]{1,2,0:T(2,128)} %param.13) | copy-start | bytes 388
  3.3 21.8 %copy-start.5 = (s32[1,16]{1,0:T(1,128)S(1)}, s32[1,16]{1,0:T(1,128)}, u32[]{:S(2)}) copy-start(s32[1,16]{1,0:T(1,128)} %param.12) | copy-start | bytes 196
  3.3 21.9 %copy-start.3 = (s32[1,16]{1,0:T(1,128)S(1)}, s32[1,16]{1,0:T(1,128)}, u32[]{:S(2)}) copy-start(s32[1,16]{1,0:T(1,128)} %param.11) | copy-start | bytes 196
  3.3 22.0 %copy-start.2 = (bf16[1,256,768]{2,1,0:T(8,128)(2,1)S(1)}, bf16[1,256,768]{2,1,0:T(8,128)(2,1)}, u32[]{:S(2)}) copy-start(bf16[1,256,768]{2,1,0:T(8,128)(2,1)} %param.10) | copy-start | bytes 1179652
  26.2 26.4 %copy-start = (bf16[768,768]{1,0:T(8,128)(2,1)S(1)}, bf16[768,768]{1,0:T(8,128)(2,1)}, u32[]{:S(2)}) copy-start(bf16[768,768]{1,0:T(8,128)(2,1)} %wk_ref.1) | copy-start | bytes 3538948
  52.7 1.5 %copy-start.1 = (bf16[768,768]{1,0:T(8,128)(2,1)S(1)}, bf16[768,768]{1,0:T(8,128)(2,1)}, u32[]{:S(2)}) copy-start(bf16[768,768]{1,0:T(8,128)(2,1)} %wv_ref.1) | copy-start | bytes 3538948

commit v12 on v11

--- a/solution.py
+++ b/solution.py
@@ -130,20 +130,22 @@
     contract = (((1,), (1,)), ((), ()))
     lead = (((0,), (0,)), ((), ()))
     zero = jnp.zeros((), jnp.bfloat16)
+    query_scaled = query * jnp.asarray(scale, jnp.bfloat16)
+    grad_scaled = grad * jnp.asarray(scale, jnp.bfloat16)
     outs, dks, dvs = [], [], []
     for head in range(lanes // HEAD_DIM):
         mine = lane == head
-        query_h = jnp.where(mine, query, zero)
-        grad_h = jnp.where(mine, grad, zero)
-        score_clean = lax.dot_general(query_h, key_clean, contract, preferred_element_type=jnp.float32) * scale
-        score_noisy = lax.dot_general(query_h, key_noisy, contract, preferred_element_type=jnp.float32) * scale
+        query_h = jnp.where(mine, query_scaled, zero)
+        grad_h = jnp.where(mine, grad_scaled, zero)
+        score_clean = lax.dot_general(query_h, key_clean, contract, preferred_element_type=jnp.float32)
+        score_noisy = lax.dot_general(query_h, key_noisy, contract, preferred_element_type=jnp.float32)
         score_clean = jnp.where(allow_clean, score_clean, -jnp.inf)
         score_noisy = jnp.where(allow_noisy, score_noisy, -jnp.inf)
         peak = jnp.maximum(
             jnp.max(score_clean, axis=-1, keepdims=True), jnp.max(score_noisy, axis=-1, keepdims=True)
         )
-        exp_clean = jnp.where(allow_clean, jnp.exp(score_clean - peak), 0.0)
-        exp_noisy = jnp.where(allow_noisy, jnp.exp(score_noisy - peak), 0.0)
+        exp_clean = jnp.exp(score_clean - peak)
+        exp_noisy = jnp.exp(score_noisy - peak)
         denom = jnp.sum(exp_clean, axis=-1, keepdims=True) + jnp.sum(exp_noisy, axis=-1, keepdims=True)
         inverse = 1.0 / denom
         prob_clean = exp_clean * inverse
@@ -153,11 +155,11 @@
         mixed = mixed + jnp.dot(weight_noisy, value_noisy, preferred_element_type=jnp.float32)
         out_h = mixed.astype(jnp.bfloat16)
         delta = jnp.sum(
-            jnp.where(mine, grad.astype(jnp.float32) * out_h.astype(jnp.float32), 0.0),
+            jnp.where(mine, grad_scaled.astype(jnp.float32) * out_h.astype(jnp.float32), 0.0),
             axis=-1, keepdims=True,
         )
         dprob = lax.dot_general(grad_h, value_clean, contract, preferred_element_type=jnp.float32)
-        dscore = (prob_clean * (dprob - delta) * scale).astype(jnp.bfloat16)
+        dscore = (prob_clean * (dprob - delta)).astype(jnp.bfloat16)
         outs.append(out_h)
         dks.append(lax.dot_general(dscore, query, lead, preferred_element_type=jnp.float32))
         dvs.append(lax.dot_general(weight_clean, grad, lead, preferred_element_type=jnp.float32))

time: 122 us -> 120 us (0.984)
  no operation moved by 1% of the time
where the time goes in v12:
time: 120 us
  Pallas kernels  109 us (91%)
  other arithmetic  5.64 us (5%)
  local copies, waits for them, and re-layouts  4.33 us (4%)
  between operations  1.4 us (1%)
    pallas_call x1, Pallas kernels, sum_back(): pl.pallas_call(functools.partial(sum_back_kernel, axes, span, chunks, sta...  61.8 us
    pallas_call x1, Pallas kernels, attention_heads(): pl.pallas_call(attention_kernel, out_shape=(jax.ShapeDtypeStruct((rows, w...  25.2 us
    pallas_call x1, Pallas kernels, gather_front(): pl.pallas_call(functools.partial(gather_front_kernel, axes, span, chunks)...  21.8 us
    unnamed x14, local copies, waits for them, and re-layouts  2.97 us

profile of v12, /device:TPU:1, one launch (start us, length us, event | category | flops | bytes accessed | tf_op | source)
XLA Modules:
  0.0 120.2 jit_solution(8530356494179764146)
XLA Ops:
  0.6 0.7 fusion.1
  1.4 0.1 eq.12
  1.5 1.9 %broadcast_select_fusion.noisy_ref = bf16[256,768]{1,0:T(8,128)(2,1)} fusion(pred[256]{0:T(512)(128)(4,1)S(1)} %eq.12, bf16[768]{0:T(1024)(128)(2,1)} %param.17, bf16[1,256,768]{2,1,0:T(8,128)(2,1)} %param.9), kind=kLoop, calls=%fused_computation.3 | loop fusion | flops 196608 | bytes 788224 | tf_op jit(solution)/shard_map/jit(_where)/select_n | solution.py:415
  3.3 0.0 copy-start.4
  3.3 0.0 copy-start.5
  3.3 0.0 copy-start.3
  3.3 0.0 copy-start.2
  3.3 21.8 %shard_map.104 = (bf16[1280,768]{1,0:T(8,128)(2,1)}, bf16[1280,768]{1,0:T(8,128)(2,1)}, bf16[256,768]{1,0:T(8,128)(2,1)}, bf16[256,768]{1,0:T(8,128)(2,1)}, bf16[256,768]{1,0:T(8,128)(2,1)}) custom-call(bf16[256,768]{1,0:T(8,128)(2,1)} %bitcast.23, bf16[256,768]{1,0:T(8,128)(2,1)} %broadcast_select_fusion.noisy_ref, bf16[768,768]{1,0:T(8,128)(2,1)} %wq_ref.1, ...), custom_call_target="tpu_custom_call" | custom-call | flops 3925868544 | bytes 9437184 | tf_op jit(solution)/shard_map/pallas_call | solution.py:378
  25.1 0.0 copy-done.4
  25.2 0.0 copy-done.5
  25.2 0.0 copy-done.3
  25.2 0.1 convert_multiply_fusion.1
  25.3 0.1 mul.43
  25.3 0.0 copy-done.2
  25.4 0.9 fusion.g_ref
  26.2 0.0 copy-start
  26.2 25.2 %shard_map.105 = (bf16[256,768]{1,0:T(8,128)(2,1)}, f32[1280,768]{1,0:T(8,128)}, f32[1280,768]{1,0:T(8,128)}) custom-call(s32[1]{0:T(128)} %bitcast.place_ref, bf16[256,768]{1,0:T(8,128)(2,1)} %get-tuple-element.12.q_ref, bf16[1280,768]{1,0:T(8,128)(2,1)} %get-tuple-element.13.kc_ref, bf16[1280,768]{1,0:T(8,128)(2,1)} %get-tuple-element.14.vc_ref, ...), custom_call_target="tpu_custom_call" | custom-call | flops 5637144576 | bytes 13369344 | tf_op jit(solution)/shard_map/pallas_call | solution.py:185
  51.5 0.0 copy-done
  51.5 0.0 copy-start.1
  51.5 1.5 %copy.11 = bf16[768,768]{0,1:T(8,128)(2,1)} copy(bf16[768,768]{1,0:T(8,128)(2,1)S(1)} %copy-done) | data formatting | bytes 2359296 | tf_op args[6]
  53.0 0.0 copy-done.1
  53.0 1.4 %copy.12 = bf16[768,768]{0,1:T(8,128)(2,1)} copy(bf16[768,768]{1,0:T(8,128)(2,1)S(1)} %copy-done.1) | data formatting | bytes 2359296 | tf_op args[7]
  54.4 61.8 %shard_map.106 = (f32[256,768]{1,0:T(8,128)}, f32[8,128]{1,0:T(8,128)}) custom-call(f32[1280,768]{1,0:T(8,128)} %get-tuple-element.18.dk_ref, f32[1280,768]{1,0:T(8,128)} %get-tuple-element.19.dv_ref, bf16[768,768]{1,0:T(8,128)(2,1)} %bitcast.21, bf16[768,768]{1,0:T(8,128)(2,1)} %bitcast.22), custom_call_target="tpu_custom_call" | custom-call | flops 6039797760 | bytes 11010048 | tf_op jit(solution)/shard_map/pallas_call | solution.py:289
  116.3 1.2 slice.11
  118.1 2.1 %multiply_bitcast_fusion = f32[1,256,768]{2,1,0:T(8,128)} fusion(f32[256,768]{1,0:T(8,128)} %get-tuple-element.20, f32[]{:T(128)} %bitcast.10), kind=kLoop, calls=%fused_computation.2 | loop fusion | flops 196608 | bytes 1572868 | tf_op jit(solution)/shard_map/broadcast_in_dim | solution.py:433
  (2 shorter events, 0.0 us)
Async XLA Ops:
  3.3 21.8 %copy-start.4 = (s32[1,16,2]{1,2,0:T(2,128)S(1)}, s32[1,16,2]{1,2,0:T(2,128)}, u32[]{:S(2)}) copy-start(s32[1,16,2]{1,2,0:T(2,128)} %param.13) | copy-start | bytes 388
  3.3 21.8 %copy-start.5 = (s32[1,16]{1,0:T(1,128)S(1)}, s32[1,16]{1,0:T(1,128)}, u32[]{:S(2)}) copy-start(s32[1,16]{1,0:T(1,128)} %param.12) | copy-start | bytes 196
  3.3 21.9 %copy-start.3 = (s32[1,16]{1,0:T(1,128)S(1)}, s32[1,16]{1,0:T(1,128)}, u32[]{:S(2)}) copy-start(s32[1,16]{1,0:T(1,128)} %param.11) | copy-start | bytes 196
  3.3 22.0 %copy-start.2 = (bf16[1,256,768]{2,1,0:T(8,128)(2,1)S(1)}, bf16[1,256,768]{2,1,0:T(8,128)(2,1)}, u32[]{:S(2)}) copy-start(bf16[1,256,768]{2,1,0:T(8,128)(2,1)} %param.10) | copy-start | bytes 1179652
  26.2 25.2 %copy-start = (bf16[768,768]{1,0:T(8,128)(2,1)S(1)}, bf16[768,768]{1,0:T(8,128)(2,1)}, u32[]{:S(2)}) copy-start(bf16[768,768]{1,0:T(8,128)(2,1)} %wk_ref.1) | copy-start | bytes 3538948
  51.5 1.5 %copy-start.1 = (bf16[768,768]{1,0:T(8,128)(2,1)S(1)}, bf16[768,768]{1,0:T(8,128)(2,1)}, u32[]{:S(2)}) copy-start(bf16[768,768]{1,0:T(8,128)(2,1)} %wv_ref.1) | copy-start | bytes 3538948

commit v13 on v12

--- a/solution.py
+++ b/solution.py
@@ -110,7 +110,7 @@
 
 
 def attention_kernel(place_ref, q_ref, kc_ref, vc_ref, kn_ref, vn_ref, g_ref,
-                     out_ref, dk_ref, dv_ref):
+                     out_ref, dk_ref, dv_ref, clean_bias, noisy_bias):
     scale = 1.0 / math.sqrt(HEAD_DIM)
     query = q_ref[...]
     key_clean = kc_ref[...]
@@ -120,12 +120,17 @@
     grad = g_ref[...]
     rows, lanes = query.shape
     context = key_clean.shape[0]
-    row_block = lax.broadcasted_iota(jnp.int32, (rows, context), 0) // BLOCK * BLOCK
-    col = lax.broadcasted_iota(jnp.int32, (rows, context), 1)
-    allow_clean = (col >= row_block) & (col < row_block + WINDOW) & (col >= place_ref[0])
-    own_row = lax.broadcasted_iota(jnp.int32, (rows, rows), 0) // BLOCK
-    own_col = lax.broadcasted_iota(jnp.int32, (rows, rows), 1) // BLOCK
-    allow_noisy = own_row == own_col
+
+    @pl.when(pl.program_id(0) == 0)
+    def _():
+        row_block = lax.broadcasted_iota(jnp.int32, (rows, context), 0) // BLOCK * BLOCK
+        col = lax.broadcasted_iota(jnp.int32, (rows, context), 1)
+        allow_clean = (col >= row_block) & (col < row_block + WINDOW) & (col >= place_ref[0])
+        own_row = lax.broadcasted_iota(jnp.int32, (rows, rows), 0) // BLOCK
+        own_col = lax.broadcasted_iota(jnp.int32, (rows, rows), 1) // BLOCK
+        clean_bias[...] = jnp.where(allow_clean, 0.0, -jnp.inf)
+        noisy_bias[...] = jnp.where(own_row == own_col, 0.0, -jnp.inf)
+
     lane = lax.broadcasted_iota(jnp.int32, (1, lanes), 1) // HEAD_DIM
     contract = (((1,), (1,)), ((), ()))
     lead = (((0,), (0,)), ((), ()))
@@ -139,8 +144,8 @@
         grad_h = jnp.where(mine, grad_scaled, zero)
         score_clean = lax.dot_general(query_h, key_clean, contract, preferred_element_type=jnp.float32)
         score_noisy = lax.dot_general(query_h, key_noisy, contract, preferred_element_type=jnp.float32)
-        score_clean = jnp.where(allow_clean, score_clean, -jnp.inf)
-        score_noisy = jnp.where(allow_noisy, score_noisy, -jnp.inf)
+        score_clean = score_clean + clean_bias[...]
+        score_noisy = score_noisy + noisy_bias[...]
         peak = jnp.maximum(
             jnp.max(score_clean, axis=-1, keepdims=True), jnp.max(score_noisy, axis=-1, keepdims=True)
         )
@@ -194,6 +199,10 @@
             grid=(pairs,),
             in_specs=[row_spec, ctx_spec, ctx_spec, row_spec, row_spec, row_spec],
             out_specs=[row_spec, ctx_spec, ctx_spec],
+            scratch_shapes=[
+                pltpu.VMEM((rows, context), jnp.float32),
+                pltpu.VMEM((rows, rows), jnp.float32),
+            ],
         ),
         cost_estimate=pl.CostEstimate(
             flops=flops,

time: 120 us -> 118 us (0.983)
  Pallas kernels: 109 us -> 107 us
    pallas_call x1, Pallas kernels: 25.2 us -> 22.9 us  [attention_heads(): pl.pallas_call(attention_kernel, out_shape=(jax.ShapeDtypeStruct((rows, w...]
where the time goes in v13:
time: 118 us
  Pallas kernels  107 us (91%)
  other arithmetic  5.64 us (5%)
  local copies, waits for them, and re-layouts  4.33 us (4%)
  between operations  1.4 us (1%)
    pallas_call x1, Pallas kernels, sum_back(): pl.pallas_call(functools.partial(sum_back_kernel, axes, span, chunks, sta...  61.8 us
    pallas_call x1, Pallas kernels, attention_heads(): pl.pallas_call(attention_kernel, out_shape=(jax.ShapeDtypeStruct((rows, w...  22.9 us
    pallas_call x1, Pallas kernels, gather_front(): pl.pallas_call(functools.partial(gather_front_kernel, axes, span, chunks)...  21.8 us
    unnamed x14, local copies, waits for them, and re-layouts  2.97 us

profile of v13, /device:TPU:1, one launch (start us, length us, event | category | flops | bytes accessed | tf_op | source)
XLA Modules:
  0.0 117.9 jit_solution(3256040273843467007)
XLA Ops:
  0.6 0.7 fusion.1
  1.4 0.1 eq.12
  1.5 1.9 %broadcast_select_fusion.noisy_ref = bf16[256,768]{1,0:T(8,128)(2,1)} fusion(pred[256]{0:T(512)(128)(4,1)S(1)} %eq.12, bf16[768]{0:T(1024)(128)(2,1)} %param.17, bf16[1,256,768]{2,1,0:T(8,128)(2,1)} %param.9), kind=kLoop, calls=%fused_computation.3 | loop fusion | flops 196608 | bytes 788224 | tf_op jit(solution)/shard_map/jit(_where)/select_n | solution.py:424
  3.3 0.0 copy-start.4
  3.3 0.0 copy-start.5
  3.3 0.0 copy-start.3
  3.3 0.0 copy-start.2
  3.3 21.8 %shard_map.104 = (bf16[1280,768]{1,0:T(8,128)(2,1)}, bf16[1280,768]{1,0:T(8,128)(2,1)}, bf16[256,768]{1,0:T(8,128)(2,1)}, bf16[256,768]{1,0:T(8,128)(2,1)}, bf16[256,768]{1,0:T(8,128)(2,1)}) custom-call(bf16[256,768]{1,0:T(8,128)(2,1)} %bitcast.23, bf16[256,768]{1,0:T(8,128)(2,1)} %broadcast_select_fusion.noisy_ref, bf16[768,768]{1,0:T(8,128)(2,1)} %wq_ref.1, ...), custom_call_target="tpu_custom_call" | custom-call | flops 3925868544 | bytes 9437184 | tf_op jit(solution)/shard_map/pallas_call | solution.py:387
  25.1 0.0 copy-done.4
  25.2 0.0 copy-done.5
  25.2 0.0 copy-done.3
  25.2 0.1 convert_multiply_fusion.1
  25.3 0.1 mul.43
  25.3 0.0 copy-done.2
  25.4 0.9 fusion.g_ref
  26.2 0.0 copy-start
  26.2 22.9 %shard_map.105 = (bf16[256,768]{1,0:T(8,128)(2,1)}, f32[1280,768]{1,0:T(8,128)}, f32[1280,768]{1,0:T(8,128)}) custom-call(s32[1]{0:T(128)} %bitcast.place_ref, bf16[256,768]{1,0:T(8,128)(2,1)} %get-tuple-element.12.q_ref, bf16[1280,768]{1,0:T(8,128)(2,1)} %get-tuple-element.13.kc_ref, bf16[1280,768]{1,0:T(8,128)(2,1)} %get-tuple-element.14.vc_ref, ...), custom_call_target="tpu_custom_call" | custom-call | flops 5637144576 | bytes 13369344 | tf_op jit(solution)/shard_map/pallas_call | solution.py:190
  49.1 0.0 copy-done
  49.2 0.0 copy-start.1
  49.2 1.5 %copy.11 = bf16[768,768]{0,1:T(8,128)(2,1)} copy(bf16[768,768]{1,0:T(8,128)(2,1)S(1)} %copy-done) | data formatting | bytes 2359296 | tf_op args[6]
  50.7 0.0 copy-done.1
  50.7 1.4 %copy.12 = bf16[768,768]{0,1:T(8,128)(2,1)} copy(bf16[768,768]{1,0:T(8,128)(2,1)S(1)} %copy-done.1) | data formatting | bytes 2359296 | tf_op args[7]
  52.1 61.8 %shard_map.106 = (f32[256,768]{1,0:T(8,128)}, f32[8,128]{1,0:T(8,128)}) custom-call(f32[1280,768]{1,0:T(8,128)} %get-tuple-element.18.dk_ref, f32[1280,768]{1,0:T(8,128)} %get-tuple-element.19.dv_ref, bf16[768,768]{1,0:T(8,128)(2,1)} %bitcast.21, bf16[768,768]{1,0:T(8,128)(2,1)} %bitcast.22), custom_call_target="tpu_custom_call" | custom-call | flops 6039797760 | bytes 11010048 | tf_op jit(solution)/shard_map/pallas_call | solution.py:298
  113.9 1.2 %slice.11 = f32[1,1]{1,0:T(1,128)} slice(f32[8,128]{1,0:T(8,128)} %get-tuple-element.21), slice={[0:1], [0:1]} | slice | bytes 8 | tf_op jit(solution)/shard_map/slice | solution.py:438
  115.8 2.1 %multiply_bitcast_fusion = f32[1,256,768]{2,1,0:T(8,128)} fusion(f32[256,768]{1,0:T(8,128)} %get-tuple-element.20, f32[]{:T(128)} %bitcast.10), kind=kLoop, calls=%fused_computation.2 | loop fusion | flops 196608 | bytes 1572868 | tf_op jit(solution)/shard_map/broadcast_in_dim | solution.py:442
  (2 shorter events, 0.0 us)
Async XLA Ops:
  3.3 21.8 %copy-start.4 = (s32[1,16,2]{1,2,0:T(2,128)S(1)}, s32[1,16,2]{1,2,0:T(2,128)}, u32[]{:S(2)}) copy-start(s32[1,16,2]{1,2,0:T(2,128)} %param.13) | copy-start | bytes 388
  3.3 21.8 %copy-start.5 = (s32[1,16]{1,0:T(1,128)S(1)}, s32[1,16]{1,0:T(1,128)}, u32[]{:S(2)}) copy-start(s32[1,16]{1,0:T(1,128)} %param.12) | copy-start | bytes 196
  3.3 21.9 %copy-start.3 = (s32[1,16]{1,0:T(1,128)S(1)}, s32[1,16]{1,0:T(1,128)}, u32[]{:S(2)}) copy-start(s32[1,16]{1,0:T(1,128)} %param.11) | copy-start | bytes 196
  3.3 22.0 %copy-start.2 = (bf16[1,256,768]{2,1,0:T(8,128)(2,1)S(1)}, bf16[1,256,768]{2,1,0:T(8,128)(2,1)}, u32[]{:S(2)}) copy-start(bf16[1,256,768]{2,1,0:T(8,128)(2,1)} %param.10) | copy-start | bytes 1179652
  26.2 22.9 %copy-start = (bf16[768,768]{1,0:T(8,128)(2,1)S(1)}, bf16[768,768]{1,0:T(8,128)(2,1)}, u32[]{:S(2)}) copy-start(bf16[768,768]{1,0:T(8,128)(2,1)} %wk_ref.1) | copy-start | bytes 3538948
  49.2 1.5 %copy-start.1 = (bf16[768,768]{1,0:T(8,128)(2,1)S(1)}, bf16[768,768]{1,0:T(8,128)(2,1)}, u32[]{:S(2)}) copy-start(bf16[768,768]{1,0:T(8,128)(2,1)} %wv_ref.1) | copy-start | bytes 3538948

commit v14 on v13

--- a/solution.py
+++ b/solution.py
@@ -321,7 +321,8 @@
 
 
 def gather_front_kernel(axes, span, chunks, own_ref, noisy_ref, wq_ref, wk_ref, wv_ref,
-                        kc_ref, vc_ref, q_ref, kn_ref, vn_ref, got, send_sems, recv_sems):
+                        kc_ref, vc_ref, q_ref, kn_ref, vn_ref, wkt_ref, wvt_ref,
+                        got, send_sems, recv_sems):
     me, left, right, has_left, has_right = chain_ends(axes)
     chain_barrier(axes, left, right, has_left, has_right)
     rows = own_ref.shape[0]
@@ -351,6 +352,8 @@
         @pl.when(has_right)
         def _():
             copy(0, chunk).start()
+    wkt_ref[...] = wk_ref[...].T
+    wvt_ref[...] = wv_ref[...].T
     noisy = noisy_ref[...]
     q_ref[...] = project_rows(noisy, wq_ref)
     kn_ref[...] = project_rows(noisy, wk_ref)
@@ -383,12 +386,13 @@
     vmem = pl.BlockSpec(memory_space=pltpu.VMEM)
     context = jax.ShapeDtypeStruct(((span + 1) * rows, width), jnp.bfloat16)
     local = jax.ShapeDtypeStruct((rows, width), jnp.bfloat16)
+    square = jax.ShapeDtypeStruct(w_key.shape[::-1], w_key.dtype)
     flops = 2 * width * width * rows * (2 * (span + 1) + 3)
     return pl.pallas_call(
         functools.partial(gather_front_kernel, axes, span, chunks),
-        out_shape=(context, context, local, local, local),
+        out_shape=(context, context, local, local, local, square, square),
         in_specs=[vmem] * 5,
-        out_specs=[vmem] * 5,
+        out_specs=[vmem] * 7,
         scratch_shapes=[
             pltpu.VMEM((span, chunks, piece, width), own.dtype),
             pltpu.SemaphoreType.DMA((span, chunks)),
@@ -422,7 +426,7 @@
     bits = block_bits.reshape(tok_count)
     masked = bits == 1
     noisy = jnp.where(masked[:, None], mask_embed[None, :], clean_rows)
-    key_clean, value_clean, query, key_noisy, value_noisy = gather_front(
+    key_clean, value_clean, query, key_noisy, value_noisy, key_back, value_back = gather_front(
         clean_rows, noisy, w_query, w_key, w_value, span, ("dp", "seq")
     )
     level_f = levels[0].astype(jnp.float32)
@@ -434,7 +438,7 @@
     attn_rows, dkey_rows, dvalue_rows = attention_heads(
         place, query, key_clean, value_clean, key_noisy, value_noisy, grad_out
     )
-    raw, total = sum_back(dkey_rows, dvalue_rows, w_key.T, w_value.T, span, tok_count, ("dp", "seq"))
+    raw, total = sum_back(dkey_rows, dvalue_rows, key_back, value_back, span, tok_count, ("dp", "seq"))
     total_squares = total[0, 0]
     entries = float(tok_count * width * lax.axis_size("dp") * lax.axis_size("seq"))
     rms = jnp.sqrt(total_squares / entries + EPS)

time: 118 us -> 119 us (level)
  other arithmetic: 5.64 us -> 8.62 us
  local copies, waits for them, and re-layouts: 4.33 us -> 1.36 us
    unnamed x14 -> x0, local copies, waits for them, and re-layouts: 2.97 us -> none
    mul x2, other arithmetic: 0.09 us -> 1.4 us  [on_device(): block_weight[:, None] * block_bits.astype(jnp.float32)]
where the time goes in v14:
time: 119 us; the launch traced here: 118 us
  Pallas kernels  107 us (90%)
  other arithmetic  8.62 us (7%)
  local copies, waits for them, and re-layouts  1.36 us (1%)
  between operations  1.35 us (1%)
    pallas_call x1, Pallas kernels, sum_back(): pl.pallas_call(functools.partial(sum_back_kernel, axes, span, chunks, sta...  61.9 us
    pallas_call x1, Pallas kernels, attention_heads(): pl.pallas_call(attention_kernel, out_shape=(jax.ShapeDtypeStruct((rows, w...  22.8 us
    pallas_call x1, Pallas kernels, gather_front(): pl.pallas_call(functools.partial(gather_front_kernel, axes, span, chunks)...  22.4 us

profile of v14, /device:TPU:1, one launch (start us, length us, event | category | flops | bytes accessed | tf_op | source)
XLA Modules:
  0.0 118.5 jit_solution(9000802479525208787)
XLA Ops:
  0.6 0.7 convert_bitcast_fusion
  1.3 0.7 fusion.2
  2.0 0.7 fusion.1
  2.7 0.1 eq.12
  2.8 0.7 convert_multiply_fusion.1
  3.5 0.1 mul.43
  3.6 1.9 %fusion.g_ref = bf16[256,768]{1,0:T(8,128)(2,1)} fusion(bf16[1,256,768]{2,1,0:T(8,128)(2,1)} %param.10, f32[256]{0:T(256)S(1)} %mul.43), kind=kLoop, calls=%fused_computation.1 | loop fusion | flops 589824 | bytes 787456 | tf_op jit(solution)/shard_map/convert_element_type | solution.py:436
  5.5 1.9 %broadcast_select_fusion.noisy_ref = bf16[256,768]{1,0:T(8,128)(2,1)} fusion(pred[256]{0:T(512)(128)(4,1)S(1)} %eq.12, bf16[768]{0:T(1024)(128)(2,1)} %param.17, bf16[1,256,768]{2,1,0:T(8,128)(2,1)} %param.9), kind=kLoop, calls=%fused_computation.3 | loop fusion | flops 196608 | bytes 788224 | tf_op jit(solution)/shard_map/jit(_where)/select_n | solution.py:428
  7.4 22.4 %shard_map.104 = (bf16[1280,768]{1,0:T(8,128)(2,1)}, bf16[1280,768]{1,0:T(8,128)(2,1)}, bf16[256,768]{1,0:T(8,128)(2,1)}, bf16[256,768]{1,0:T(8,128)(2,1)}, bf16...) custom-call(bf16[256,768]{1,0:T(8,128)(2,1)} %bitcast.19, ...), custom_call_target="tpu_custom_call" | custom-call | flops 3925868544 | bytes 9437184 | tf_op jit(solution)/shard_map/pallas_call | solution.py:391
  29.8 22.8 %shard_map.105 = (bf16[256,768]{1,0:T(8,128)(2,1)}, f32[1280,768]{1,0:T(8,128)}, f32[1280,768]{1,0:T(8,128)}) custom-call(s32[1]{0:T(128)} %bitcast.place_ref, bf16[256,768]{1,0:T(8,128)(2,1)} %get-tuple-element.14.q_ref, bf16[1280,768]{1,0:T(8,128)(2,1)} %get-tuple-element.15.kc_ref, bf16[1280,768]{1,0:T(8,128)(2,1)} %get-tuple-element.16.vc_ref, ...), custom_call_target="tpu_custom_call" | custom-call | flops 5637144576 | bytes 13369344 | tf_op jit(solution)/shard_map/pallas_call | solution.py:190
  52.6 61.9 %shard_map.106 = (f32[256,768]{1,0:T(8,128)}, f32[8,128]{1,0:T(8,128)}) custom-call(f32[1280,768]{1,0:T(8,128)} %get-tuple-element.20.dk_ref, f32[1280,768]{1,0:T(8,128)} %get-tuple-element.21.dv_ref, bf16[768,768]{1,0:T(8,128)(2,1)} %get-tuple-element.22.wk_ref, bf16[768,768]{1,0:T(8,128)(2,1)} %get-tuple-element.23.wv_ref), custom_call_target="tpu_custom_call" | custom-call | flops 6039797760 | bytes 11010048 | tf_op jit(solution)/shard_map/pallas_call | solution.py:298
  114.5 1.2 %slice.11 = f32[1,1]{1,0:T(1,128)} slice(f32[8,128]{1,0:T(8,128)} %get-tuple-element.25), slice={[0:1], [0:1]} | slice | bytes 8 | tf_op jit(solution)/shard_map/slice | solution.py:442
  116.4 2.1 %multiply_bitcast_fusion = f32[1,256,768]{2,1,0:T(8,128)} fusion(f32[256,768]{1,0:T(8,128)} %get-tuple-element.24, f32[]{:T(128)} %bitcast.8), kind=kLoop, calls=%fused_computation.2 | loop fusion | flops 196608 | bytes 1572868 | tf_op jit(solution)/shard_map/broadcast_in_dim | solution.py:446
